TPU v7x, 32 devices: a whole 2x2x4 slice. The times are simulated.
32 devices in a mesh: dp: 8 (over z, y), tensor: 4 (over x, core).
Axes of the slice: x: 2, y: 2, z: 4, core: 2. Of those that a mesh axis runs over, the one named last changes fastest.
Arguments:
- tokens: bfloat16 [2, 8192, 768], P(None, 'dp'), may hold values from -6 to 6
- cotangent: bfloat16 [2, 8192, 768], P(None, 'dp'), may hold values from -6 to 6
- prev_logits: float32 [2, 8192, 12], P(None, 'dp'), may hold values from -3 to 3
- routes: int32 [2, 8192, 2], P(None, 'dp'), may hold values from 0 to 11, all different within a row; in each aligned block of 1024 rows (0 to 1023, 1024 to 2047, ..., all dimensions but the last counted through in order) at most 256 rows name the same one
- norm_attn: bfloat16 [768], P('dp'), may hold values from 0.099609375 to 1.8984375
- norm_moe: bfloat16 [768], P('dp'), may hold values from 0.099609375 to 1.8984375
- w_qkv: bfloat16 [3, 768, 768], P(None, 'dp', 'tensor'), may hold values from -0.21875 to 0.21875
- w_out: bfloat16 [768, 768], P('tensor', 'dp'), may hold values from -3 to 3
- w_router: bfloat16 [768, 12], P('dp'), may hold values from -0.15625 to 0.15625
- w_const: bfloat16 [768, 4], P('dp'), may hold values from -0.21875 to 0.21875
- const_vec: bfloat16 [2, 768], P(None, 'dp'), may hold values from -5 to 5
- w_in: bfloat16 [8, 2, 768, 2048], P('dp', None, None, 'tensor'), may hold values from -0.21875 to 0.21875
- w_down: bfloat16 [8, 2048, 768], P('dp', 'tensor'), may hold values from -0.125 to 0.125
Outputs:
- result: bfloat16 [2, 8192, 768], P(None, 'dp')
- grad_tokens: bfloat16 [2, 8192, 768], P(None, 'dp')
- grad_prev: float32 [2, 8192, 12], P(None, 'dp')
- grad_norm_attn: float32 [768], P('dp')
- grad_norm_moe: float32 [768], P('dp')
- grad_qkv: float32 [3, 768, 768], P(None, 'dp', 'tensor')
- grad_out: float32 [768, 768], P('tensor', 'dp')
- grad_router: float32 [768, 12], P('dp')
- grad_const: float32 [768, 4], P('dp')
- grad_vec: float32 [2, 768], P(None, 'dp')
- grad_in: float32 [8, 2, 768, 2048], P('dp', None, None, 'tensor')
- grad_down: float32 [8, 2048, 768], P('dp', 'tensor')
Inputs may be any that keep to these rules, and one draw needn't show every extreme that they name: Numbers below 8 name feed-forward experts; 8 is the zero expert, 9 the copy expert, 10 and 11 the constant experts. A token's two routes differ. In each micro-batch the 1024 tokens of one index of dp name each number at most 256 times, a bound that some block reaches.
All inputs are finite; a program needn't handle non-finite values.
Results may differ from a plain program's by a relative error of at most 0.015.
Values may be sent and summed in bfloat16 or wider, within the bound.
A program may use at most 320 MiB of HBM per device.

v0:
```python
import jax
import jax.numpy as jnp
from jax import lax
from jax.sharding import PartitionSpec as P

HD = 64
LEN = 1024
BLK = 256


EPSILON = 1e-06


def norm_scale(values):
    return lax.rsqrt(jnp.mean(values * values, axis=-1, keepdims=True) + EPSILON)


def norm_back(values, scale, gain, grad):
    normed = values * scale
    grad_gain = jnp.sum(grad * normed, axis=0)
    scaled = grad * gain
    grad_values = scale * (scaled - normed * jnp.mean(scaled * normed, axis=-1, keepdims=True))
    return (grad_values, grad_gain)


def rope_tables():
    half = HD // 2
    ladder = jnp.arange(half, dtype=jnp.float32) * (2.0 / HD)
    frequency = jnp.exp(ladder * -jnp.log(jnp.float32(10000.0)))
    angle = jnp.arange(LEN, dtype=jnp.float32)[:, None] * frequency[None, :]
    return (jnp.cos(angle), jnp.sin(angle))


def rotate(field, cosine, sine):
    half = field.shape[-1] // 2
    first = field[..., :half]
    second = field[..., half:]
    return jnp.concatenate(
        [first * cosine - second * sine, second * cosine + first * sine], axis=-1
    )


def seen_keys(start, end):
    key_block = jnp.arange(end, dtype=jnp.int32) // BLK
    query_block = jnp.arange(start, end, dtype=jnp.int32) // BLK
    return key_block[None, :] <= query_block[:, None]


def attend(query_scaled, keys, values):
    step_rows = min(512, LEN)
    pieces = []
    totals = []
    for start in range(0, LEN, step_rows):
        end = start + step_rows
        scores = jnp.einsum(
            "qhd,khd->hqk", query_scaled[start:end], keys[:end], preferred_element_type=jnp.float32
        )
        scores = jnp.where(seen_keys(start, end), scores, -1e30)
        highest = jnp.max(scores, axis=-1, keepdims=True)
        exponent = jnp.exp(scores - highest)
        total = jnp.sum(exponent, axis=-1, keepdims=True)
        weights = (exponent / total).astype(jnp.bfloat16)
        attended = jnp.einsum(
            "hqk,khd->qhd", weights, values[:end], preferred_element_type=jnp.float32
        )
        pieces.append(attended.astype(jnp.bfloat16))
        totals.append(highest + jnp.log(total))
    return (jnp.concatenate(pieces, axis=0), jnp.concatenate(totals, axis=1))


def attend_back(query_scaled, keys, values, log_total, grad_attended, scale):
    step_rows = min(512, LEN)
    grad_query_parts = []
    grad_keys = jnp.zeros(keys.shape, jnp.float32)
    grad_values = jnp.zeros(values.shape, jnp.float32)
    for start in range(0, LEN, step_rows):
        end = start + step_rows
        query_part = query_scaled[start:end]
        grad_part = grad_attended[start:end]
        scores = jnp.einsum(
            "qhd,khd->hqk", query_part, keys[:end], preferred_element_type=jnp.float32
        )
        scores = jnp.where(seen_keys(start, end), scores, -1e30)
        probs = jnp.exp(scores - log_total[:, start:end])
        value_part = jnp.einsum(
            "hqk,qhd->khd",
            probs.astype(jnp.bfloat16),
            grad_part,
            preferred_element_type=jnp.float32,
        )
        grad_probs = jnp.einsum(
            "qhd,khd->hqk", grad_part, values[:end], preferred_element_type=jnp.float32
        )
        grad_scores = (
            probs * (grad_probs - jnp.sum(grad_probs * probs, axis=-1, keepdims=True))
        ).astype(jnp.bfloat16)
        grad_query_parts.append(
            jnp.einsum("hqk,khd->qhd", grad_scores, keys[:end], preferred_element_type=jnp.float32)
            * scale
        )
        key_part = jnp.einsum(
            "hqk,qhd->khd", grad_scores, query_part, preferred_element_type=jnp.float32
        )
        padding = ((0, LEN - end), (0, 0), (0, 0))
        grad_keys = grad_keys + jnp.pad(key_part, padding)
        grad_values = grad_values + jnp.pad(value_part, padding)
    return (jnp.concatenate(grad_query_parts, axis=0), grad_keys, grad_values)


def indicator(kind, value):
    return (kind == value).astype(jnp.float32)


def body(
    tokens,
    cotangent,
    prev_logits,
    routes,
    norm_attn,
    norm_moe,
    w_qkv,
    w_out,
    w_router,
    w_const,
    const_vec,
    w_in,
    w_down,
):
    micro, rows, width = tokens.shape
    experts = lax.axis_size("dp")
    columns = prev_logits.shape[2]
    capacity = 4 * max(1, 3 * rows // (4 * (experts + 4)))
    local_width = w_qkv.shape[2]
    local_heads = local_width // HD
    sequences = rows // LEN
    scale = HD ** (-0.5)
    cosine, sine = rope_tables()
    cosine = cosine[:, None, :]
    sine = sine[:, None, :]
    hidden_width = w_in.shape[3]
    catalog = jnp.arange(columns, dtype=jnp.int32)
    expert_ids = jnp.arange(experts, dtype=jnp.int32)
    zero_row = jnp.zeros((1, width), jnp.bfloat16)

    def join_slots(piece):
        return lax.all_gather(piece, "tensor", axis=1, tiled=True)

    def slot_total(term_sums):
        return lax.psum_scatter(term_sums, "tensor", scatter_dimension=1, tiled=True).astype(
            jnp.bfloat16
        )

    def to_experts(buffer):
        return lax.all_to_all(buffer, "dp", split_axis=0, concat_axis=0, tiled=True)

    def from_experts(terms):
        return lax.all_to_all(
            join_slots(slot_total(terms)), "dp", split_axis=0, concat_axis=0, tiled=True
        )

    def head_total(term_sums):
        return lax.psum(term_sums, "tensor")

    grad_gain_attn = jnp.zeros((width,), jnp.float32)
    grad_gain_moe = jnp.zeros((width,), jnp.float32)
    grad_qkv = jnp.zeros((3, width, local_width), jnp.float32)
    grad_out = jnp.zeros((local_width, width), jnp.float32)
    grad_router = jnp.zeros((width, columns), jnp.float32)
    grad_const = jnp.zeros((width, 4), jnp.float32)
    grad_vector = jnp.zeros((2, width), jnp.float32)
    grad_gate = jnp.zeros((width, hidden_width), jnp.float32)
    grad_up = jnp.zeros((width, hidden_width), jnp.float32)
    grad_down = jnp.zeros((hidden_width, width), jnp.float32)
    outputs = []
    input_grads = []
    logit_grads = []
    for index in range(micro):
        gain_attn, gain_moe, qkv_weight, out_weight, router_weight, const_weight, vectors = (
            lax.all_gather(norm_attn, "dp", axis=0, tiled=True),
            lax.all_gather(norm_moe, "dp", axis=0, tiled=True),
            lax.all_gather(w_qkv, "dp", axis=1, tiled=True),
            lax.all_gather(w_out, "dp", axis=1, tiled=True),
            lax.all_gather(w_router, "dp", axis=0, tiled=True),
            lax.all_gather(w_const, "dp", axis=0, tiled=True),
            lax.all_gather(const_vec, "dp", axis=1, tiled=True),
        )
        gate_weight = w_in[0, 0]
        up_weight = w_in[0, 1]
        down_weight = w_down[0]
        gain_attn = gain_attn.astype(jnp.float32)
        gain_moe = gain_moe.astype(jnp.float32)
        vectors = vectors.astype(jnp.float32)
        inputs = tokens[index].astype(jnp.float32)
        scale_attn = norm_scale(inputs)
        normed_attn = (inputs * scale_attn * gain_attn).astype(jnp.bfloat16)
        projected = jnp.einsum(
            "rd,idc->irc", normed_attn, qkv_weight, preferred_element_type=jnp.float32
        )
        projected = projected.reshape(3, sequences, LEN, local_heads, HD)
        query = rotate(projected[0], cosine, sine).astype(jnp.bfloat16)
        query_scaled = query * jnp.bfloat16(scale)
        keys = rotate(projected[1], cosine, sine).astype(jnp.bfloat16)
        values = projected[2].astype(jnp.bfloat16)
        attended, log_total = lax.map(
            lambda packed: attend(packed[0], packed[1], packed[2]), (query_scaled, keys, values)
        )
        attended_rows = attended.reshape(rows, local_width)
        mixed = head_total(jnp.dot(attended_rows, out_weight, preferred_element_type=jnp.float32))
        state = inputs + mixed
        scale_moe = norm_scale(state)
        normed = state * scale_moe * gain_moe
        normed_low = normed.astype(jnp.bfloat16)
        logits = (
            jnp.dot(normed_low, router_weight, preferred_element_type=jnp.float32)
            + prev_logits[index]
        )
        choose = routes[index]
        route_hot = (choose[:, :, None] == catalog[None, None, :]).astype(jnp.float32)
        picked = jnp.sum(route_hot * logits[:, None, :], axis=2)
        gates = jax.nn.softmax(picked, axis=-1)
        const_logits = jnp.dot(normed_low, const_weight, preferred_element_type=jnp.float32)
        alpha_zero = jax.nn.softmax(const_logits[:, 0:2], axis=-1)
        alpha_one = jax.nn.softmax(const_logits[:, 2:4], axis=-1)
        const_zero = alpha_zero[:, 0:1] * normed + alpha_zero[:, 1:2] * vectors[0]
        const_one = alpha_one[:, 0:1] * normed + alpha_one[:, 1:2] * vectors[1]
        flat_routes = choose.reshape(rows * 2)
        expert_hits = (flat_routes[:, None] == expert_ids[None, :]).astype(jnp.int32)
        order = jnp.sum(jnp.cumsum(expert_hits, axis=0) * expert_hits, axis=1) - 1
        slots = jnp.where(flat_routes < experts, flat_routes * capacity + order, experts * capacity)
        table = jnp.full((experts * capacity + 1,), rows * 2, jnp.int32)
        table = table.at[slots].set(jnp.arange(rows * 2, dtype=jnp.int32))[: experts * capacity]
        padded = jnp.concatenate([normed_low, zero_row], axis=0)
        arrived = to_experts(padded[table // 2].reshape(experts, capacity, width))
        arrived = arrived.reshape(-1, width)
        gate_hidden = jnp.dot(arrived, gate_weight, preferred_element_type=jnp.float32)
        up_hidden = jnp.dot(arrived, up_weight, preferred_element_type=jnp.float32)
        active = jax.nn.silu(gate_hidden)
        hidden = (active * up_hidden).astype(jnp.bfloat16)
        answer_terms = jnp.dot(hidden, down_weight, preferred_element_type=jnp.float32).reshape(
            experts, -1, width
        )
        answers = from_experts(answer_terms).reshape(experts * capacity, width)
        answers = jnp.concatenate([answers, zero_row], axis=0)
        slot_pairs = slots.reshape(rows, 2)
        kinds = [choose[:, pick][:, None] for pick in range(2)]
        branches = []
        for pick in range(2):
            kind = kinds[pick]
            routed = answers[slot_pairs[:, pick]].astype(jnp.float32)
            branch = (kind < experts).astype(jnp.float32) * routed
            branch = branch + indicator(kind, experts + 1) * normed
            branch = branch + indicator(kind, experts + 2) * const_zero
            branch = branch + indicator(kind, experts + 3) * const_one
            branches.append(branch)
        outputs.append(
            (state + (gates[:, 0:1] * branches[0] + gates[:, 1:2] * branches[1])).astype(
                jnp.bfloat16
            )
        )
        grad_result = cotangent[index].astype(jnp.float32)
        grad_pick = jnp.stack(
            [jnp.sum(branches[pick] * grad_result, axis=-1) for pick in range(2)], axis=-1
        )
        grad_picked = gates * (grad_pick - jnp.sum(gates * grad_pick, axis=-1, keepdims=True))
        grad_logits = jnp.sum(route_hot * grad_picked[:, :, None], axis=1)
        logit_grads.append(grad_logits)
        logits_low = grad_logits.astype(jnp.bfloat16)
        grad_router = grad_router + jnp.einsum(
            "rd,re->de", normed_low, logits_low, preferred_element_type=jnp.float32
        )
        grad_normed = jnp.dot(logits_low, router_weight.T, preferred_element_type=jnp.float32)
        grad_branch = [gates[:, pick : pick + 1] * grad_result for pick in range(2)]
        grad_copy = (
            indicator(kinds[0], experts + 1) * grad_branch[0]
            + indicator(kinds[1], experts + 1) * grad_branch[1]
        )
        grad_branch_zero = (
            indicator(kinds[0], experts + 2) * grad_branch[0]
            + indicator(kinds[1], experts + 2) * grad_branch[1]
        )
        grad_branch_one = (
            indicator(kinds[0], experts + 3) * grad_branch[0]
            + indicator(kinds[1], experts + 3) * grad_branch[1]
        )
        grad_alpha_zero = jnp.stack(
            [
                jnp.sum(grad_branch_zero * normed, axis=-1),
                jnp.sum(grad_branch_zero * vectors[0], axis=-1),
            ],
            axis=-1,
        )
        grad_alpha_one = jnp.stack(
            [
                jnp.sum(grad_branch_one * normed, axis=-1),
                jnp.sum(grad_branch_one * vectors[1], axis=-1),
            ],
            axis=-1,
        )
        grad_mix_zero = alpha_zero * (
            grad_alpha_zero - jnp.sum(alpha_zero * grad_alpha_zero, axis=-1, keepdims=True)
        )
        grad_mix_one = alpha_one * (
            grad_alpha_one - jnp.sum(alpha_one * grad_alpha_one, axis=-1, keepdims=True)
        )
        const_low = jnp.concatenate([grad_mix_zero, grad_mix_one], axis=-1).astype(jnp.bfloat16)
        grad_const = grad_const + jnp.einsum(
            "rd,rc->dc", normed_low, const_low, preferred_element_type=jnp.float32
        )
        grad_vector = grad_vector + jnp.stack(
            [
                jnp.sum(alpha_zero[:, 1:2] * grad_branch_zero, axis=0),
                jnp.sum(alpha_one[:, 1:2] * grad_branch_one, axis=0),
            ],
            axis=0,
        )
        grad_normed = grad_normed + jnp.dot(
            const_low, const_weight.T, preferred_element_type=jnp.float32
        )
        grad_normed = (
            grad_normed
            + grad_copy
            + alpha_zero[:, 0:1] * grad_branch_zero
            + alpha_one[:, 0:1] * grad_branch_one
        )
        pair_grads = jnp.stack(
            [(kinds[pick] < experts).astype(jnp.float32) * grad_branch[pick] for pick in range(2)],
            axis=1,
        )
        pair_grads = jnp.concatenate(
            [pair_grads.reshape(rows * 2, width).astype(jnp.bfloat16), zero_row], axis=0
        )
        grad_arrived = to_experts(pair_grads[table].reshape(experts, capacity, width)).reshape(
            -1, width
        )
        grad_down = grad_down + jnp.einsum(
            "rf,rd->fd", hidden, grad_arrived, preferred_element_type=jnp.float32
        )
        grad_hidden = jnp.dot(grad_arrived, down_weight.T, preferred_element_type=jnp.float32)
        sigma = jax.nn.sigmoid(gate_hidden)
        grad_gate_hidden = (
            grad_hidden * up_hidden * (sigma * (1.0 + gate_hidden * (1.0 - sigma)))
        ).astype(jnp.bfloat16)
        grad_up_hidden = (grad_hidden * active).astype(jnp.bfloat16)
        grad_gate = grad_gate + jnp.einsum(
            "rd,rf->df", arrived, grad_gate_hidden, preferred_element_type=jnp.float32
        )
        grad_up = grad_up + jnp.einsum(
            "rd,rf->df", arrived, grad_up_hidden, preferred_element_type=jnp.float32
        )
        row_terms = jnp.dot(
            grad_gate_hidden, gate_weight.T, preferred_element_type=jnp.float32
        ) + jnp.dot(grad_up_hidden, up_weight.T, preferred_element_type=jnp.float32)
        returned = from_experts(row_terms.reshape(experts, -1, width)).reshape(
            experts * capacity, width
        )
        returned = jnp.concatenate([returned, zero_row], axis=0)
        grad_normed = (
            grad_normed
            + returned[slot_pairs[:, 0]].astype(jnp.float32)
            + returned[slot_pairs[:, 1]].astype(jnp.float32)
        )
        grad_state, gain_term = norm_back(state, scale_moe, gain_moe, grad_normed)
        grad_gain_moe = grad_gain_moe + gain_term
        grad_state = grad_result + grad_state
        state_low = grad_state.astype(jnp.bfloat16)
        grad_out = grad_out + jnp.einsum(
            "rc,rd->cd", attended_rows, state_low, preferred_element_type=jnp.float32
        )
        grad_attended = jnp.dot(state_low, out_weight.T, preferred_element_type=jnp.float32).astype(
            jnp.bfloat16
        )
        grad_attended = grad_attended.reshape(sequences, LEN, local_heads, HD)
        grad_query, grad_keys, grad_values = lax.map(
            lambda packed: attend_back(
                packed[0], packed[1], packed[2], packed[3], packed[4], scale
            ),
            (query_scaled, keys, values, log_total, grad_attended),
        )
        grad_projected = jnp.stack(
            [rotate(grad_query, cosine, -sine), rotate(grad_keys, cosine, -sine), grad_values],
            axis=0,
        )
        grad_projected = grad_projected.reshape(3, rows, local_width).astype(jnp.bfloat16)
        grad_qkv = grad_qkv + jnp.einsum(
            "rd,irc->idc", normed_attn, grad_projected, preferred_element_type=jnp.float32
        )
        grad_normed_attn = head_total(
            jnp.einsum(
                "irc,idc->rd", grad_projected, qkv_weight, preferred_element_type=jnp.float32
            )
        )
        grad_inputs, gain_term = norm_back(inputs, scale_attn, gain_attn, grad_normed_attn)
        grad_gain_attn = grad_gain_attn + gain_term
        input_grads.append((grad_state + grad_inputs).astype(jnp.bfloat16))
    dense = (
        lax.psum_scatter(grad_gain_attn, "dp", scatter_dimension=0, tiled=True),
        lax.psum_scatter(grad_gain_moe, "dp", scatter_dimension=0, tiled=True),
        lax.psum_scatter(grad_qkv, "dp", scatter_dimension=1, tiled=True),
        lax.psum_scatter(grad_out, "dp", scatter_dimension=1, tiled=True),
        lax.psum_scatter(grad_router, "dp", scatter_dimension=0, tiled=True),
        lax.psum_scatter(grad_const, "dp", scatter_dimension=0, tiled=True),
        lax.psum_scatter(grad_vector, "dp", scatter_dimension=1, tiled=True),
    )
    return (
        jnp.stack(outputs),
        jnp.stack(input_grads),
        jnp.stack(logit_grads),
        dense[0],
        dense[1],
        dense[2],
        dense[3],
        dense[4],
        dense[5],
        dense[6],
        jnp.stack([grad_gate, grad_up], axis=0)[None],
        grad_down[None],
    )


def solution(mesh):
    in_specs = (
        P(None, "dp", None),
        P(None, "dp", None),
        P(None, "dp", None),
        P(None, "dp", None),
        P("dp"),
        P("dp"),
        P(None, "dp", "tensor"),
        P("tensor", "dp"),
        P("dp", None),
        P("dp", None),
        P(None, "dp"),
        P("dp", None, None, "tensor"),
        P("dp", "tensor", None),
    )
    out_specs = (
        P(None, "dp", None),
        P(None, "dp", None),
        P(None, "dp", None),
        P("dp"),
        P("dp"),
        P(None, "dp", "tensor"),
        P("tensor", "dp"),
        P("dp", None),
        P("dp", None),
        P(None, "dp"),
        P("dp", None, None, "tensor"),
        P("dp", "tensor", None),
    )
    return jax.shard_map(body, mesh=mesh, in_specs=in_specs, out_specs=out_specs, check_vma=False)
```

profile of v0, /device:TPU:26, one launch (start us, length us, event | category | flops | bytes accessed | tf_op | source)
XLA Modules:
  0.0 1580.8 jit_solution(14864263070802809503)
XLA Ops:
  11.5 17.4 %all-reduce.19 = (bf16[768]{0:T(1024)(128)(2,1)S(1)}, bf16[768]{0:T(1024)(128)(2,1)}) all-reduce(bf16[768]{0:T(1024)(128)(2,1)S(1)} %dynamic-update-slice, bf16[768]{0:T(1024)(128)(2,1)S(1)} %dynamic-update-slice.1), channel_id=1, replica_groups=mesh['dp'=8,'tensor'=4] {'dp'}, use_global_device_ids=true, to_apply=%add.12 | all-reduce | flops 1536 | bytes 6144
  31.6 37.2 %all_gather.41 = bf16[3,768,192]{2,0,1:T(4,128)(2,1)S(1)} all-gather(bf16[3,96,192]{2,0,1:T(4,128)(2,1)S(1)} %copy.151), channel_id=1, replica_groups=mesh['dp'=8,'tensor'=4] {'dp'}, dimensions={1}, use_global_device_ids=true | all-gather | bytes 995328 | tf_op jit(solution)/shard_map/all_gather | solution.py:181
  80.7 31.5 %all_gather.42 = bf16[192,768]{0,1:T(8,128)(2,1)S(1)} all-gather(bf16[192,96]{0,1:T(8,128)(2,1)} %copy.154), channel_id=1, replica_groups=mesh['dp'=8,'tensor'=4] {'dp'}, dimensions={1}, use_global_device_ids=true | all-gather | bytes 331776 | tf_op jit(solution)/shard_map/all_gather | solution.py:182
  142.7 8.1 scatter_custom_fusion.1
  151.3 107.6 %all-reduce.25.cloned.1.call-done = (f32[1024,768]{1,0:T(8,128)}, f32[1024,768]{1,0:T(8,128)}) async-done(((f32[1024,768]{1,0:T(8,128)}, f32[1024,768]{1,0:T(8,128)}), (f32[1024,768]{1,0:T(8,128)}, f32[1024,768]{1,0:T(8,128)})) %all-reduce.25.cloned.1.call-update) | async-done | bytes 6291472 | tf_op jit(solution)/shard_map/psum | solution.py:162
  268.0 9.4 gather_fusion.3
  277.4 74.8 %all_to_all.40 = bf16[8,256,768]{2,1,0:T(8,128)(2,1)S(1)} all-to-all(bf16[8,256,768]{2,1,0:T(8,128)(2,1)} %bitcast.593), channel_id=1, replica_groups=mesh['dp'=8,'tensor'=4] {'dp'}, dimensions={0} | all-to-all | bytes 6291456 | tf_op jit(solution)/shard_map/all_to_all | solution.py:154
  378.9 9.4 gather_fusion
  395.2 27.7 %reduce-scatter.22.cloned.1.call-done = f32[8,64,768]{2,1,0:T(8,128)} async-done(((f32[8,256,768]{2,1,0:T(8,128)}), f32[8,64,768]{2,1,0:T(8,128)}) %reduce-scatter.22.cloned.1.call-update) | async-done | bytes 1572880 | tf_op jit(solution)/shard_map/reduce_scatter | solution.py:149
  425.6 38.0 %all-to-all-done = bf16[8,256,768]{2,1,0:T(8,128)(2,1)} async-done(((bf16[8,256,768]{2,1,0:T(8,128)(2,1)}), bf16[8,256,768]{2,1,0:T(8,128)(2,1)}, u32[]{:S(2)}, u32[]{:S(2)}) %all-to-all-start) | async-done | bytes 3145760 | tf_op jit(solution)/shard_map/all_to_all | solution.py:154
  486.7 51.7 %reduce-scatter.20.cloned.1.call-done = f32[8,64,768]{2,1,0:T(8,128)} async-done(((f32[8,256,768]{2,1,0:T(8,128)}), f32[8,64,768]{2,1,0:T(8,128)}) %reduce-scatter.20.cloned.1.call-update) | async-done | bytes 1572880 | tf_op jit(solution)/shard_map/reduce_scatter | solution.py:149
  540.9 28.7 %all-gather.8.cloned.1.call-done = bf16[8,256,768]{2,1,0:T(8,128)(2,1)} async-done(((bf16[8,64,768]{2,1,0:T(8,128)(2,1)}), bf16[8,256,768]{2,1,0:T(8,128)(2,1)}) %all-gather.8.cloned.1.call-update) | async-done | bytes 3145744 | tf_op jit(solution)/shard_map/all_gather | solution.py:146
  577.3 75.9 %all-gather.2 = bf16[8,96,2]{1,2,0:T(2,128)(2,1)S(1)} all-gather(bf16[1,96,2]{1,2,0:T(2,128)(2,1)S(1)} %bitcast.713), channel_id=1, replica_groups=mesh['dp'=8,'tensor'=4] {'dp'}, dimensions={0}, use_global_device_ids=true | all-gather | bytes 3456 | tf_op jit(solution)/shard_map/all_gather | solution.py:185
  653.3 15.0 all-gather.1
  669.0 32.2 %all-gather = bf16[8,96,12]{1,2,0:T(8,128)(2,1)S(1)} all-gather(bf16[1,96,12]{1,2,0:T(8,128)(2,1)S(1)} %bitcast.711), channel_id=1, replica_groups=mesh['dp'=8,'tensor'=4] {'dp'}, dimensions={0}, use_global_device_ids=true | all-gather | bytes 20736 | tf_op jit(solution)/shard_map/all_gather | solution.py:183
  717.9 8.1 gather_fusion.5
  753.7 12.2 fusion.52
  785.6 12.8 gather_fusion.9
  798.3 62.9 %all_to_all.41 = bf16[8,256,768]{2,1,0:T(8,128)(2,1)S(1)} all-to-all(bf16[8,256,768]{2,1,0:T(8,128)(2,1)} %bitcast.594), channel_id=1, replica_groups=mesh['dp'=8,'tensor'=4] {'dp'}, dimensions={0} | all-to-all | bytes 6291456 | tf_op jit(solution)/shard_map/all_to_all | solution.py:154
  892.7 12.4 gather_fusion.6
  912.2 20.2 %reduce-scatter.26.cloned.1.call-done = f32[8,64,768]{2,1,0:T(8,128)} async-done(((f32[8,256,768]{2,1,0:T(8,128)}), f32[8,64,768]{2,1,0:T(8,128)}) %reduce-scatter.26.cloned.1.call-update) | async-done | bytes 1572880 | tf_op jit(solution)/shard_map/reduce_scatter | solution.py:149
  934.8 41.1 %all-to-all-done.4 = bf16[8,256,768]{2,1,0:T(8,128)(2,1)} async-done(((bf16[8,256,768]{2,1,0:T(8,128)(2,1)}), bf16[8,256,768]{2,1,0:T(8,128)(2,1)}, u32[]{:S(2)}, u32[]{:S(2)}) %all-to-all-start.4) | async-done | bytes 3145760 | tf_op jit(solution)/shard_map/all_to_all | solution.py:154
  996.0 51.4 %reduce-scatter.24.cloned.1.call-done = f32[8,64,768]{2,1,0:T(8,128)} async-done(((f32[8,256,768]{2,1,0:T(8,128)}), f32[8,64,768]{2,1,0:T(8,128)}) %reduce-scatter.24.cloned.1.call-update) | async-done | bytes 1572880 | tf_op jit(solution)/shard_map/reduce_scatter | solution.py:149
  1051.1 27.4 %all-gather.12.cloned.1.call-done = bf16[8,256,768]{2,1,0:T(8,128)(2,1)} async-done(((bf16[8,64,768]{2,1,0:T(8,128)(2,1)}), bf16[8,256,768]{2,1,0:T(8,128)(2,1)}) %all-gather.12.cloned.1.call-update) | async-done | bytes 3145744 | tf_op jit(solution)/shard_map/all_gather | solution.py:146
  1084.5 8.3 multiply_reduce_fusion.19
  1114.0 8.1 gather_fusion.11
  1130.0 27.4 %all-to-all-done.5 = bf16[8,256,768]{2,1,0:T(8,128)(2,1)} async-done(((bf16[8,256,768]{2,1,0:T(8,128)(2,1)}), bf16[8,256,768]{2,1,0:T(8,128)(2,1)}, u32[]{:S(2)}, u32[]{:S(2)}) %all-to-all-start.5) | async-done | bytes 3145760 | tf_op jit(solution)/shard_map/all_to_all | solution.py:157
  1264.0 51.6 %reduce-scatter.32.cloned.1.call-done = f32[96,12]{1,0:T(8,128)} async-done(((f32[768,12]{1,0:T(8,128)}), f32[96,12]{1,0:T(8,128)}) %reduce-scatter.32.cloned.1.call-update) | async-done | bytes 4624
  1353.2 27.2 %reduce-scatter.30.cloned.1.call-done = f32[96,192]{1,0:T(8,128)} async-done(((f32[768,192]{1,0:T(8,128)}), f32[96,192]{1,0:T(8,128)}) %reduce-scatter.30.cloned.1.call-update) | async-done | bytes 73744
  1382.0 119.9 %all-reduce.23.cloned.1.call-done = (f32[1024,768]{1,0:T(8,128)}, f32[1024,768]{1,0:T(8,128)}) async-done(((f32[1024,768]{1,0:T(8,128)}, f32[1024,768]{1,0:T(8,128)}), (f32[1024,768]{1,0:T(8,128)}, f32[1024,768]{1,0:T(8,128)})) %all-reduce.23.cloned.1.call-update) | async-done | bytes 6291472 | tf_op jit(solution)/shard_map/psum | solution.py:162
  1506.6 17.1 %all-reduce.16 = (f32[768]{0:T(1024)S(1)}, f32[768]{0:T(1024)S(1)}) all-reduce(f32[768]{0:T(1024)S(1)} %add.586, f32[768]{0:T(1024)S(1)} %add.587), channel_id=6, replica_groups=mesh['dp'=8,'tensor'=4] {'dp'}, use_global_device_ids=true, to_apply=%region_72.73.clone | all-reduce | flops 1536 | bytes 12288
  1533.4 38.7 %reduce-scatter.28.cloned.1.call-done = f32[96,576]{1,0:T(8,128)} async-done(((f32[768,576]{1,0:T(8,128)}), f32[96,576]{1,0:T(8,128)}) %reduce-scatter.28.cloned.1.call-update) | async-done | bytes 221200
  (663 shorter events, 451.4 us)
Async XLA Ops:
  7.2 352.5 %copy-start = (bf16[1,512,768]{2,1,0:T(8,128)(2,1)S(1)}, bf16[1,512,768]{2,1,0:T(8,128)(2,1)}, u32[]{:S(2)}) copy-start(bf16[1,512,768]{2,1,0:T(8,128)(2,1)} %param.25) | copy-start | bytes 2359300
  7.2 251.7 %all-reduce.25.cloned.1.call-start = ((), (), s32[]{:S(2)}) async-start(), calls=%async_computation.31 | async-start | bytes 12582912 | tf_op jit(solution)/shard_map/psum | solution.py:162
  72.7 54.1 %copy-start.69 = (bf16[1,1024,192]{1,2,0:T(8,128)(2,1)}, bf16[1,1024,192]{1,2,0:T(8,128)(2,1)S(1)}, u32[]{:S(2)}) copy-start(bf16[1,1024,192]{1,2,0:T(8,128)(2,1)S(1)} %slice.686) | copy-start | bytes 1179652
  137.4 285.5 %reduce-scatter.22.cloned.1.call-start = ((), (), s32[]{:S(2)}) async-start(), calls=%async_computation.19 | async-start | bytes 7864320 | tf_op jit(solution)/shard_map/reduce_scatter | solution.py:149
  138.9 954.0 %copy-start.100 = (f32[768]{0:T(1024)}, f32[768]{0:T(1024)S(1)}, u32[]{:S(2)}) copy-start(f32[768]{0:T(1024)S(1)} %convert_element_type.390) | copy-start | bytes 9220
  277.4 74.8 %copy-start.44 = (bf16[1,2,768,512]{3,2,1,0:T(8,128)(2,1)S(1)}, bf16[1,2,768,512]{3,2,1,0:T(8,128)(2,1)}, u32[]{:S(2)}) copy-start(bf16[1,2,768,512]{3,2,1,0:T(8,128)(2,1)} %param.24) | copy-start | bytes 4718596
  388.3 75.3 %all-to-all-start = ((bf16[8,256,768]{2,1,0:T(8,128)(2,1)}), bf16[8,256,768]{2,1,0:T(8,128)(2,1)}, u32[]{:S(2)}, u32[]{:S(2)}) async-start(bf16[8,256,768]{2,1,0:T(8,128)(2,1)} %bitcast.591), calls=%async_computation | async-start | bytes 6291456 | tf_op jit(solution)/shard_map/all_to_all | solution.py:154
  395.2 68.4 %copy-start.45 = (bf16[1,2,768,512]{3,2,1,0:T(8,128)(2,1)S(1)}, bf16[1,2,768,512]{3,2,1,0:T(8,128)(2,1)}, u32[]{:S(2)}) copy-start(bf16[1,2,768,512]{3,2,1,0:T(8,128)(2,1)} %param.24) | copy-start | bytes 4718596
  395.2 85.6 %all-gather.10.cloned.1.call-start = ((), (), s32[]{:S(2)}) async-start(), calls=%async_computation.20 | async-start | bytes 3932160 | tf_op jit(solution)/shard_map/all_gather | solution.py:146
  425.4 113.0 %reduce-scatter.20.cloned.1.call-start = ((), (), s32[]{:S(2)}) async-start(), calls=%async_computation.17 | async-start | bytes 7864320 | tf_op jit(solution)/shard_map/reduce_scatter | solution.py:149
  480.8 88.7 %all-to-all-start.3 = ((bf16[8,256,768]{2,1,0:T(8,128)(2,1)}), bf16[8,256,768]{2,1,0:T(8,128)(2,1)}, u32[]{:S(2)}, u32[]{:S(2)}) async-start(bf16[8,256,768]{2,1,0:T(8,128)(2,1)} %all-gather.10.cloned.1.call-done), calls=%async_computation.5 | async-start | bytes 6291456 | tf_op jit(solution)/shard_map/all_to_all | solution.py:157
  486.7 82.8 %all-gather.8.cloned.1.call-start = ((), (), s32[]{:S(2)}) async-start(), calls=%async_computation.18 | async-start | bytes 3932160 | tf_op jit(solution)/shard_map/all_gather | solution.py:146
  540.8 112.4 %copy-start.162 = (bf16[96,4]{0,1:T(4,128)(2,1)S(1)}, bf16[96,4]{0,1:T(4,128)(2,1)}, u32[]{:S(2)}) copy-start(bf16[96,4]{0,1:T(4,128)(2,1)} %param.22) | copy-start | bytes 2308
  540.8 128.2 %copy-start.160 = (bf16[96,12]{0,1:T(8,128)(2,1)S(1)}, bf16[96,12]{0,1:T(8,128)(2,1)}, u32[]{:S(2)}) copy-start(bf16[96,12]{0,1:T(8,128)(2,1)} %param.21) | copy-start | bytes 6916
  569.5 164.3 %all-to-all-start.1 = ((bf16[8,256,768]{2,1,0:T(8,128)(2,1)}), bf16[8,256,768]{2,1,0:T(8,128)(2,1)}, u32[]{:S(2)}, u32[]{:S(2)}) async-start(bf16[8,256,768]{2,1,0:T(8,128)(2,1)} %all-gather.8.cloned.1.call-done), calls=%async_computation.2 | async-start | bytes 6291456 | tf_op jit(solution)/shard_map/all_to_all | solution.py:157
  575.5 356.9 %reduce-scatter.26.cloned.1.call-start = ((), (), s32[]{:S(2)}) async-start(), calls=%async_computation.23 | async-start | bytes 7864320 | tf_op jit(solution)/shard_map/reduce_scatter | solution.py:149
  798.3 62.9 %copy-start.170 = (f32[2048,512]{1,0:T(8,128)S(1)}, f32[2048,512]{1,0:T(8,128)}, u32[]{:S(2)}) copy-start(f32[2048,512]{1,0:T(8,128)} %copy-done.169) | copy-start | bytes 12582916
  905.1 70.8 %all-to-all-start.4 = ((bf16[8,256,768]{2,1,0:T(8,128)(2,1)}), bf16[8,256,768]{2,1,0:T(8,128)(2,1)}, u32[]{:S(2)}, u32[]{:S(2)}) async-start(bf16[8,256,768]{2,1,0:T(8,128)(2,1)} %bitcast.592), calls=%async_computation.6 | async-start | bytes 6291456 | tf_op jit(solution)/shard_map/all_to_all | solution.py:154
  912.2 76.8 %all-gather.14.cloned.1.call-start = ((), (), s32[]{:S(2)}) async-start(), calls=%async_computation.24 | async-start | bytes 3932160 | tf_op jit(solution)/shard_map/all_gather | solution.py:146
  934.8 112.6 %reduce-scatter.24.cloned.1.call-start = ((), (), s32[]{:S(2)}) async-start(), calls=%async_computation.21 | async-start | bytes 7864320 | tf_op jit(solution)/shard_map/reduce_scatter | solution.py:149
  989.0 89.5 %all-to-all-start.7 = ((bf16[8,256,768]{2,1,0:T(8,128)(2,1)}), bf16[8,256,768]{2,1,0:T(8,128)(2,1)}, u32[]{:S(2)}, u32[]{:S(2)}) async-start(bf16[8,256,768]{2,1,0:T(8,128)(2,1)} %all-gather.14.cloned.1.call-done), calls=%async_computation.11 | async-start | bytes 6291456 | tf_op jit(solution)/shard_map/all_to_all | solution.py:157
  995.9 54.6 %copy-start.144 = (f32[3,512]{1,0:T(4,128)S(1)}, f32[3,512]{1,0:T(4,128)}, u32[]{:S(2)}) copy-start(f32[3,512]{1,0:T(4,128)} %copy-done.143) | copy-start | bytes 18436
  995.9 54.6 %copy-start.146 = (f32[3,512]{1,0:T(4,128)S(1)}, f32[3,512]{1,0:T(4,128)}, u32[]{:S(2)}) copy-start(f32[3,512]{1,0:T(4,128)} %copy-done.145) | copy-start | bytes 18436
  995.9 82.6 %all-gather.12.cloned.1.call-start = ((), (), s32[]{:S(2)}) async-start(), calls=%async_computation.22 | async-start | bytes 3932160 | tf_op jit(solution)/shard_map/all_gather | solution.py:146
  1078.5 78.9 %all-to-all-start.5 = ((bf16[8,256,768]{2,1,0:T(8,128)(2,1)}), bf16[8,256,768]{2,1,0:T(8,128)(2,1)}, u32[]{:S(2)}, u32[]{:S(2)}) async-start(bf16[8,256,768]{2,1,0:T(8,128)(2,1)} %all-gather.12.cloned.1.call-done), calls=%async_computation.8 | async-start | bytes 6291456 | tf_op jit(solution)/shard_map/all_to_all | solution.py:157
  1084.5 176.6 %reduce-scatter.36.cloned.1.call-start = ((), (), s32[]{:S(2)}) async-start(), calls=%async_computation.29 | async-start | bytes 442368
  1098.9 163.7 %reduce-scatter.34.cloned.1.call-start = ((), (), s32[]{:S(2)}) async-start(), calls=%async_computation.28 | async-start | bytes 442368
  1102.2 213.5 %reduce-scatter.32.cloned.1.call-start = ((), (), s32[]{:S(2)}) async-start(), calls=%async_computation.27 | async-start | bytes 442368
  1105.6 274.8 %reduce-scatter.30.cloned.1.call-start = ((), (), s32[]{:S(2)}) async-start(), calls=%async_computation.26 | async-start | bytes 884736
  1242.6 259.3 %all-reduce.23.cloned.1.call-start = ((), (), s32[]{:S(2)}) async-start(), calls=%async_computation.30 | async-start | bytes 12582912 | tf_op jit(solution)/shard_map/psum | solution.py:162
  1255.5 316.7 %reduce-scatter.28.cloned.1.call-start = ((), (), s32[]{:S(2)}) async-start(), calls=%async_computation.25 | async-start | bytes 2211840
  1257.1 60.0 %copy-start.31 = (bf16[2048,512]{1,0:T(8,128)(2,1)S(1)}, bf16[2048,512]{1,0:T(8,128)(2,1)}, u32[]{:S(2)}) copy-start(bf16[2048,512]{1,0:T(8,128)(2,1)} %copy-done.30) | copy-start | bytes 6291460
  (167 other events, 1286.1 us)
Sparse Core Ops, SparseCore 0:
  137.5 121.3 all-reduce.24
  364.2 58.6 reduce-scatter.21
  425.5 28.5 all-gather.9
  480.9 57.4 reduce-scatter.19
  540.9 28.5 all-gather.7
  873.9 58.4 reduce-scatter.25
  934.9 28.5 all-gather.13
  989.1 58.2 reduce-scatter.23
  1049.9 28.5 all-gather.11
  1099.0 89.2 reduce-scatter.35
  1191.5 60.4 reduce-scatter.33
  1255.2 60.4 reduce-scatter.31
  1318.9 61.4 reduce-scatter.29
  1382.8 119.0 all-reduce.22
  1505.6 66.4 reduce-scatter.27
where the time goes:
time: 1590 us; the launch traced here: 1580 us
  waiting for transfers between devices  659 us (41%)
  blocking collectives  364 us (23%)
  local copies, waits for them, and re-layouts  227 us (14%)
  matrix products  164 us (10%)
  other arithmetic  109 us (7%)
  starting transfers between devices  39.6 us (2%)
  between operations  18.2 us (1%)
    psum x2, waiting for transfers between devices, head_total(): return lax.psum(term_sums, 'tensor')  227 us
    reduce_scatter x4, waiting for transfers between devices, slot_total(): lax.psum_scatter(term_sums, 'tensor', scatter_dimension=1, tiled=True)  151 us
    all_to_all x2, blocking collectives, to_experts(): return lax.all_to_all(buffer, 'dp', split_axis=0, concat_axis=0, tiled=True)  138 us
    unnamed x20, waiting for transfers between devices  118 us
    all_to_all x2, waiting for transfers between devices, to_experts(): return lax.all_to_all(buffer, 'dp', split_axis=0, concat_axis=0, tiled=True)  79.1 us
    all_gather x1, blocking collectives, body(): lax.all_gather(const_vec, 'dp', axis=1, tiled=True)  75.9 us
    all_gather x4, waiting for transfers between devices, join_slots(): return lax.all_gather(piece, 'tensor', axis=1, tiled=True)  56.1 us
    unnamed x382, local copies, waits for them, and re-layouts  43.4 us
  transfers between devices with their start and end apart: 21, of which 14 were waited for; matrix products, arithmetic and copies ran while one was open for 22% of the time, Pallas kernels for 0%

commit v1 on v0

v1 whole, which is shorter than its diff:
```python
import functools

import jax
import jax.numpy as jnp
import numpy as np
from jax import lax
from jax.experimental import pallas as pl
from jax.experimental.pallas import tpu as pltpu
from jax.sharding import PartitionSpec as P

HD = 64
LEN = 1024
BLK = 256
EPSILON = 1e-06
LANES = 128
F32 = jnp.float32
BF16 = jnp.bfloat16
MESH = pl.DeviceIdType.MESH
VMEM_LIMIT = 56 * 1024 * 1024


def mm(a, b):
    return lax.dot_general(a, b, (((1,), (0,)), ((), ())), preferred_element_type=F32)


def mm_nt(a, b):
    return lax.dot_general(a, b, (((1,), (1,)), ((), ())), preferred_element_type=F32)


def mm_tn(a, b):
    return lax.dot_general(a, b, (((0,), (0,)), ((), ())), preferred_element_type=F32)


def vspec():
    return pl.BlockSpec(memory_space=pltpu.VMEM)


def aspec():
    return pl.BlockSpec(memory_space=pl.ANY)


def struct(shape, dtype):
    return jax.ShapeDtypeStruct(shape, dtype)


def compute_call(kernel, outs, *args, flops=1e9, scratch=()):
    nbytes = sum(int(np.prod(a.shape)) * a.dtype.itemsize for a in args) + sum(
        int(np.prod(o.shape)) * o.dtype.itemsize for o in outs
    )
    return pl.pallas_call(
        kernel,
        out_shape=outs,
        in_specs=[vspec()] * len(args),
        out_specs=[vspec()] * len(outs),
        scratch_shapes=list(scratch),
        compiler_params=pltpu.CompilerParams(vmem_limit_bytes=VMEM_LIMIT),
        cost_estimate=pl.CostEstimate(
            flops=int(flops), bytes_accessed=nbytes, transcendentals=0
        ),
    )(*args)


def greet(peers):
    barrier = pltpu.get_barrier_semaphore()
    for peer in peers:
        pl.semaphore_signal(barrier, inc=1, device_id=peer, device_id_type=MESH)
    pl.semaphore_wait(barrier, len(peers))


def remote(src, dst, send, recv, peer):
    return pltpu.make_async_remote_copy(
        src_ref=src,
        dst_ref=dst,
        send_sem=send,
        recv_sem=recv,
        device_id=peer,
        device_id_type=MESH,
    )


def comm_call(kernel, outs, sems, cid, *args):
    return pl.pallas_call(
        kernel,
        out_shape=outs,
        in_specs=[aspec()] * len(args),
        out_specs=[aspec()] * len(outs),
        scratch_shapes=[pltpu.SemaphoreType.DMA(s) for s in sems],
        compiler_params=pltpu.CompilerParams(collective_id=cid, has_side_effects=True),
    )(*args)


def core_share(cid, *arrays):
    count = len(arrays)

    def kernel(*refs):
        ins, outs, (send, recv, local) = refs[:count], refs[count : 2 * count], refs[2 * count :]
        d, t = lax.axis_index("dp"), lax.axis_index("tensor")
        c = lax.rem(t, 2)
        peer = (d, t + 1 - 2 * c)
        greet([peer])
        copies = []
        for i in range(count):
            copies.append(remote(ins[i], outs[i].at[c], send.at[i], recv.at[i], peer))
            copies.append(pltpu.make_async_copy(ins[i], outs[i].at[c], local.at[i]))
        for copy in copies:
            copy.start()
        for copy in copies:
            copy.wait()

    outs = [struct((2,) + a.shape, a.dtype) for a in arrays]
    return comm_call(kernel, outs, [(count,)] * 3, cid, *arrays)


def plane_peers(n, d, t):
    return [(lax.rem(d + j, n), t) for j in range(1, n)]


def all_peers(n, d, t):
    other = lax.rem(t + 2, 4)
    return plane_peers(n, d, t) + [(lax.rem(d + j, n), other) for j in range(n)]


def gather_weights(cid, n, packed):
    def kernel(in_ref, out_ref, send, recv, local):
        d, t = lax.axis_index("dp"), lax.axis_index("tensor")
        m = lax.div(t, 2)
        peers = all_peers(n, d, t)
        greet(peers)
        mine = pltpu.make_async_copy(in_ref, out_ref.at[m, d], local.at[0])
        mine.start()
        copies = []
        for i, peer in enumerate(peers):
            copies.append(remote(in_ref, out_ref.at[m, d], send.at[i], recv.at[i], peer))
        for copy in copies:
            copy.start()
        for copy in copies:
            copy.wait()
        mine.wait()

    outs = [struct((2, n) + packed.shape, packed.dtype)]
    return comm_call(kernel, outs, [(2 * n,), (2 * n,), (1,)], cid, packed)[0]


def spread_gradients(cid, n, *arrays):
    count = len(arrays)

    def kernel(*refs):
        ins, outs, (send, recv, local) = refs[:count], refs[count : 2 * count], refs[2 * count :]
        d, t = lax.axis_index("dp"), lax.axis_index("tensor")
        m = lax.div(t, 2)
        peers = all_peers(n, d, t)
        greet(peers)
        copies = []
        for k in range(count):
            copies.append(
                pltpu.make_async_copy(ins[k].at[m, d], outs[k].at[m, d], local.at[k])
            )
            for i, (pd, pt) in enumerate(peers):
                pm = lax.div(pt, 2)
                copies.append(
                    remote(
                        ins[k].at[pm, pd],
                        outs[k].at[m, d],
                        send.at[k, i],
                        recv.at[k, i],
                        (pd, pt),
                    )
                )
        for copy in copies:
            copy.start()
        for copy in copies:
            copy.wait()

    outs = [struct(a.shape, a.dtype) for a in arrays]
    return comm_call(kernel, outs, [(count, 2 * n), (count, 2 * n), (count,)], cid, *arrays)


def dispatch(cid, n, *arrays):
    count = len(arrays)

    def kernel(*refs):
        ins, outs, (send, recv, local) = refs[:count], refs[count : 2 * count], refs[2 * count :]
        d, t = lax.axis_index("dp"), lax.axis_index("tensor")
        peers = plane_peers(n, d, t)
        greet(peers)
        copies = []
        for k in range(count):
            copies.append(pltpu.make_async_copy(ins[k].at[d], outs[k].at[d], local.at[k]))
            for i, (pd, pt) in enumerate(peers):
                copies.append(
                    remote(ins[k].at[pd], outs[k].at[d], send.at[k, i], recv.at[k, i], (pd, pt))
                )
        for copy in copies:
            copy.start()
        for copy in copies:
            copy.wait()

    outs = [struct(a.shape, a.dtype) for a in arrays]
    return comm_call(kernel, outs, [(count, n), (count, n), (count,)], cid, *arrays)


def give_back(cid, n, *arrays):
    count = len(arrays)

    def kernel(*refs):
        ins, outs = refs[:count], refs[count : 2 * count]
        send, recv, local, csend, crecv = refs[2 * count :]
        d, t = lax.axis_index("dp"), lax.axis_index("tensor")
        c = lax.rem(t, 2)
        partner = (d, t + 1 - 2 * c)
        peers = plane_peers(n, d, t)
        greet(peers + [partner])
        arrivals = []
        own = []
        passed = []
        for k in range(count):
            own.append(pltpu.make_async_copy(ins[k].at[d], outs[k].at[c, d], local.at[k]))
            passed.append(
                remote(ins[k].at[d], outs[k].at[c, d], csend.at[k, 0], crecv.at[k, 0], partner)
            )
            for i, (pd, pt) in enumerate(peers):
                arrivals.append(
                    remote(
                        ins[k].at[pd], outs[k].at[c, d], send.at[k, i], recv.at[k, i], (pd, pt)
                    )
                )
        for copy in own + passed + arrivals:
            copy.start()
        for k in range(count):
            for i in range(n - 1):
                arrivals[k * (n - 1) + i].wait_recv()
                source = lax.rem(d + n - 1 - i, n)
                block = outs[k].at[c, source]
                copy = remote(block, block, csend.at[k, i + 1], crecv.at[k, i + 1], partner)
                copy.start()
                passed.append(copy)
        for copy in arrivals:
            copy.wait_send()
        for copy in own + passed:
            copy.wait()

    outs = [struct((2,) + a.shape, a.dtype) for a in arrays]
    return comm_call(
        kernel, outs, [(count, n), (count, n), (count,), (count, n), (count, n)], cid, *arrays
    )


def share_output(cid, full):
    rows = full.shape[0]
    half = rows // 2

    def kernel(in_ref, out_ref, send, recv, local):
        d, t = lax.axis_index("dp"), lax.axis_index("tensor")
        m, c = lax.div(t, 2), lax.rem(t, 2)
        across = (d, lax.rem(t + 2, 4))
        partner = (d, t + 1 - 2 * c)
        greet([across, partner])
        mine = pltpu.make_async_copy(in_ref, out_ref.at[m], local.at[0])
        mine.start()
        first = remote(
            in_ref.at[pl.ds(c * half, half)],
            out_ref.at[m, pl.ds(c * half, half)],
            send.at[0],
            recv.at[0],
            across,
        )
        first.start()
        first.wait_recv()
        block = out_ref.at[1 - m, pl.ds(c * half, half)]
        second = remote(block, block, send.at[1], recv.at[1], partner)
        second.start()
        first.wait_send()
        second.wait()
        mine.wait()

    outs = [struct((2,) + full.shape, full.dtype)]
    return comm_call(kernel, outs, [(2,), (2,), (1,)], cid, full)[0]


def route_kernel(experts, half, padded, columns_ref, rows_ref, dy_ref, pos_ref, post_ref, slot_ref):
    rows = columns_ref.shape[0]
    lanes = post_ref.shape[0]
    first, second = rows_ref[0:1, :], rows_ref[1:2, :]
    ids = lax.broadcasted_iota(jnp.int32, (lanes, rows), 0)
    hit = ((ids == first) | (ids == second)) & (ids < experts)
    before = (
        lax.broadcasted_iota(jnp.int32, (rows, rows), 0)
        < lax.broadcasted_iota(jnp.int32, (rows, rows), 1)
    )
    count = mm(hit.astype(F32).astype(BF16), before.astype(F32).astype(BF16))
    place = jnp.where(hit, count, -1.0)
    post_ref[...] = place
    pos_ref[...] = jnp.transpose(place)
    base = lax.rem(lax.axis_index("tensor"), 2) * half
    build_slots(experts, half, padded, base, post_ref, dy_ref, slot_ref)


def slot_hot(half, padded, base, places):
    rows = places.shape[1]
    slot = lax.broadcasted_iota(jnp.int32, (padded, rows), 0)
    wanted = jnp.where(slot < half, slot + base, -2).astype(F32)
    return (wanted == places).astype(F32).astype(BF16)


def build_slots(experts, half, padded, base, post_ref, source_ref, slot_ref):
    def step(e, carry):
        hot = slot_hot(half, padded, base, post_ref[pl.ds(e, 1), :])
        slot_ref[e] = mm(hot, source_ref[...]).astype(BF16)
        return carry

    lax.fori_loop(0, experts, step, 0)


def rope_constants():
    half = HD // 2
    frequency = 10000.0 ** (-2.0 * np.arange(half) / HD)
    angle = np.arange(LEN)[:, None] * frequency[None, :]
    cosine, sine = np.cos(angle), np.sin(angle)
    cosine = np.concatenate([cosine, cosine, cosine, cosine], axis=1)
    sine = np.concatenate([-sine, sine, -sine, sine], axis=1)
    return cosine.astype(np.float32), sine.astype(np.float32)


def turn(field, cosine, sine):
    lane = lax.broadcasted_iota(jnp.int32, field.shape, 1)
    other = jnp.where(
        lax.rem(lane, HD) < HD // 2,
        pltpu.roll(field, LANES - HD // 2, 1),
        pltpu.roll(field, HD // 2, 1),
    )
    return field * cosine + other * sine


def attention_kernel(
    x_ref, gain_ref, w_ref, cos_ref, sin_ref, a_ref, q_ref, k_ref, v_ref, o_ref, lse_ref
):
    width = q_ref.shape[1]
    pairs = width // LANES
    blocks = LEN // BLK
    for i in range(blocks):
        rows = pl.ds(i * BLK, BLK)
        x = x_ref[rows, :].astype(F32)
        r = lax.rsqrt(jnp.mean(x * x, axis=-1, keepdims=True) + EPSILON)
        a = (x * r * gain_ref[...]).astype(BF16)
        a_ref[rows, :] = a
        cosine, sine = cos_ref[rows, :], sin_ref[rows, :]
        for p in range(pairs):
            lanes = pl.ds(p * LANES, LANES)
            q = turn(mm(a, w_ref[:, p * LANES : (p + 1) * LANES]), cosine, sine).astype(BF16)
            q_ref[rows, lanes] = q * BF16(HD**-0.5)
            start = width + p * LANES
            k_ref[rows, lanes] = turn(mm(a, w_ref[:, start : start + LANES]), cosine, sine).astype(
                BF16
            )
            start = 2 * width + p * LANES
            v_ref[rows, lanes] = mm(a, w_ref[:, start : start + LANES]).astype(BF16)
    head = lax.broadcasted_iota(jnp.int32, (BLK, LANES), 1) < HD
    for p in range(pairs):
        lanes = pl.ds(p * LANES, LANES)
        for i in range(blocks):
            rows = pl.ds(i * BLK, BLK)
            seen = pl.ds(0, (i + 1) * BLK)
            q, k, v = q_ref[rows, lanes], k_ref[seen, lanes], v_ref[seen, lanes]
            halves = []
            for side in range(2):
                mask = head if side == 0 else jnp.logical_not(head)
                s = mm_nt(jnp.where(mask, q, jnp.zeros_like(q)), k)
                high = jnp.max(s, axis=-1, keepdims=True)
                e = jnp.exp(s - high)
                total = jnp.sum(e, axis=-1, keepdims=True)
                halves.append(mm((e / total).astype(BF16), v))
                log_total = jnp.broadcast_to(high + jnp.log(total), (BLK, LANES))
                lse_ref[2 * p + side : 2 * p + side + 1, rows] = jnp.transpose(log_total)[0:1, :]
            o_ref[rows, lanes] = jnp.where(head, halves[0], halves[1]).astype(BF16)


def pick(hot, values):
    return jnp.sum(jnp.where(hot, values, 0.0), axis=-1, keepdims=True)


def lane_ids(rows):
    return lax.broadcasted_iota(jnp.int32, (rows, LANES), 1)


def column(value, lane, rows):
    return jnp.where(lane_ids(rows) == lane, value, 0.0)


def soft_pair(first, second):
    high = jnp.maximum(first, second)
    e0, e1 = jnp.exp(first - high), jnp.exp(second - high)
    return e0 / (e0 + e1), e1 / (e0 + e1)


def middle_kernel(
    experts,
    half,
    padded,
    x_ref,
    o_ref,
    wo_ref,
    small_ref,
    gain_ref,
    prev_ref,
    routes_ref,
    post_ref,
    h_ref,
    ub_ref,
    stat_ref,
    slot_ref,
    gate_ref,
    pieces_ref,
):
    rows_all = x_ref.shape[0]
    for i in range(rows_all // BLK):
        rows = pl.ds(i * BLK, BLK)
        z = mm_nt(o_ref[0, rows, :], wo_ref[0]) + mm_nt(o_ref[1, rows, :], wo_ref[1])
        h = x_ref[rows, :].astype(F32) + z
        r = lax.rsqrt(jnp.mean(h * h, axis=-1, keepdims=True) + EPSILON)
        ub = (h * r * gain_ref[...]).astype(BF16)
        h_ref[rows, :] = h
        ub_ref[rows, :] = ub
        scores = mm(ub, small_ref[...])
        logits = scores + prev_ref[rows, :]
        ids = lane_ids(BLK)
        hot0 = ids == routes_ref[rows, 0:1]
        hot1 = ids == routes_ref[rows, 1:2]
        g0, g1 = soft_pair(pick(hot0, logits), pick(hot1, logits))
        base = experts + 4
        c = [pick(ids == base + j, scores) for j in range(4)]
        a00, a01 = soft_pair(c[0], c[1])
        a10, a11 = soft_pair(c[2], c[3])
        stats = [g0, g1, a00, a01, a10, a11, r]
        table = column(stats[0], 0, BLK)
        for j in range(1, len(stats)):
            table = table + column(stats[j], j, BLK)
        stat_ref[rows, :] = table
        gates = jnp.where(hot0, g0, 0.0) + jnp.where(hot1, g1, 0.0)
        gates = jnp.transpose(gates)
        for piece in range(3):
            part = gates.astype(BF16)
            pieces_ref[piece, :, rows] = part
            gates = gates - part.astype(F32)
    base = lax.rem(lax.axis_index("tensor"), 2) * half

    def step(e, carry):
        hot = slot_hot(half, padded, base, post_ref[pl.ds(e, 1), :])
        slot_ref[e] = mm(hot, ub_ref[...]).astype(BF16)
        total = jnp.zeros((8, padded), F32)
        for piece in range(3):
            group = pl.ds(pl.multiple_of(lax.div(e, 16) * 16, 16), 16)
            chosen = lax.broadcasted_iota(jnp.int32, (16, rows_all), 0) == lax.rem(e, 16)
            line = jnp.where(chosen, pieces_ref[piece, group, :].astype(F32), 0.0)
            line = jnp.broadcast_to(jnp.sum(line, axis=0, keepdims=True), (8, rows_all))
            total = total + mm_nt(line.astype(BF16), hot)
        gate_ref[e] = total
        return carry

    lax.fori_loop(0, experts, step, 0)


def expert_kernel(
    sources,
    padded,
    x_ref,
    dy_ref,
    gate_ref,
    *refs,
):
    weights, outs = refs[:8], refs[8:19]
    in_refs, down_refs = weights[0:4], weights[4:8]
    gy_ref, dx_ref, dg_ref = outs[0:3]
    gin_refs, gdown_refs = outs[3:7], outs[7:11]
    xt_ref, scaled_ref, scale_ref, y_acc, dx_acc, win_ref, wdown_ref = refs[19:]
    step = pl.program_id(0)
    last = pl.num_programs(0) - 1

    @pl.when(step == 0)
    def _():
        xt_ref[...] = jnp.transpose(x_ref[...])
        for s in range(sources):
            rows = pl.ds(s * padded, padded)
            line = jnp.broadcast_to(gate_ref[s, 0:1, :], (LANES, padded))
            scale = jnp.transpose(line)
            scale_ref[rows, :] = scale
            scaled_ref[rows, :] = (dy_ref[rows, :].astype(F32) * scale[:, 0:1]).astype(BF16)
        y_acc[...] = jnp.zeros_like(y_acc)
        dx_acc[...] = jnp.zeros_like(dx_acc)

    per = pl.num_programs(0) // 4
    for i in range(4):

        @pl.when(lax.div(step, per) == i)
        def _():
            win_ref[...] = in_refs[i][0]
            wdown_ref[...] = down_refs[i][0]

    x = x_ref[...]
    gate = mm(x, win_ref[0])
    up = mm(x, win_ref[1])
    sigma = 1.0 / (1.0 + jnp.exp(-gate))
    active = gate * sigma
    hidden = (active * up).astype(BF16)
    y_acc[...] += mm(hidden, wdown_ref[...])
    scaled = scaled_ref[...]
    grad_hidden = mm_nt(scaled, wdown_ref[...])
    grad_gate = (grad_hidden * up * (sigma * (1.0 + gate * (1.0 - sigma)))).astype(BF16)
    grad_up = (grad_hidden * active).astype(BF16)
    dx_acc[...] += mm_nt(grad_gate, win_ref[0]) + mm_nt(grad_up, win_ref[1])
    xt = xt_ref[...]
    part_gate = mm(xt, grad_gate).astype(BF16)
    part_up = mm(xt, grad_up).astype(BF16)
    part_down = mm_tn(hidden, scaled).astype(BF16)
    for i in range(4):

        @pl.when(lax.div(step, per) == i)
        def _():
            gin_refs[i][0, 0] = part_gate
            gin_refs[i][0, 1] = part_up
            gdown_refs[i][0] = part_down

    @pl.when(step == last)
    def _():
        for s in range(sources):
            rows = pl.ds(s * padded, padded)
            y = y_acc[rows, :]
            gy_ref[s] = (y * scale_ref[rows, 0:1]).astype(BF16)
            dot = jnp.sum(y * dy_ref[rows, :].astype(F32), axis=-1, keepdims=True)
            dg_ref[s] = jnp.transpose(jnp.broadcast_to(dot, (padded, LANES)))[0:8, :]
            dx_ref[s] = dx_acc[rows, :].astype(BF16)


def back_kernel(
    experts,
    half,
    padded,
    h_ref,
    ub_ref,
    stat_ref,
    routes_ref,
    pos_ref,
    dy_ref,
    gy_ref,
    dx_ref,
    dg_ref,
    small_ref,
    gain_ref,
    vec_ref,
    o_ref,
    wo_ref,
    result_ref,
    prev_ref,
    dh_ref,
    do_ref,
    grad_wo_ref,
    grad_small_ref,
    mixed_ref,
    low_ref,
    dzb_ref,
    row_ref,
):
    rows_all = h_ref.shape[0]
    width = h_ref.shape[1]
    row_ref[...] = jnp.zeros_like(row_ref)
    columns = experts + 4
    for i in range(rows_all // BLK):
        rows = pl.ds(i * BLK, BLK)
        ids = lane_ids(BLK)
        stats = stat_ref[rows, :]
        g0, g1, a00, a01, a10, a11, r = [stats[:, j : j + 1] for j in range(7)]
        e0, e1 = routes_ref[rows, 0:1], routes_ref[rows, 1:2]
        hot0, hot1 = ids == e0, ids == e1
        places = pos_ref[rows, :]
        sums = jnp.zeros((BLK, width), F32)
        grads = jnp.zeros((BLK, width), F32)
        gate_grads = jnp.zeros((BLK, LANES), F32)

        def step(e, carry):
            sums, grads, gate_grads = carry
            place = pick(ids == e, places)
            for side in range(2):
                slot = lax.broadcasted_iota(jnp.int32, (BLK, padded), 1)
                wanted = jnp.where(slot < half, slot + side * half, -2).astype(F32)
                hot = wanted == place
                low = hot.astype(F32).astype(BF16)
                sums = sums + mm(low, gy_ref[side, e])
                grads = grads + mm(low, dx_ref[side, e])
                value = jnp.sum(
                    jnp.where(hot, dg_ref[side, e, 0:1, :], 0.0), axis=-1, keepdims=True
                )
                gate_grads = gate_grads + jnp.where(ids == e, value, 0.0)
            return sums, grads, gate_grads

        sums, grads, gate_grads = lax.fori_loop(
            0, experts, step, (sums, grads, gate_grads)
        )
        h = h_ref[rows, :]
        n = h * r
        u = n * gain_ref[...]
        dy = dy_ref[rows, :].astype(F32)
        vec0, vec1 = vec_ref[0:1, :], vec_ref[1:2, :]

        def named(number):
            return jnp.where(e0 == number, g0, 0.0) + jnp.where(e1 == number, g1, 0.0)

        copied, first, second = named(experts + 1), named(experts + 2), named(experts + 3)
        on_u = copied + first * a00 + second * a10
        result = h + (sums + on_u * u + (first * a01) * vec0 + (second * a11) * vec1)
        result_ref[rows, :] = result.astype(BF16)
        s_u = jnp.sum(dy * u, axis=-1, keepdims=True)
        s_0 = jnp.sum(dy * vec0, axis=-1, keepdims=True)
        s_1 = jnp.sum(dy * vec1, axis=-1, keepdims=True)
        table = (
            gate_grads
            + jnp.where(ids == experts + 1, s_u, 0.0)
            + jnp.where(ids == experts + 2, a00 * s_u + a01 * s_0, 0.0)
            + jnp.where(ids == experts + 3, a10 * s_u + a11 * s_1, 0.0)
        )
        dg0, dg1 = pick(hot0, table), pick(hot1, table)
        mean = g0 * dg0 + g1 * dg1
        dl = jnp.where(hot0, g0 * (dg0 - mean), 0.0) + jnp.where(hot1, g1 * (dg1 - mean), 0.0)
        prev_ref[rows, :] = dl
        d00, d01 = first * s_u, first * s_0
        d10, d11 = second * s_u, second * s_1
        m0 = a00 * d00 + a01 * d01
        m1 = a10 * d10 + a11 * d11
        mixing = (
            jnp.where(ids == columns, a00 * (d00 - m0), 0.0)
            + jnp.where(ids == columns + 1, a01 * (d01 - m0), 0.0)
            + jnp.where(ids == columns + 2, a10 * (d10 - m1), 0.0)
            + jnp.where(ids == columns + 3, a11 * (d11 - m1), 0.0)
        )
        low = (dl + mixing).astype(BF16)
        low_ref[rows, :] = low
        du = grads + mm_nt(low, small_ref[...]) + on_u * dy
        row_ref[0:1, :] += jnp.sum(du * n, axis=0, keepdims=True)
        row_ref[1:2, :] += jnp.sum((first * a01) * dy, axis=0, keepdims=True)
        row_ref[2:3, :] += jnp.sum((second * a11) * dy, axis=0, keepdims=True)
        dn = du * gain_ref[...]
        dh = dy + r * (dn - n * jnp.mean(dn * n, axis=-1, keepdims=True))
        dh_ref[rows, :] = dh
        dzb = dh.astype(BF16)
        dzb_ref[rows, :] = dzb
        do_ref[rows, :] = mm(dzb, wo_ref[...]).astype(BF16)
    grad_wo_ref[...] = mm_tn(dzb_ref[...], o_ref[...]).astype(BF16)
    lines = jnp.concatenate([row_ref[...], jnp.zeros((LANES - 8, width), F32)], axis=0)
    grad_small_ref[...] = mm_tn(ub_ref[...], low_ref[...])
    mixed_ref[...] = jnp.transpose(lines)


def attention_back_kernel(
    q_ref,
    k_ref,
    v_ref,
    do_ref,
    lse_ref,
    a_ref,
    w_ref,
    cos_ref,
    sin_ref,
    da_ref,
    grad_w_ref,
    dp_ref,
    dk_acc,
    dv_acc,
):
    width = q_ref.shape[1]
    pairs = width // LANES
    blocks = LEN // BLK
    head = lax.broadcasted_iota(jnp.int32, (BLK, LANES), 1) < HD
    for p in range(pairs):
        lanes = pl.ds(p * LANES, LANES)
        dk_acc[...] = jnp.zeros_like(dk_acc)
        dv_acc[...] = jnp.zeros_like(dv_acc)
        for i in range(blocks):
            rows = pl.ds(i * BLK, BLK)
            seen = pl.ds(0, (i + 1) * BLK)
            q, do = q_ref[rows, lanes], do_ref[rows, lanes]
            k, v = k_ref[seen, lanes], v_ref[seen, lanes]
            zero = jnp.zeros_like(q)
            parts = []
            dk = dk_acc[seen, :]
            dv = dv_acc[seen, :]
            for side in range(2):
                mask = head if side == 0 else jnp.logical_not(head)
                qm, dom = jnp.where(mask, q, zero), jnp.where(mask, do, zero)
                log_total = lse_ref[2 * p + side : 2 * p + side + 1, rows]
                prob = jnp.exp(mm_nt(k, qm) - log_total)
                grad_prob = mm_nt(v, dom)
                total = jnp.sum(prob * grad_prob, axis=0, keepdims=True)
                grad_score = (prob * (grad_prob - total)).astype(BF16)
                dv = dv + mm(prob.astype(BF16), dom)
                dk = dk + mm(grad_score, qm)
                parts.append(mm_tn(grad_score, k))
            dk_acc[seen, :] = dk
            dv_acc[seen, :] = dv
            dq = jnp.where(head, parts[0], parts[1]) * (HD**-0.5)
            dp_ref[rows, lanes] = turn(dq, cos_ref[rows, :], -sin_ref[rows, :]).astype(BF16)
        dp_ref[:, pl.ds(width + p * LANES, LANES)] = turn(
            dk_acc[...], cos_ref[...], -sin_ref[...]
        ).astype(BF16)
        dp_ref[:, pl.ds(2 * width + p * LANES, LANES)] = dv_acc[...].astype(BF16)
    for i in range(blocks):
        rows = pl.ds(i * BLK, BLK)
        da_ref[rows, :] = mm_nt(dp_ref[rows, :], w_ref[...]).astype(BF16)
    for j in range(3 * pairs):
        lanes = pl.ds(j * LANES, LANES)
        grad_w_ref[:, lanes] = mm_tn(a_ref[...], dp_ref[:, lanes]).astype(BF16)


def finish_kernel(x_ref, dh_ref, da_ref, gain_ref, grad_ref, row_ref):
    rows_all, width = x_ref.shape
    total = jnp.zeros((1, width), F32)
    for i in range(rows_all // BLK):
        rows = pl.ds(i * BLK, BLK)
        x = x_ref[rows, :].astype(F32)
        r = lax.rsqrt(jnp.mean(x * x, axis=-1, keepdims=True) + EPSILON)
        n = x * r
        da = da_ref[0, rows, :].astype(F32) + da_ref[1, rows, :].astype(F32)
        total = total + jnp.sum(da * n, axis=0, keepdims=True)
        dn = da * gain_ref[...]
        grad = dh_ref[rows, :] + r * (dn - n * jnp.mean(dn * n, axis=-1, keepdims=True))
        grad_ref[rows, :] = grad.astype(BF16)
    row_ref[...] = jnp.broadcast_to(total, row_ref.shape)


def across_chips(value):
    return lax.ppermute(value, "tensor", [(0, 2), (2, 0), (1, 3), (3, 1)])


def across_cores(value):
    return lax.ppermute(value, "tensor", [(0, 1), (1, 0), (2, 3), (3, 2)])


def body(
    tokens,
    cotangent,
    prev_logits,
    routes,
    norm_attn,
    norm_moe,
    w_qkv,
    w_out,
    w_router,
    w_const,
    const_vec,
    w_in,
    w_down,
):
    rows, width = tokens.shape[1:]
    n = lax.axis_size("dp")
    experts = n
    columns = prev_logits.shape[2]
    capacity = 4 * max(1, 3 * rows // (4 * (experts + 4)))
    half = capacity // 2
    padded = -(-half // 16) * 16
    share = w_qkv.shape[2]
    local = 2 * share
    part = w_qkv.shape[1]
    t = lax.axis_index("tensor")
    m, c = t // 2, t % 2

    def mine(value):
        return lax.dynamic_index_in_dim(value, m, 0, keepdims=False)

    x, dy, choose = mine(tokens), mine(cotangent), mine(routes)
    prev = jnp.pad(mine(prev_logits), ((0, 0), (0, LANES - columns)))
    cosine, sine = (jnp.asarray(v) for v in rope_constants())

    small = jnp.concatenate(
        [
            w_router,
            w_const,
            norm_attn[:, None],
            norm_moe[:, None],
            const_vec.T,
            jnp.zeros((part, LANES - columns - 8), BF16),
        ],
        axis=1,
    )
    packed = jnp.concatenate([w_qkv[0], w_qkv[1], w_qkv[2], w_out.T, small], axis=1)
    spread = gather_weights(0, n, packed).reshape(2, n * part, packed.shape[1])
    w_heads = jnp.concatenate(
        [spread[j, :, i * share : (i + 1) * share] for i in range(3) for j in range(2)], axis=1
    )
    wo_own = jnp.concatenate(
        [spread[j, :, 3 * share : 4 * share] for j in range(2)], axis=1
    )
    table = spread[0, :, 4 * share :]
    extra = table[:, columns + 4 : columns + 8].astype(F32).T
    gain_attn, gain_moe, vectors = extra[0:1], extra[1:2], extra[2:4]
    keep = jnp.arange(LANES) < columns + 4
    small_all = jnp.where(keep[None, :], table, jnp.zeros_like(table))
    wo_all = core_share(1, wo_own)[0]

    in_x, down_x = across_chips(w_in), across_chips(w_down)
    in_c, down_c = across_cores(w_in), across_cores(w_down)
    in_d, down_d = across_cores(in_x), across_cores(down_x)

    pos, post, dy_slots = compute_call(
        functools.partial(route_kernel, experts, half, padded),
        [
            struct((rows, LANES), F32),
            struct((LANES, rows), F32),
            struct((experts, padded, width), BF16),
        ],
        choose,
        choose.T,
        dy,
        flops=2 * experts * padded * rows * width,
    )
    dy_arrived = lax.all_to_all(dy_slots, "dp", split_axis=0, concat_axis=0, tiled=True)

    a, q, k, v, o, lse = compute_call(
        attention_kernel,
        [
            struct((rows, width), BF16),
            struct((rows, local), BF16),
            struct((rows, local), BF16),
            struct((rows, local), BF16),
            struct((rows, local), BF16),
            struct((8, rows), F32),
        ],
        x,
        gain_attn,
        w_heads,
        cosine,
        sine,
        flops=2 * rows * width * 3 * local + 8 * rows * rows * local,
    )
    o_all = core_share(2, o)[0]
    h, ub, stats, slots, gate_slots = compute_call(
        functools.partial(middle_kernel, experts, half, padded),
        [
            struct((rows, width), F32),
            struct((rows, width), BF16),
            struct((rows, LANES), F32),
            struct((experts, padded, width), BF16),
            struct((experts, 8, padded), F32),
        ],
        x,
        o_all,
        wo_all,
        small_all,
        gain_moe,
        prev,
        choose,
        post,
        flops=4 * rows * width * width + 2 * experts * padded * rows * width,
        scratch=[pltpu.VMEM((3, LANES, rows), BF16)],
    )
    arrived, gate_arrived = dispatch(3, n, slots, gate_slots)

    hidden_width = w_in.shape[3]
    slots_all = experts * padded
    chunk = min(256 if slots_all <= 1024 else 128, hidden_width)
    per = hidden_width // chunk

    def in_map(i):
        return lambda f: (0, 0, 0, jnp.clip(f - per * i, 0, per - 1))

    def down_map(i):
        return lambda f: (0, jnp.clip(f - per * i, 0, per - 1), 0)

    in_blocks = [pl.BlockSpec((1, 2, width, chunk), in_map(i)) for i in range(4)]
    down_blocks = [pl.BlockSpec((1, chunk, width), down_map(i)) for i in range(4)]
    expert_outs = (
        [
            struct((n, padded, width), BF16),
            struct((n, padded, width), BF16),
            struct((n, 8, padded), F32),
        ]
        + [struct(w_in.shape, BF16)] * 4
        + [struct(w_down.shape, BF16)] * 4
    )

    def whole(shape):
        return pl.BlockSpec(
            shape, lambda f: (0,) * len(shape), pipeline_mode=pl.Buffered(1)
        )

    parts = pl.pallas_call(
        functools.partial(expert_kernel, n, padded),
        grid=(4 * per,),
        out_shape=expert_outs,
        in_specs=[
            whole((slots_all, width)),
            whole((slots_all, width)),
            whole((n, 8, padded)),
        ]
        + in_blocks
        + down_blocks,
        out_specs=[
            whole((n, padded, width)),
            whole((n, padded, width)),
            whole((n, 8, padded)),
        ]
        + in_blocks
        + down_blocks,
        scratch_shapes=[
            pltpu.VMEM((width, slots_all), BF16),
            pltpu.VMEM((slots_all, width), BF16),
            pltpu.VMEM((slots_all, LANES), F32),
            pltpu.VMEM((slots_all, width), F32),
            pltpu.VMEM((slots_all, width), F32),
            pltpu.VMEM((2, width, chunk), BF16),
            pltpu.VMEM((chunk, width), BF16),
        ],
        compiler_params=pltpu.CompilerParams(vmem_limit_bytes=VMEM_LIMIT),
        cost_estimate=pl.CostEstimate(
            flops=18 * slots_all * width * 4 * hidden_width,
            bytes_accessed=30_000_000,
            transcendentals=0,
        ),
    )(
        arrived.reshape(slots_all, width),
        dy_arrived.reshape(slots_all, width),
        gate_arrived,
        w_in,
        in_c,
        in_x,
        in_d,
        w_down,
        down_c,
        down_x,
        down_d,
    )
    gy, dx, dg = parts[0:3]
    gin, gdown = parts[3:7], parts[7:11]
    gy_all, dx_all, dg_all = give_back(4, n, gy, dx, dg)

    def total_in(own, core, chip, diagonal):
        own = own.astype(F32) + across_cores(core).astype(F32)
        chip = (chip.astype(F32) + across_cores(diagonal).astype(F32)).astype(BF16)
        return own + across_chips(chip).astype(F32)

    grad_in = total_in(*gin)
    grad_down = total_in(*gdown)

    result, dl, dh, do, grad_wo, grad_small, grad_lines = compute_call(
        functools.partial(back_kernel, experts, half, padded),
        [
            struct((rows, width), BF16),
            struct((rows, LANES), F32),
            struct((rows, width), F32),
            struct((rows, local), BF16),
            struct((width, local), BF16),
            struct((width, LANES), F32),
            struct((width, LANES), F32),
        ],
        h,
        ub,
        stats,
        choose,
        pos,
        dy,
        gy_all,
        dx_all,
        dg_all,
        small_all,
        gain_moe,
        vectors,
        o,
        wo_own,
        flops=8 * experts * padded * rows * width,
        scratch=[
            pltpu.VMEM((rows, LANES), BF16),
            pltpu.VMEM((rows, width), BF16),
            pltpu.VMEM((8, width), F32),
        ],
    )
    results = share_output(5, result)
    da, grad_heads = compute_call(
        attention_back_kernel,
        [struct((rows, width), BF16), struct((width, 3 * local), BF16)],
        q,
        k,
        v,
        do,
        lse,
        a,
        w_heads,
        cosine,
        sine,
        flops=4 * rows * width * 3 * local + 20 * rows * rows * local,
        scratch=[
            pltpu.VMEM((rows, 3 * local), BF16),
            pltpu.VMEM((rows, LANES), F32),
            pltpu.VMEM((rows, LANES), F32),
        ],
    )
    da_all = core_share(6, da)[0]
    grad_x, grad_line = compute_call(
        finish_kernel,
        [struct((rows, width), BF16), struct((8, width), F32)],
        x,
        dh,
        da_all,
        gain_attn,
    )
    input_grads = share_output(7, grad_x)

    grads = jnp.stack(
        [
            jnp.concatenate(
                [
                    grad_heads[:, (2 * i + j) * share : (2 * i + j + 1) * share]
                    for i in range(3)
                ]
                + [grad_wo[:, j * share : (j + 1) * share]],
                axis=1,
            )
            for j in range(2)
        ]
    ).reshape(2, n, part, 4 * share)
    lines = grad_small + jnp.pad(
        jnp.concatenate([grad_line[0:1].T, grad_lines[:, 0:3]], axis=1),
        ((0, 0), (columns + 4, LANES - columns - 8)),
    )
    lines = jnp.broadcast_to(lines.reshape(1, n, part, LANES), (2, n, part, LANES))
    grads_in, lines_in = spread_gradients(8, n, grads, lines)
    grads = jnp.sum(grads_in.astype(F32), axis=(0, 1))
    lines = jnp.sum(lines_in, axis=(0, 1))
    dl = dl[:, :columns]
    dl_x = across_chips(dl)
    logit_grads = jnp.where(m == 0, jnp.stack([dl, dl_x]), jnp.stack([dl_x, dl]))
    return (
        results,
        input_grads,
        logit_grads,
        lines[:, columns + 4],
        lines[:, columns + 5],
        jnp.stack([grads[:, i * share : (i + 1) * share] for i in range(3)]),
        grads[:, 3 * share :].T,
        lines[:, :columns],
        lines[:, columns : columns + 4],
        lines[:, columns + 6 : columns + 8].T,
        grad_in,
        grad_down,
    )


def solution(mesh):
    in_specs = (
        P(None, "dp", None),
        P(None, "dp", None),
        P(None, "dp", None),
        P(None, "dp", None),
        P("dp"),
        P("dp"),
        P(None, "dp", "tensor"),
        P("tensor", "dp"),
        P("dp", None),
        P("dp", None),
        P(None, "dp"),
        P("dp", None, None, "tensor"),
        P("dp", "tensor", None),
    )
    out_specs = (
        P(None, "dp", None),
        P(None, "dp", None),
        P(None, "dp", None),
        P("dp"),
        P("dp"),
        P(None, "dp", "tensor"),
        P("tensor", "dp"),
        P("dp", None),
        P("dp", None),
        P(None, "dp"),
        P("dp", None, None, "tensor"),
        P("dp", "tensor", None),
    )
    return jax.shard_map(body, mesh=mesh, in_specs=in_specs, out_specs=out_specs, check_vma=False)
```

time: 1590 us -> 739 us (0.46)
  Pallas kernels: 0 us -> 659 us
  waiting for transfers between devices: 659 us -> 0.04 us
  blocking collectives: 364 us -> 0 us
  local copies, waits for them, and re-layouts: 227 us -> 35.3 us
  matrix products: 164 us -> 0 us
  other arithmetic: 109 us -> 18.5 us
  starting transfers between devices: 39.6 us -> 13 us
  between operations: 18.2 us -> 1.31 us
    pallas_call x0 -> x16, Pallas kernels: none -> 659 us  [the longest x9 492 us: comm_call(): pl.pallas_call(kernel, out_shape=outs, in_specs=[aspec()] * len(args), ou...]
    psum x2 -> x0, waiting for transfers between devices: 227 us -> none  [head_total(): return lax.psum(term_sums, 'tensor')]
    all_gather x5 -> x0, blocking collectives: 192 us -> none  [the longest x1 75.9 us: body(): lax.all_gather(const_vec, 'dp', axis=1, tiled=True)]
    dot_general x64 -> x0, matrix products: 159 us -> none  [the longest x2 12.5 us: body(): jnp.dot(grad_arrived, down_weight.T, preferred_element_type=jnp.float32)]
    reduce_scatter x4 -> x0, waiting for transfers between devices: 151 us -> none  [slot_total(): lax.psum_scatter(term_sums, 'tensor', scatter_dimension=1, tiled=True)]
    all_to_all x2 -> x0, blocking collectives: 138 us -> none  [to_experts(): return lax.all_to_all(buffer, 'dp', split_axis=0, concat_axis=0, tiled=True)]
    unnamed x20 -> x0, waiting for transfers between devices: 118 us -> none
    all_to_all x6 -> x1, waiting for transfers between devices: 106 us -> 0.01 us  [body(): lax.all_to_all(dy_slots, 'dp', split_axis=0, concat_axis=0, tiled=True)]
  transfers between devices with their start and end apart: 21 -> 14, of which waited for: 14 -> 0; matrix products, arithmetic and copies ran while one was open for 22% -> 6% of each run, Pallas kernels for 0% -> 84%
where the time goes in v1:
time: 739 us; the launch traced here: 727 us
  Pallas kernels  659 us (89%)
  local copies, waits for them, and re-layouts  35.3 us (5%)
  other arithmetic  18.5 us (3%)
  starting transfers between devices  13 us (2%)
    pallas_call x9, Pallas kernels, comm_call(): pl.pallas_call(kernel, out_shape=outs, in_specs=[aspec()] * len(args), ou...  492 us
    pallas_call x6, Pallas kernels, compute_call(): pl.pallas_call(kernel, out_shape=outs, in_specs=[vspec()] * len(args), ou...  120 us
    pallas_call x1, Pallas kernels, body(): pl.pallas_call(functools.partial(expert_kernel, n, padded), grid=(4 * per...  47.9 us
  transfers between devices with their start and end apart: 14, of which 0 were waited for; matrix products, arithmetic and copies ran while one was open for 6% of the time, Pallas kernels for 84%

profile of v1, /device:TPU:26, one launch (start us, length us, event | category | flops | bytes accessed | tf_op | source)
XLA Modules:
  0.0 727.5 jit_solution(15904452493671555053)
XLA Ops:
  3.0 3.8 dynamic-slice_bitcast_fusion
  6.8 6.3 shard_map.242
  13.2 6.2 all-to-all-start
  19.4 1.5 collective-permute-start.4
  22.7 88.7 %shard_map.238 = bf16[2,8,96,896]{3,2,1,0:T(8,128)(2,1)} custom-call(bf16[96,896]{1,0:T(8,128)(2,1)} %concatenate.19.in_ref), custom_call_target="tpu_custom_call" | custom-call | tf_op jit(solution)/shard_map/pallas_call | solution.py:82
  114.5 3.8 slice_bitcast_fusion.1
  119.4 19.5 %shard_map.241.wo_ref = bf16[2,768,384]{2,1,0:T(8,128)(2,1)} custom-call(bf16[768,384]{1,0:T(8,128)(2,1)} %pad_maximum_fusion.3.refs_0_.wo_ref), custom_call_target="tpu_custom_call" | custom-call | tf_op jit(solution)/shard_map/pallas_call | solution.py:82
  138.8 4.1 concatenate.20.w_ref
  143.6 19.1 %shard_map.239 = (bf16[1024,768]{1,0:T(8,128)(2,1)}, bf16[1024,384]{1,0:T(8,128)(2,1)}, bf16[1024,384]{1,0:T(8,128)(2,1)}, bf16[1024,384]{1,0:T(8,128)(2,1)}, bf...) custom-call(bf16[1024,768]{1,0:T(8,128)(2,1)} %get-tuple-element.188.x_ref, f32[1,768]{1,0:T(1,128)} %get-tuple-element.186.gain_ref, ...), custom_call_target="tpu_custom_call" | custom-call | flops 5033164800 | bytes 9145344 | tf_op jit(solution)/shard_map/pallas_call | solution.py:50
  162.7 25.4 %shard_map.240.o_ref = bf16[2,1024,384]{2,1,0:T(8,128)(2,1)} custom-call(bf16[1024,384]{1,0:T(8,128)(2,1)} %get-tuple-element.55.refs_0_.o_ref), custom_call_target="tpu_custom_call" | custom-call | tf_op jit(solution)/shard_map/pallas_call | solution.py:82
  189.0 13.8 %shard_map.243 = (f32[1024,768]{1,0:T(8,128)}, bf16[1024,768]{1,0:T(8,128)(2,1)}, f32[1024,128]{1,0:T(8,128)}, bf16[8,128,768]{2,1,0:T(8,128)(2,1)}, f32[8,8,128]{2,1,0:T(8,128)}) custom-call(bf16[1024,768]{1,0:T(8,128)(2,1)} %get-tuple-element.188.x_ref, bf16[2,1024,384]{2,1,0:T(8,128)(2,1)} %shard_map.240.o_ref, bf16[2,768,384]{2,1,0:T(8,128)(2,1)} %shard_map.241.wo_ref, ...), custom_call_target="tpu_custom_call" | custom-call | flops 4026531840 | bytes 12430336 | tf_op jit(solution)/shard_map/pallas_call | solution.py:50
  202.8 42.3 %shard_map.244 = (bf16[8,128,768]{2,1,0:T(8,128)(2,1)}, f32[8,8,128]{2,1,0:T(8,128)}) custom-call(bf16[8,128,768]{2,1,0:T(8,128)(2,1)} %get-tuple-element.61.refs_0_, f32[8,8,128]{2,1,0:T(8,128)} %get-tuple-element.62.refs_1_), custom_call_target="tpu_custom_call" | custom-call | tf_op jit(solution)/shard_map/pallas_call | solution.py:82
  246.5 47.9 %shard_map.245 = (bf16[8,128,768]{2,1,0:T(8,128)(2,1)}, bf16[8,128,768]{2,1,0:T(8,128)(2,1)}, f32[8,8,128]{2,1,0:T(8,128)}, bf16[1,2,768,512]{3,2,1,0:T(8,128)(2...) custom-call(bf16[1024,768]{1,0:T(8,128)(2,1)} %bitcast.79, ...), custom_call_target="tpu_custom_call" | custom-call | flops 28991029248 | bytes 30000000 | tf_op jit(solution)/shard_map/pallas_call | solution.py:882
  295.5 75.0 %shard_map.246 = (bf16[2,8,128,768]{3,2,1,0:T(8,128)(2,1)}, bf16[2,8,128,768]{3,2,1,0:T(8,128)(2,1)}, f32[2,8,8,128]{3,2,1,0:T(8,128)}) custom-call(bf16[8,128,768]{2,1,0:T(8,128)(2,1)} %get-tuple-element.66.refs_0_, bf16[8,128,768]{2,1,0:T(8,128)(2,1)} %get-tuple-element.67.refs_1_, f32[8,8,128]{2,1,0:T(8,128)} %get-tuple-element.68.refs_2_), custom_call_target="tpu_custom_call" | custom-call | tf_op jit(solution)/shard_map/pallas_call | solution.py:82
  370.5 48.7 %shard_map.247 = (bf16[1024,768]{1,0:T(8,128)(2,1)}, f32[1024,128]{1,0:T(8,128)}, f32[1024,768]{1,0:T(8,128)}, bf16[1024,384]{1,0:T(8,128)(2,1)}, bf16[768,384]{...) custom-call(f32[1024,768]{1,0:T(8,128)} %get-tuple-element.57.h_ref, ...), custom_call_target="tpu_custom_call" | custom-call | flops 6442450944 | bytes 22692864 | tf_op jit(solution)/shard_map/pallas_call | solution.py:50
  419.1 1.9 slice_bitcast_fusion.17
  421.6 25.6 %shard_map.249 = (bf16[1024,768]{1,0:T(8,128)(2,1)}, bf16[768,1152]{1,0:T(8,128)(2,1)}) custom-call(bf16[1024,384]{1,0:T(8,128)(2,1)} %get-tuple-element.74.q_ref, bf16[1024,384]{1,0:T(8,128)(2,1)} %get-tuple-element.75.k_ref, bf16[1024,384]{1,0:T(8,128)(2,1)} %get-tuple-element.76.v_ref, bf16[1024,384]{1,0:T(8,128)(2,1)} %get-tuple-element.77.do_ref, ...), custom_call_target="tpu_custom_call" | custom-call | flops 11676942336 | bytes 10911744 | tf_op jit(solution)/shard_map/pallas_call | solution.py:50
  447.1 48.8 %shard_map.250.da_ref = bf16[2,1024,768]{2,1,0:T(8,128)(2,1)} custom-call(bf16[1024,768]{1,0:T(8,128)(2,1)} %get-tuple-element.80.refs_0_), custom_call_target="tpu_custom_call" | custom-call | tf_op jit(solution)/shard_map/pallas_call | solution.py:82
  496.0 6.4 shard_map.251
  505.5 1.6 pad_maximum_fusion.refs_0_
  508.3 75.6 %shard_map.253 = (bf16[2,8,96,768]{3,2,1,0:T(8,128)(2,1)}, f32[2,8,96,128]{3,2,1,0:T(8,128)}) custom-call(bf16[2,8,96,768]{3,2,1,0:T(8,128)(2,1)} %pad_maximum_fusion.refs_0_, f32[2,8,96,128]{3,2,1,0:T(8,128)} %broadcast_in_dim.34.refs_1_), custom_call_target="tpu_custom_call" | custom-call | tf_op jit(solution)/shard_map/pallas_call | solution.py:82
  585.2 3.1 add_convert_fusion
  588.3 1.9 collective-permute-start.9
  590.5 1.4 add_convert_fusion.1
  594.6 65.7 %shard_map.248 = bf16[2,1024,768]{2,1,0:T(8,128)(2,1)} custom-call(bf16[1024,768]{1,0:T(8,128)(2,1)} %get-tuple-element.72.in_ref), custom_call_target="tpu_custom_call" | custom-call | tf_op jit(solution)/shard_map/pallas_call | solution.py:82
  660.3 50.6 %shard_map.252 = bf16[2,1024,768]{2,1,0:T(8,128)(2,1)} custom-call(bf16[1024,768]{1,0:T(8,128)(2,1)} %get-tuple-element.81.in_ref), custom_call_target="tpu_custom_call" | custom-call | tf_op jit(solution)/shard_map/pallas_call | solution.py:82
  713.6 1.2 copy.117
  715.6 3.1 convert_add_fusion.1
  718.8 3.8 convert_add_fusion
  722.6 1.7 copy.128
  724.3 1.4 copy-done.3
  725.6 1.7 copy.129
  (113 shorter events, 24.7 us)
Async XLA Ops:
  0.6 112.1 %copy-start = (f32[2,1024,12]{1,0,2:T(2,128)S(1)}, f32[2,1024,12]{1,0,2:T(2,128)}, u32[]{:S(2)}) copy-start(f32[2,1024,12]{1,0,2:T(2,128)} %param.17) | copy-start | bytes 294916
  0.7 112.0 %collective-permute-start.1 = (bf16[1,2,768,512]{3,2,1,0:T(8,128)(2,1)}, bf16[1,2,768,512]{3,2,1,0:T(8,128)(2,1)}, u32[]{:S(2)}, u32[]{:S(2)}) collective-permute-start(bf16[1,2,768,512]{3,2,1,0:T(8,128)(2,1)} %refs_0_.1), channel_id=1, source_target_pairs={{0,2},{2,0},{1,3},{3,1},{4,6},{6,4},{5,7},{7,5},{8,10},{10,8},{9,1... | collective-permute-start | bytes 4718600 | tf_op jit(solution)/shard_map/ppermute | solution.py:728
  2.2 4.6 copy-start.6
  13.1 8.0 %copy-start.18 = (bf16[96]{0:T(256)(128)(2,1)S(1)}, bf16[96]{0:T(256)(128)(2,1)}, u32[]{:S(2)}) copy-start(bf16[96]{0:T(256)(128)(2,1)} %param.19) | copy-start | bytes 580
  13.1 8.1 %copy-start.19 = (bf16[96]{0:T(256)(128)(2,1)S(1)}, bf16[96]{0:T(256)(128)(2,1)}, u32[]{:S(2)}) copy-start(bf16[96]{0:T(256)(128)(2,1)} %param.20) | copy-start | bytes 580
  13.1 8.2 %copy-start.16 = (bf16[96,12]{0,1:T(8,128)(2,1)S(1)}, bf16[96,12]{0,1:T(8,128)(2,1)}, u32[]{:S(2)}) copy-start(bf16[96,12]{0,1:T(8,128)(2,1)} %param.23) | copy-start | bytes 6916
  13.1 8.3 %copy-start.17 = (bf16[96,4]{0,1:T(4,128)(2,1)S(1)}, bf16[96,4]{0,1:T(4,128)(2,1)}, u32[]{:S(2)}) copy-start(bf16[96,4]{0,1:T(4,128)(2,1)} %param.24) | copy-start | bytes 2308
  13.1 8.5 %copy-start.20 = (bf16[2,96]{1,0:T(2,128)(2,1)S(1)}, bf16[2,96]{1,0:T(2,128)(2,1)}, u32[]{:S(2)}) copy-start(bf16[2,96]{1,0:T(2,128)(2,1)} %param.25) | copy-start | bytes 1156
  13.1 8.6 %copy-start.15 = (bf16[192,96]{1,0:T(8,128)(2,1)S(1)}, bf16[192,96]{1,0:T(8,128)(2,1)}, u32[]{:S(2)}) copy-start(bf16[192,96]{1,0:T(8,128)(2,1)} %param.22) | copy-start | bytes 110596
  13.1 8.7 %copy-start.14 = (bf16[3,96,192]{2,1,0:T(8,128)(2,1)S(1)}, bf16[3,96,192]{2,1,0:T(8,128)(2,1)}, u32[]{:S(2)}) copy-start(bf16[3,96,192]{2,1,0:T(8,128)(2,1)} %param.21) | copy-start | bytes 331780
  13.2 232.0 %all-to-all-start = ((bf16[8,128,768]{2,1,0:T(8,128)(2,1)}), bf16[8,128,768]{2,1,0:T(8,128)(2,1)S(1)}, u32[]{:S(2)}, u32[]{:S(2)}) async-start(bf16[8,128,768]{2,1,0:T(8,128)(2,1)} %get-tuple-element.64), calls=%async_computation | async-start | bytes 3145728 | tf_op jit(solution)/shard_map/all_to_all | solution.py:812
  19.3 225.7 %collective-permute-start.3 = (bf16[1,512,768]{2,1,0:T(8,128)(2,1)}, bf16[1,512,768]{2,1,0:T(8,128)(2,1)}, u32[]{:S(2)}, u32[]{:S(2)}) collective-permute-start(bf16[1,512,768]{2,1,0:T(8,128)(2,1)} %refs_4_.1), channel_id=1, source_target_pairs={{0,1},{1,0},{2,3},{3,2},{4,5},{5,4},{6,7},{7,6},{8,9},{9,8},{10,11... | collective-permute-start | bytes 2359304 | tf_op jit(solution)/shard_map/ppermute | solution.py:732
  19.4 124.2 %collective-permute-start.4 = (bf16[1,512,768]{2,1,0:T(8,128)(2,1)}, bf16[1,512,768]{2,1,0:T(8,128)(2,1)}, u32[]{:S(2)}, u32[]{:S(2)}) collective-permute-start(bf16[1,512,768]{2,1,0:T(8,128)(2,1)} %refs_4_.1), channel_id=1, source_target_pairs={{0,2},{2,0},{1,3},{3,1},{4,6},{6,4},{5,7},{7,5},{8,10},{10,8},{9,1... | collective-permute-start | bytes 2359304 | tf_op jit(solution)/shard_map/ppermute | solution.py:728
  20.8 224.3 %collective-permute-start = (bf16[1,2,768,512]{3,2,1,0:T(8,128)(2,1)}, bf16[1,2,768,512]{3,2,1,0:T(8,128)(2,1)}, u32[]{:S(2)}, u32[]{:S(2)}) collective-permute-start(bf16[1,2,768,512]{3,2,1,0:T(8,128)(2,1)} %refs_0_.1), channel_id=1, source_target_pairs={{0,1},{1,0},{2,3},{3,2},{4,5},{5,4},{6,7},{7,6},{8,9},{9,8},{10,11... | collective-permute-start | bytes 4718600 | tf_op jit(solution)/shard_map/ppermute | solution.py:732
  112.7 132.5 %collective-permute-start.2 = (bf16[1,2,768,512]{3,2,1,0:T(8,128)(2,1)}, bf16[1,2,768,512]{3,2,1,0:T(8,128)(2,1)}, u32[]{:S(2)}, u32[]{:S(2)}) collective-permute-start(bf16[1,2,768,512]{3,2,1,0:T(8,128)(2,1)} %collective-permute-done.1.refs_2_), channel_id=1, source_target_pairs={{0,1},{1,0},{2,3},{3,2},{4,5},{5,4},{6,7},{7,6},{8,9},{9,8},{10,11... | collective-permute-start | bytes 4718600 | tf_op jit(solution)/shard_map/ppermute | solution.py:732
  143.6 101.5 %collective-permute-start.5 = (bf16[1,512,768]{2,1,0:T(8,128)(2,1)}, bf16[1,512,768]{2,1,0:T(8,128)(2,1)S(1)}, u32[]{:S(2)}, u32[]{:S(2)}) collective-permute-start(bf16[1,512,768]{2,1,0:T(8,128)(2,1)} %collective-permute-done.4.refs_6_), channel_id=1, source_target_pairs={{0,1},{1,0},{2,3},{3,2},{4,5},{5,4},{6,7},{7,6},{8,9},{9,8},{10,11... | collective-permute-start | bytes 2359304 | tf_op jit(solution)/shard_map/ppermute | solution.py:732
  294.4 421.2 %collective-permute-start.10 = (bf16[1,512,768]{2,1,0:T(8,128)(2,1)}, bf16[1,512,768]{2,1,0:T(8,128)(2,1)}, u32[]{:S(2)}, u32[]{:S(2)}) collective-permute-start(bf16[1,512,768]{2,1,0:T(8,128)(2,1)} %get-tuple-element.95), channel_id=1, source_target_pairs={{0,1},{1,0},{2,3},{3,2},{4,5},{5,4},{6,7},{7,6},{8,9},{9,8},{10,11... | collective-permute-start | bytes 2359304 | tf_op jit(solution)/shard_map/ppermute | solution.py:732
  294.5 296.0 %collective-permute-start.11 = (bf16[1,512,768]{2,1,0:T(8,128)(2,1)}, bf16[1,512,768]{2,1,0:T(8,128)(2,1)}, u32[]{:S(2)}, u32[]{:S(2)}) collective-permute-start(bf16[1,512,768]{2,1,0:T(8,128)(2,1)} %get-tuple-element.97), channel_id=1, source_target_pairs={{0,1},{1,0},{2,3},{3,2},{4,5},{5,4},{6,7},{7,6},{8,9},{9,8},{10,11... | collective-permute-start | bytes 2359304 | tf_op jit(solution)/shard_map/ppermute | solution.py:732
  295.0 423.8 %collective-permute-start.7 = (bf16[1,2,768,512]{3,2,1,0:T(8,128)(2,1)}, bf16[1,2,768,512]{3,2,1,0:T(8,128)(2,1)}, u32[]{:S(2)}, u32[]{:S(2)}) collective-permute-start(bf16[1,2,768,512]{3,2,1,0:T(8,128)(2,1)} %get-tuple-element.91), channel_id=1, source_target_pairs={{0,1},{1,0},{2,3},{3,2},{4,5},{5,4},{6,7},{7,6},{8,9},{9,8},{10,11... | collective-permute-start | bytes 4718600 | tf_op jit(solution)/shard_map/ppermute | solution.py:732
  295.1 290.1 %collective-permute-start.8 = (bf16[1,2,768,512]{3,2,1,0:T(8,128)(2,1)}, bf16[1,2,768,512]{3,2,1,0:T(8,128)(2,1)}, u32[]{:S(2)}, u32[]{:S(2)}) collective-permute-start(bf16[1,2,768,512]{3,2,1,0:T(8,128)(2,1)} %get-tuple-element.93), channel_id=1, source_target_pairs={{0,1},{1,0},{2,3},{3,2},{4,5},{5,4},{6,7},{7,6},{8,9},{9,8},{10,11... | collective-permute-start | bytes 4718600 | tf_op jit(solution)/shard_map/ppermute | solution.py:732
  421.0 292.5 %collective-permute-start.6 = (f32[1024,12]{1,0:T(8,128)}, f32[1024,12]{1,0:T(8,128)}, u32[]{:S(2)}, u32[]{:S(2)}) collective-permute-start(f32[1024,12]{1,0:T(8,128)} %get-tuple-element.177), channel_id=1, source_target_pairs={{0,2},{2,0},{1,3},{3,1},{4,6},{6,4},{5,7},{7,5},{8,10},{10,8},{9,1... | collective-permute-start | bytes 147464 | tf_op jit(solution)/shard_map/ppermute | solution.py:728
  496.0 7.5 %copy-start.10 = (bf16[768,384]{1,0:T(8,128)(2,1)S(1)}, bf16[768,384]{1,0:T(8,128)(2,1)}, u32[]{:S(2)}) copy-start(bf16[768,384]{1,0:T(8,128)(2,1)} %get-tuple-element.84) | copy-start | bytes 1769476
  505.5 1.6 copy-start.12
  508.3 76.8 %copy-start.8 = (bf16[1,2,768,512]{3,2,1,0:T(8,128)(2,1)S(1)}, bf16[1,2,768,512]{3,2,1,0:T(8,128)(2,1)}, u32[]{:S(2)}) copy-start(bf16[1,2,768,512]{3,2,1,0:T(8,128)(2,1)} %get-tuple-element.92) | copy-start | bytes 4718596
  585.1 5.1 copy-start.5
  588.3 2.2 copy-start.11
  588.3 130.5 %collective-permute-start.9 = (bf16[1,2,768,512]{3,2,1,0:T(8,128)(2,1)}, bf16[1,2,768,512]{3,2,1,0:T(8,128)(2,1)S(1)}, u32[]{:S(2)}, u32[]{:S(2)}) collective-permute-start(bf16[1,2,768,512]{3,2,1,0:T(8,128)(2,1)} %add_convert_fusion), channel_id=1, source_target_pairs={{0,2},{2,0},{1,3},{3,1},{4,6},{6,4},{5,7},{7,5},{8,10},{10,8},{9,1... | collective-permute-start | bytes 4718600 | tf_op jit(solution)/shard_map/ppermute | solution.py:728
  591.9 123.7 %collective-permute-start.12 = (bf16[1,512,768]{2,1,0:T(8,128)(2,1)S(1)}, bf16[1,512,768]{2,1,0:T(8,128)(2,1)}, u32[]{:S(2)}, u32[]{:S(2)}) collective-permute-start(bf16[1,512,768]{2,1,0:T(8,128)(2,1)S(1)} %add_convert_fusion.1), channel_id=1, source_target_pairs={{0,2},{2,0},{1,3},{3,1},{4,6},{6,4},{5,7},{7,5},{8,10},{10,8},{9,1... | collective-permute-start | bytes 2359304 | tf_op jit(solution)/shard_map/ppermute | solution.py:728
  715.6 3.1 copy-start.9
  718.8 3.8 copy-start.2
  722.6 3.0 copy-start.3
  725.6 1.7 copy-start.1
  (4 other events, 5.4 us)

commit v2 on v1

--- a/solution.py
+++ b/solution.py
@@ -118,27 +118,6 @@
 def all_peers(n, d, t):
     other = lax.rem(t + 2, 4)
     return plane_peers(n, d, t) + [(lax.rem(d + j, n), other) for j in range(n)]
-
-
-def gather_weights(cid, n, packed):
-    def kernel(in_ref, out_ref, send, recv, local):
-        d, t = lax.axis_index("dp"), lax.axis_index("tensor")
-        m = lax.div(t, 2)
-        peers = all_peers(n, d, t)
-        greet(peers)
-        mine = pltpu.make_async_copy(in_ref, out_ref.at[m, d], local.at[0])
-        mine.start()
-        copies = []
-        for i, peer in enumerate(peers):
-            copies.append(remote(in_ref, out_ref.at[m, d], send.at[i], recv.at[i], peer))
-        for copy in copies:
-            copy.start()
-        for copy in copies:
-            copy.wait()
-        mine.wait()
-
-    outs = [struct((2, n) + packed.shape, packed.dtype)]
-    return comm_call(kernel, outs, [(2 * n,), (2 * n,), (1,)], cid, packed)[0]
 
 
 def spread_gradients(cid, n, *arrays):
@@ -173,30 +152,6 @@
 
     outs = [struct(a.shape, a.dtype) for a in arrays]
     return comm_call(kernel, outs, [(count, 2 * n), (count, 2 * n), (count,)], cid, *arrays)
-
-
-def dispatch(cid, n, *arrays):
-    count = len(arrays)
-
-    def kernel(*refs):
-        ins, outs, (send, recv, local) = refs[:count], refs[count : 2 * count], refs[2 * count :]
-        d, t = lax.axis_index("dp"), lax.axis_index("tensor")
-        peers = plane_peers(n, d, t)
-        greet(peers)
-        copies = []
-        for k in range(count):
-            copies.append(pltpu.make_async_copy(ins[k].at[d], outs[k].at[d], local.at[k]))
-            for i, (pd, pt) in enumerate(peers):
-                copies.append(
-                    remote(ins[k].at[pd], outs[k].at[d], send.at[k, i], recv.at[k, i], (pd, pt))
-                )
-        for copy in copies:
-            copy.start()
-        for copy in copies:
-            copy.wait()
-
-    outs = [struct(a.shape, a.dtype) for a in arrays]
-    return comm_call(kernel, outs, [(count, n), (count, n), (count,)], cid, *arrays)
 
 
 def give_back(cid, n, *arrays):
@@ -277,38 +232,11 @@
     return comm_call(kernel, outs, [(2,), (2,), (1,)], cid, full)[0]
 
 
-def route_kernel(experts, half, padded, columns_ref, rows_ref, dy_ref, pos_ref, post_ref, slot_ref):
-    rows = columns_ref.shape[0]
-    lanes = post_ref.shape[0]
-    first, second = rows_ref[0:1, :], rows_ref[1:2, :]
-    ids = lax.broadcasted_iota(jnp.int32, (lanes, rows), 0)
-    hit = ((ids == first) | (ids == second)) & (ids < experts)
-    before = (
-        lax.broadcasted_iota(jnp.int32, (rows, rows), 0)
-        < lax.broadcasted_iota(jnp.int32, (rows, rows), 1)
-    )
-    count = mm(hit.astype(F32).astype(BF16), before.astype(F32).astype(BF16))
-    place = jnp.where(hit, count, -1.0)
-    post_ref[...] = place
-    pos_ref[...] = jnp.transpose(place)
-    base = lax.rem(lax.axis_index("tensor"), 2) * half
-    build_slots(experts, half, padded, base, post_ref, dy_ref, slot_ref)
-
-
 def slot_hot(half, padded, base, places):
     rows = places.shape[1]
     slot = lax.broadcasted_iota(jnp.int32, (padded, rows), 0)
     wanted = jnp.where(slot < half, slot + base, -2).astype(F32)
     return (wanted == places).astype(F32).astype(BF16)
-
-
-def build_slots(experts, half, padded, base, post_ref, source_ref, slot_ref):
-    def step(e, carry):
-        hot = slot_hot(half, padded, base, post_ref[pl.ds(e, 1), :])
-        slot_ref[e] = mm(hot, source_ref[...]).astype(BF16)
-        return carry
-
-    lax.fori_loop(0, experts, step, 0)
 
 
 def rope_constants():
@@ -331,132 +259,372 @@
     return field * cosine + other * sine
 
 
-def attention_kernel(
-    x_ref, gain_ref, w_ref, cos_ref, sin_ref, a_ref, q_ref, k_ref, v_ref, o_ref, lse_ref
+def pick(hot, values):
+    return jnp.sum(jnp.where(hot, values, 0.0), axis=-1, keepdims=True)
+
+
+def lane_ids(rows):
+    return lax.broadcasted_iota(jnp.int32, (rows, LANES), 1)
+
+
+def soft_pair(first, second):
+    high = jnp.maximum(first, second)
+    e0, e1 = jnp.exp(first - high), jnp.exp(second - high)
+    return e0 / (e0 + e1), e1 / (e0 + e1)
+
+
+def half_mask(rows):
+    return lax.broadcasted_iota(jnp.int32, (rows, LANES), 1) < HD
+
+
+def swap_halves(value):
+    return pltpu.roll(value, HD, 1)
+
+
+def front_kernel(
+    n,
+    half,
+    padded,
+    gathered,
+    tokens_ref,
+    cotangent_ref,
+    prev_all_ref,
+    routes_all_ref,
+    packed_ref,
+    cos_ref,
+    sin_ref,
+    win_ref,
+    wdown_ref,
+    a_ref,
+    q_ref,
+    k_ref,
+    v_ref,
+    o_ref,
+    lse_ref,
+    h_ref,
+    ub_ref,
+    stat_ref,
+    pos_ref,
+    wo_ref,
+    small_ref,
+    extra_ref,
+    spread_ref,
+    arrived_ref,
+    gate_arrived_ref,
+    dy_arrived_ref,
+    in_c_ref,
+    in_x_ref,
+    in_d_ref,
+    down_c_ref,
+    down_x_ref,
+    down_d_ref,
+    x_ref,
+    dy_ref,
+    prev_ref,
+    routes_ref,
+    place_ref,
+    gates_ref,
+    slot_ref,
+    gate_ref,
+    dy_slot_ref,
+    load,
+    pack_send,
+    pack_recv,
+    dy_send,
+    dy_recv,
+    slot_send,
+    slot_recv,
+    gate_send,
+    gate_recv,
+    stay,
+    core_send,
+    core_recv,
+    w_send,
+    w_recv,
 ):
-    width = q_ref.shape[1]
-    pairs = width // LANES
-    blocks = LEN // BLK
-    for i in range(blocks):
-        rows = pl.ds(i * BLK, BLK)
+    rows_all, width = x_ref.shape
+    blocks = rows_all // BLK
+    pairs = q_ref.shape[0]
+    local = pairs * LANES
+    columns = prev_ref.shape[1]
+    d, t = lax.axis_index("dp"), lax.axis_index("tensor")
+    m, c = lax.div(t, 2), lax.rem(t, 2)
+    partner = (d, t + 1 - 2 * c)
+    across = (d, lax.rem(t + 2, 4))
+    loads = [
+        pltpu.make_async_copy(src.at[m], dst, load.at[i])
+        for i, (src, dst) in enumerate(
+            [
+                (routes_all_ref, routes_ref),
+                (cotangent_ref, dy_ref),
+                (tokens_ref, x_ref),
+                (prev_all_ref, prev_ref),
+            ]
+        )
+    ]
+    for copy in loads:
+        copy.start()
+    peers = all_peers(n, d, t)
+    greet(peers + [partner])
+    pack_copies = []
+    if gathered:
+        spread_ref[...] = packed_ref[...]
+    else:
+        part = packed_ref.shape[0]
+        place = pl.ds(pl.multiple_of(d * part, part), part)
+        spread_ref[m, place, :] = packed_ref[...]
+        for i, peer in enumerate(peers):
+            pack_copies.append(
+                remote(
+                    packed_ref,
+                    spread_ref.at[m, place, :],
+                    pack_send.at[i],
+                    pack_recv.at[i],
+                    peer,
+                )
+            )
+        for copy in pack_copies:
+            copy.start()
+
+    loads[0].wait()
+    line = lax.broadcasted_iota(jnp.int32, (rows_all, LANES), 1)
+    named = jnp.where(
+        line == 0,
+        routes_ref[:, 0:1].astype(F32),
+        jnp.where(line == 1, routes_ref[:, 1:2].astype(F32), 0.0),
+    )
+    named = jnp.transpose(named)
+    ids = lax.broadcasted_iota(jnp.int32, (LANES, rows_all), 0).astype(F32)
+    hit = ((ids == named[0:1, :]) | (ids == named[1:2, :])) & (ids < float(n))
+    before = lax.broadcasted_iota(jnp.int32, (rows_all, rows_all), 0) < lax.broadcasted_iota(
+        jnp.int32, (rows_all, rows_all), 1
+    )
+    count = mm(hit.astype(F32).astype(BF16), before.astype(F32).astype(BF16))
+    places = jnp.where(hit, count, -1.0)
+    place_ref[...] = places
+    pos_ref[...] = jnp.transpose(places)
+    base = c * half
+
+    def dy_copy(j):
+        e = lax.rem(d + j, n)
+        return remote(
+            dy_slot_ref.at[e], dy_arrived_ref.at[d], dy_send.at[j], dy_recv.at[j], (e, t)
+        )
+
+    def slot_copy(j):
+        e = lax.rem(d + j, n)
+        return remote(
+            slot_ref.at[e], arrived_ref.at[d], slot_send.at[j], slot_recv.at[j], (e, t)
+        )
+
+    def gate_copy(j):
+        e = lax.rem(d + j, n)
+        return remote(
+            gate_ref.at[e], gate_arrived_ref.at[d], gate_send.at[j], gate_recv.at[j], (e, t)
+        )
+
+    stays = [
+        pltpu.make_async_copy(src.at[d], dst.at[d], stay.at[i])
+        for i, (src, dst) in enumerate(
+            [
+                (dy_slot_ref, dy_arrived_ref),
+                (slot_ref, arrived_ref),
+                (gate_ref, gate_arrived_ref),
+            ]
+        )
+    ]
+    loads[1].wait()
+
+    def dy_step(i, carry):
+        j = lax.rem(i + 1, n)
+        e = lax.rem(d + j, n)
+        hot = slot_hot(half, padded, base, place_ref[pl.ds(e, 1), :])
+        dy_slot_ref[e] = mm(hot, dy_ref[...]).astype(BF16)
+
+        @pl.when(i < n - 1)
+        def _():
+            dy_copy(j).start()
+
+        return carry
+
+    lax.fori_loop(0, n, dy_step, 0)
+    stays[0].start()
+
+    for copy in pack_copies:
+        copy.wait_recv()
+    weight_copies = [
+        remote(win_ref, in_x_ref, w_send.at[0], w_recv.at[0], across),
+        remote(wdown_ref, down_x_ref, w_send.at[1], w_recv.at[1], across),
+        remote(win_ref, in_c_ref, w_send.at[2], w_recv.at[2], partner),
+        remote(wdown_ref, down_c_ref, w_send.at[3], w_recv.at[3], partner),
+        remote(in_x_ref, in_d_ref, w_send.at[4], w_recv.at[4], partner),
+        remote(down_x_ref, down_d_ref, w_send.at[5], w_recv.at[5], partner),
+    ]
+    for copy in weight_copies[0:4]:
+        copy.start()
+
+    table = spread_ref[0, :, 6 * LANES : 7 * LANES]
+    extra_ref[...] = jnp.transpose(table.astype(F32))
+    keep = lax.broadcasted_iota(jnp.int32, (width, LANES), 1) < columns + 4
+    small_ref[...] = jnp.where(keep, table, jnp.zeros_like(table))
+    mask = half_mask(width)
+    own = pl.multiple_of(c * local, LANES)
+    wo_ref[:, pl.ds(own, LANES)] = spread_ref[0, :, 3 * LANES : 4 * LANES]
+    wo_ref[:, pl.ds(own + LANES, LANES)] = spread_ref[1, :, 3 * LANES : 4 * LANES]
+    wo_ref[:, pl.ds(own + 2 * LANES, LANES)] = jnp.where(
+        mask,
+        swap_halves(spread_ref[0, :, 5 * LANES : 6 * LANES].astype(F32)),
+        spread_ref[1, :, 5 * LANES : 6 * LANES].astype(F32),
+    ).astype(BF16)
+    own_lanes = pl.ds(own, local)
+    wo_copy = remote(
+        wo_ref.at[:, own_lanes],
+        wo_ref.at[:, own_lanes],
+        core_send.at[pairs],
+        core_recv.at[pairs],
+        partner,
+    )
+    wo_copy.start()
+
+    loads[2].wait()
+    gain = extra_ref[columns + 4 : columns + 5, :]
+    head = half_mask(BLK)
+
+    def project(i, carry):
+        rows = pl.ds(pl.multiple_of(i * BLK, BLK), BLK)
         x = x_ref[rows, :].astype(F32)
         r = lax.rsqrt(jnp.mean(x * x, axis=-1, keepdims=True) + EPSILON)
-        a = (x * r * gain_ref[...]).astype(BF16)
+        a = (x * r * gain).astype(BF16)
         a_ref[rows, :] = a
         cosine, sine = cos_ref[rows, :], sin_ref[rows, :]
-        for p in range(pairs):
-            lanes = pl.ds(p * LANES, LANES)
-            q = turn(mm(a, w_ref[:, p * LANES : (p + 1) * LANES]), cosine, sine).astype(BF16)
-            q_ref[rows, lanes] = q * BF16(HD**-0.5)
-            start = width + p * LANES
-            k_ref[rows, lanes] = turn(mm(a, w_ref[:, start : start + LANES]), cosine, sine).astype(
-                BF16
-            )
-            start = 2 * width + p * LANES
-            v_ref[rows, lanes] = mm(a, w_ref[:, start : start + LANES]).astype(BF16)
-    head = lax.broadcasted_iota(jnp.int32, (BLK, LANES), 1) < HD
-    for p in range(pairs):
-        lanes = pl.ds(p * LANES, LANES)
+
+        def put(pair, q, k, v):
+            q_ref[pair, rows, :] = turn(q, cosine, sine).astype(BF16) * BF16(HD**-0.5)
+            k_ref[pair, rows, :] = turn(k, cosine, sine).astype(BF16)
+            v_ref[pair, rows, :] = v.astype(BF16)
+
+        odd = []
+        for s in range(2):
+            both = mm(a, spread_ref[s, :, 0 : 3 * LANES])
+            put(s, *(both[:, j * LANES : (j + 1) * LANES] for j in range(3)))
+            both = mm(a, spread_ref[s, :, 4 * LANES : 6 * LANES])
+            odd.append((both[:, :LANES], both[:, LANES:]))
+        put(
+            2,
+            jnp.where(head, odd[0][0], swap_halves(odd[1][0])),
+            jnp.where(head, swap_halves(odd[0][0]), odd[1][0]),
+            jnp.where(head, odd[0][1], swap_halves(odd[1][1])),
+        )
+        return carry
+
+    lax.fori_loop(0, blocks, project, 0)
+
+    def o_copy(p):
+        lanes = pl.ds(pl.multiple_of(own + p * LANES, LANES), LANES)
+        return remote(
+            o_ref.at[:, lanes], o_ref.at[:, lanes], core_send.at[p], core_recv.at[p], partner
+        )
+
+    def attend(p, carry):
+        lanes = pl.ds(pl.multiple_of(own + p * LANES, LANES), LANES)
         for i in range(blocks):
             rows = pl.ds(i * BLK, BLK)
             seen = pl.ds(0, (i + 1) * BLK)
-            q, k, v = q_ref[rows, lanes], k_ref[seen, lanes], v_ref[seen, lanes]
+            q, k, v = q_ref[p, rows, :], k_ref[p, seen, :], v_ref[p, seen, :]
             halves = []
             for side in range(2):
-                mask = head if side == 0 else jnp.logical_not(head)
-                s = mm_nt(jnp.where(mask, q, jnp.zeros_like(q)), k)
+                chosen = head if side == 0 else jnp.logical_not(head)
+                s = mm_nt(jnp.where(chosen, q, jnp.zeros_like(q)), k)
                 high = jnp.max(s, axis=-1, keepdims=True)
                 e = jnp.exp(s - high)
                 total = jnp.sum(e, axis=-1, keepdims=True)
                 halves.append(mm((e / total).astype(BF16), v))
                 log_total = jnp.broadcast_to(high + jnp.log(total), (BLK, LANES))
-                lse_ref[2 * p + side : 2 * p + side + 1, rows] = jnp.transpose(log_total)[0:1, :]
+                lse_ref[2 * p + side, :, rows] = jnp.transpose(log_total)[0:8, :]
             o_ref[rows, lanes] = jnp.where(head, halves[0], halves[1]).astype(BF16)
-
-
-def pick(hot, values):
-    return jnp.sum(jnp.where(hot, values, 0.0), axis=-1, keepdims=True)
-
-
-def lane_ids(rows):
-    return lax.broadcasted_iota(jnp.int32, (rows, LANES), 1)
-
-
-def column(value, lane, rows):
-    return jnp.where(lane_ids(rows) == lane, value, 0.0)
-
-
-def soft_pair(first, second):
-    high = jnp.maximum(first, second)
-    e0, e1 = jnp.exp(first - high), jnp.exp(second - high)
-    return e0 / (e0 + e1), e1 / (e0 + e1)
-
-
-def middle_kernel(
-    experts,
-    half,
-    padded,
-    x_ref,
-    o_ref,
-    wo_ref,
-    small_ref,
-    gain_ref,
-    prev_ref,
-    routes_ref,
-    post_ref,
-    h_ref,
-    ub_ref,
-    stat_ref,
-    slot_ref,
-    gate_ref,
-    pieces_ref,
-):
-    rows_all = x_ref.shape[0]
-    for i in range(rows_all // BLK):
-        rows = pl.ds(i * BLK, BLK)
-        z = mm_nt(o_ref[0, rows, :], wo_ref[0]) + mm_nt(o_ref[1, rows, :], wo_ref[1])
+        o_copy(p).start()
+        return carry
+
+    lax.fori_loop(0, pairs, attend, 0)
+    loads[3].wait()
+    wo_copy.wait()
+    for p in range(pairs):
+        o_copy(p).wait()
+
+    gain_moe = extra_ref[columns + 5 : columns + 6, :]
+
+    def middle(i, carry):
+        rows = pl.ds(pl.multiple_of(i * BLK, BLK), BLK)
+        z = mm_nt(o_ref[rows, :], wo_ref[...])
         h = x_ref[rows, :].astype(F32) + z
         r = lax.rsqrt(jnp.mean(h * h, axis=-1, keepdims=True) + EPSILON)
-        ub = (h * r * gain_ref[...]).astype(BF16)
+        ub = (h * r * gain_moe).astype(BF16)
         h_ref[rows, :] = h
         ub_ref[rows, :] = ub
         scores = mm(ub, small_ref[...])
-        logits = scores + prev_ref[rows, :]
-        ids = lane_ids(BLK)
-        hot0 = ids == routes_ref[rows, 0:1]
-        hot1 = ids == routes_ref[rows, 1:2]
-        g0, g1 = soft_pair(pick(hot0, logits), pick(hot1, logits))
-        base = experts + 4
-        c = [pick(ids == base + j, scores) for j in range(4)]
-        a00, a01 = soft_pair(c[0], c[1])
-        a10, a11 = soft_pair(c[2], c[3])
-        stats = [g0, g1, a00, a01, a10, a11, r]
-        table = column(stats[0], 0, BLK)
-        for j in range(1, len(stats)):
-            table = table + column(stats[j], j, BLK)
+        lane = lane_ids(BLK)
+        e0, e1 = routes_ref[rows, 0:1], routes_ref[rows, 1:2]
+        hot0, hot1 = lane == e0, lane == e1
+        prev = prev_ref[rows, :]
+        few = lax.broadcasted_iota(jnp.int32, (BLK, columns), 1)
+        g0, g1 = soft_pair(
+            pick(hot0, scores) + pick(few == e0, prev), pick(hot1, scores) + pick(few == e1, prev)
+        )
+        mix = [pick(lane == columns + j, scores) for j in range(4)]
+        a00, a01 = soft_pair(mix[0], mix[1])
+        a10, a11 = soft_pair(mix[2], mix[3])
+        table = jnp.zeros((BLK, LANES), F32)
+        for j, value in enumerate([g0, g1, a00, a01, a10, a11, r]):
+            table = jnp.where(lane == j, value, table)
         stat_ref[rows, :] = table
         gates = jnp.where(hot0, g0, 0.0) + jnp.where(hot1, g1, 0.0)
-        gates = jnp.transpose(gates)
-        for piece in range(3):
-            part = gates.astype(BF16)
-            pieces_ref[piece, :, rows] = part
-            gates = gates - part.astype(F32)
-    base = lax.rem(lax.axis_index("tensor"), 2) * half
-
-    def step(e, carry):
-        hot = slot_hot(half, padded, base, post_ref[pl.ds(e, 1), :])
+        gates_ref[:, rows] = jnp.transpose(gates)
+        return carry
+
+    lax.fori_loop(0, blocks, middle, 0)
+    piece = lax.broadcasted_iota(jnp.int32, (8, rows_all), 0)
+
+    def slot_step(i, carry):
+        j = lax.rem(i + 1, n)
+        e = lax.rem(d + j, n)
+        hot = slot_hot(half, padded, base, place_ref[pl.ds(e, 1), :])
         slot_ref[e] = mm(hot, ub_ref[...]).astype(BF16)
-        total = jnp.zeros((8, padded), F32)
-        for piece in range(3):
-            group = pl.ds(pl.multiple_of(lax.div(e, 16) * 16, 16), 16)
-            chosen = lax.broadcasted_iota(jnp.int32, (16, rows_all), 0) == lax.rem(e, 16)
-            line = jnp.where(chosen, pieces_ref[piece, group, :].astype(F32), 0.0)
-            line = jnp.broadcast_to(jnp.sum(line, axis=0, keepdims=True), (8, rows_all))
-            total = total + mm_nt(line.astype(BF16), hot)
-        gate_ref[e] = total
+        gate = gates_ref[pl.ds(e, 1), :]
+        high = gate.astype(BF16).astype(F32)
+        mid = (gate - high).astype(BF16).astype(F32)
+        low = gate - high - mid
+        lines = jnp.where(piece == 0, high, jnp.where(piece == 1, mid, low))
+        lines = jnp.where(piece < 3, lines, 0.0).astype(BF16)
+        gate = jnp.sum(mm_nt(lines, hot), axis=0, keepdims=True)
+        gate_ref[e] = jnp.broadcast_to(gate, (8, padded))
+
+        @pl.when(i < n - 1)
+        def _():
+            slot_copy(j).start()
+            gate_copy(j).start()
+
         return carry
 
-    lax.fori_loop(0, experts, step, 0)
+    lax.fori_loop(0, n, slot_step, 0)
+    stays[1].start()
+    stays[2].start()
+    weight_copies[0].wait_recv()
+    weight_copies[1].wait_recv()
+    weight_copies[4].start()
+    weight_copies[5].start()
+
+    def finish(j, carry):
+        for copy in (dy_copy(j), slot_copy(j), gate_copy(j)):
+            copy.wait()
+        return carry
+
+    lax.fori_loop(1, n, finish, 0)
+    for copy in stays:
+        copy.wait()
+    for copy in pack_copies + weight_copies[0:2]:
+        copy.wait_send()
+    for copy in weight_copies[2:6]:
+        copy.wait()
 
 
 def expert_kernel(
@@ -664,8 +832,8 @@
     dk_acc,
     dv_acc,
 ):
-    width = q_ref.shape[1]
-    pairs = width // LANES
+    pairs = q_ref.shape[0]
+    width = pairs * LANES
     blocks = LEN // BLK
     head = lax.broadcasted_iota(jnp.int32, (BLK, LANES), 1) < HD
     for p in range(pairs):
@@ -675,8 +843,8 @@
         for i in range(blocks):
             rows = pl.ds(i * BLK, BLK)
             seen = pl.ds(0, (i + 1) * BLK)
-            q, do = q_ref[rows, lanes], do_ref[rows, lanes]
-            k, v = k_ref[seen, lanes], v_ref[seen, lanes]
+            q, do = q_ref[p, rows, :], do_ref[rows, lanes]
+            k, v = k_ref[p, seen, :], v_ref[p, seen, :]
             zero = jnp.zeros_like(q)
             parts = []
             dk = dk_acc[seen, :]
@@ -684,7 +852,7 @@
             for side in range(2):
                 mask = head if side == 0 else jnp.logical_not(head)
                 qm, dom = jnp.where(mask, q, zero), jnp.where(mask, do, zero)
-                log_total = lse_ref[2 * p + side : 2 * p + side + 1, rows]
+                log_total = lse_ref[2 * p + side, 0:1, rows]
                 prob = jnp.exp(mm_nt(k, qm) - log_total)
                 grad_prob = mm_nt(v, dom)
                 total = jnp.sum(prob * grad_prob, axis=0, keepdims=True)
@@ -764,11 +932,16 @@
         return lax.dynamic_index_in_dim(value, m, 0, keepdims=False)
 
     x, dy, choose = mine(tokens), mine(cotangent), mine(routes)
-    prev = jnp.pad(mine(prev_logits), ((0, 0), (0, LANES - columns)))
     cosine, sine = (jnp.asarray(v) for v in rope_constants())
-
-    small = jnp.concatenate(
-        [
+    pairs = local // LANES
+
+    wo_rows = w_out.T
+    packed = jnp.concatenate(
+        [w_qkv[i, :, :LANES] for i in range(3)]
+        + [wo_rows[:, :LANES]]
+        + [w_qkv[i, :, LANES:] for i in range(3)]
+        + [
+            wo_rows[:, LANES:],
             w_router,
             w_const,
             norm_attn[:, None],
@@ -778,78 +951,118 @@
         ],
         axis=1,
     )
-    packed = jnp.concatenate([w_qkv[0], w_qkv[1], w_qkv[2], w_out.T, small], axis=1)
-    spread = gather_weights(0, n, packed).reshape(2, n * part, packed.shape[1])
-    w_heads = jnp.concatenate(
-        [spread[j, :, i * share : (i + 1) * share] for i in range(3) for j in range(2)], axis=1
-    )
-    wo_own = jnp.concatenate(
-        [spread[j, :, 3 * share : 4 * share] for j in range(2)], axis=1
-    )
-    table = spread[0, :, 4 * share :]
-    extra = table[:, columns + 4 : columns + 8].astype(F32).T
-    gain_attn, gain_moe, vectors = extra[0:1], extra[1:2], extra[2:4]
-    keep = jnp.arange(LANES) < columns + 4
-    small_all = jnp.where(keep[None, :], table, jnp.zeros_like(table))
-    wo_all = core_share(1, wo_own)[0]
-
-    in_x, down_x = across_chips(w_in), across_chips(w_down)
-    in_c, down_c = across_cores(w_in), across_cores(w_down)
-    in_d, down_d = across_cores(in_x), across_cores(down_x)
-
-    pos, post, dy_slots = compute_call(
-        functools.partial(route_kernel, experts, half, padded),
-        [
-            struct((rows, LANES), F32),
-            struct((LANES, rows), F32),
-            struct((experts, padded, width), BF16),
-        ],
-        choose,
-        choose.T,
-        dy,
-        flops=2 * experts * padded * rows * width,
-    )
-    dy_arrived = lax.all_to_all(dy_slots, "dp", split_axis=0, concat_axis=0, tiled=True)
-
-    a, q, k, v, o, lse = compute_call(
-        attention_kernel,
-        [
-            struct((rows, width), BF16),
-            struct((rows, local), BF16),
-            struct((rows, local), BF16),
-            struct((rows, local), BF16),
-            struct((rows, local), BF16),
-            struct((8, rows), F32),
-        ],
-        x,
-        gain_attn,
-        w_heads,
-        cosine,
-        sine,
-        flops=2 * rows * width * 3 * local + 8 * rows * rows * local,
-    )
-    o_all = core_share(2, o)[0]
-    h, ub, stats, slots, gate_slots = compute_call(
-        functools.partial(middle_kernel, experts, half, padded),
-        [
-            struct((rows, width), F32),
-            struct((rows, width), BF16),
-            struct((rows, LANES), F32),
-            struct((experts, padded, width), BF16),
-            struct((experts, 8, padded), F32),
-        ],
-        x,
+    gathered = part % 16 != 0
+    if gathered:
+        packed = lax.all_gather(packed, "dp", axis=0, tiled=True)
+        other = across_chips(packed)
+        packed = jnp.where(m == 0, jnp.stack([packed, other]), jnp.stack([other, packed]))
+    spread_width = packed.shape[-1]
+    front_outs = [
+        struct((rows, width), BF16),
+        struct((pairs, rows, LANES), BF16),
+        struct((pairs, rows, LANES), BF16),
+        struct((pairs, rows, LANES), BF16),
+        struct((rows, width), BF16),
+        struct((8, 8, rows), F32),
+        struct((rows, width), F32),
+        struct((rows, width), BF16),
+        struct((rows, LANES), F32),
+        struct((rows, LANES), F32),
+        struct((width, width), BF16),
+        struct((width, LANES), BF16),
+        struct((LANES, width), F32),
+        struct((2, width, spread_width), BF16),
+    ]
+    landing = [
+        struct((n, padded, width), BF16),
+        struct((n, 8, padded), F32),
+        struct((n, padded, width), BF16),
+    ] + [struct(w_in.shape, BF16)] * 3 + [struct(w_down.shape, BF16)] * 3
+    dma = pltpu.SemaphoreType.DMA
+    (
+        a,
+        q,
+        k,
+        v,
         o_all,
+        lse,
+        h,
+        ub,
+        stats,
+        pos,
         wo_all,
         small_all,
-        gain_moe,
-        prev,
-        choose,
-        post,
-        flops=4 * rows * width * width + 2 * experts * padded * rows * width,
-        scratch=[pltpu.VMEM((3, LANES, rows), BF16)],
-    )
-    arrived, gate_arrived = dispatch(3, n, slots, gate_slots)
+        extra,
+        spread,
+        arrived,
+        gate_arrived,
+        dy_arrived,
+        in_c,
+        in_x,
+        in_d,
+        down_c,
+        down_x,
+        down_d,
+    ) = pl.pallas_call(
+        functools.partial(front_kernel, n, half, padded, gathered),
+        out_shape=front_outs + landing,
+        in_specs=[aspec()] * 4 + [vspec()] * 3 + [aspec()] * 2,
+        out_specs=[vspec()] * len(front_outs) + [aspec()] * len(landing),
+        scratch_shapes=[
+            pltpu.VMEM((rows, width), BF16),
+            pltpu.VMEM((rows, width), BF16),
+            pltpu.VMEM((rows, columns), F32),
+            pltpu.VMEM((rows, 2), jnp.int32),
+            pltpu.VMEM((LANES, rows), F32),
+            pltpu.VMEM((LANES, rows), F32),
+            pltpu.VMEM((n, padded, width), BF16),
+            pltpu.VMEM((n, 8, padded), F32),
+            pltpu.VMEM((n, padded, width), BF16),
+            dma((4,)),
+            dma((2 * n,)),
+            dma((2 * n,)),
+            dma((n,)),
+            dma((n,)),
+            dma((n,)),
+            dma((n,)),
+            dma((n,)),
+            dma((n,)),
+            dma((3,)),
+            dma((pairs + 1,)),
+            dma((pairs + 1,)),
+            dma((6,)),
+            dma((6,)),
+        ],
+        compiler_params=pltpu.CompilerParams(
+            collective_id=0, has_side_effects=True, vmem_limit_bytes=VMEM_LIMIT
+        ),
+    )(tokens, cotangent, prev_logits, routes, packed, cosine, sine, w_in, w_down)
+    gain_attn = extra[columns + 4 : columns + 5]
+    gain_moe = extra[columns + 5 : columns + 6]
+    vectors = extra[columns + 6 : columns + 8]
+    o = lax.dynamic_slice_in_dim(o_all, c * local, local, axis=1)
+    wo_own = lax.dynamic_slice_in_dim(wo_all, c * local, local, axis=1)
+
+    def group(j, g):
+        return spread[j, :, g * LANES : (g + 1) * LANES]
+
+    w_heads = jnp.concatenate(
+        [
+            group(0, 0),
+            group(1, 0),
+            group(0, 4)[:, :HD],
+            group(1, 4)[:, :HD],
+            group(0, 1),
+            group(1, 1),
+            group(0, 4)[:, HD:],
+            group(1, 4)[:, HD:],
+            group(0, 2),
+            group(1, 2),
+            group(0, 5)[:, :HD],
+            group(1, 5)[:, :HD],
+        ],
+        axis=1,
+    )
 
     hidden_width = w_in.shape[3]
     slots_all = experts * padded
@@ -1004,10 +1217,10 @@
         [
             jnp.concatenate(
                 [
-                    grad_heads[:, (2 * i + j) * share : (2 * i + j + 1) * share]
-                    for i in range(3)
-                ]
-                + [grad_wo[:, j * share : (j + 1) * share]],
+                    piece[:, i * local + start : i * local + start + size]
+                    for piece, i in [(grad_heads, 0), (grad_heads, 1), (grad_heads, 2), (grad_wo, 0)]
+                    for start, size in [(j * LANES, LANES), (2 * LANES + j * HD, HD)]
+                ],
                 axis=1,
             )
             for j in range(2)

time: 739 us -> 669 us (0.905)
  Pallas kernels: 659 us -> 591 us
  local copies, waits for them, and re-layouts: 35.3 us -> 46.7 us
  starting transfers between devices: 13 us -> 4.06 us
    pallas_call x9 -> x5, Pallas kernels: 492 us -> 315 us  [comm_call(): pl.pallas_call(kernel, out_shape=outs, in_specs=[aspec()] * len(args), ou...]
    pallas_call x0 -> x1, Pallas kernels: none -> 146 us  [body(): pl.pallas_call(functools.partial(front_kernel, n, half, padded, gathered)...]
    pallas_call x6 -> x3, Pallas kernels: 120 us -> 80.8 us  [compute_call(): pl.pallas_call(kernel, out_shape=outs, in_specs=[vspec()] * len(args), ou...]
    unnamed x55 -> x40, local copies, waits for them, and re-layouts: 9.68 us -> 14.8 us
  transfers between devices with their start and end apart: 14 -> 7, of which waited for: 0 -> 0; matrix products, arithmetic and copies ran while one was open for 6% -> 7% of each run, Pallas kernels for 84% -> 60%
where the time goes in v2:
time: 669 us; the launch traced here: 659 us
  Pallas kernels  591 us (88%)
  local copies, waits for them, and re-layouts  46.7 us (7%)
  other arithmetic  16.3 us (2%)
    pallas_call x5, Pallas kernels, comm_call(): pl.pallas_call(kernel, out_shape=outs, in_specs=[aspec()] * len(args), ou...  315 us
    pallas_call x1, Pallas kernels, body(): pl.pallas_call(functools.partial(front_kernel, n, half, padded, gathered)...  146 us
    pallas_call x3, Pallas kernels, compute_call(): pl.pallas_call(kernel, out_shape=outs, in_specs=[vspec()] * len(args), ou...  80.8 us
    pallas_call x1, Pallas kernels, body(): pl.pallas_call(functools.partial(expert_kernel, n, padded), grid=(4 * per...  48.7 us
    unnamed x40, local copies, waits for them, and re-layouts  14.8 us
  transfers between devices with their start and end apart: 7, of which 0 were waited for; matrix products, arithmetic and copies ran while one was open for 7% of the time, Pallas kernels for 60%

profile of v2, /device:TPU:26, one launch (start us, length us, event | category | flops | bytes accessed | tf_op | source)
XLA Modules:
  0.0 659.4 jit_solution(13290782006775132439)
XLA Ops:
  7.1 2.2 copy.94.prev_all_ref
  9.3 1.3 copy.95.routes_all_ref
  11.5 146.3 %shard_map.238 = (bf16[1024,768]{1,0:T(8,128)(2,1)}, bf16[3,1024,128]{2,1,0:T(8,128)(2,1)}, bf16[3,1024,128]{2,1,0:T(8,128)(2,1)}, bf16[3,1024,128]{2,1,0:T(8,12...) custom-call(bf16[2,1024,768]{2,1,0:T(8,128)(2,1)} %tokens_ref.1, ...), custom_call_target="tpu_custom_call" | custom-call | tf_op jit(solution)/shard_map/pallas_call | solution.py:1006
  157.8 48.7 %shard_map.239 = (bf16[8,128,768]{2,1,0:T(8,128)(2,1)}, bf16[8,128,768]{2,1,0:T(8,128)(2,1)}, f32[8,8,128]{2,1,0:T(8,128)}, bf16[1,2,768,512]{3,2,1,0:T(8,128)(2...) custom-call(bf16[1024,768]{1,0:T(8,128)(2,1)} %bitcast.78, ...), custom_call_target="tpu_custom_call" | custom-call | flops 28991029248 | bytes 30000000 | tf_op jit(solution)/shard_map/pallas_call | solution.py:1095
  207.6 3.3 dynamic-slice_bitcast_fusion
  210.9 1.4 fusion.6
  212.3 1.3 slice.176.vec_ref
  213.6 2.1 constant_dynamic-slice_fusion.1.o_ref
  217.7 78.1 %shard_map.240 = (bf16[2,8,128,768]{3,2,1,0:T(8,128)(2,1)}, bf16[2,8,128,768]{3,2,1,0:T(8,128)(2,1)}, f32[2,8,8,128]{3,2,1,0:T(8,128)}) custom-call(bf16[8,128,768]{2,1,0:T(8,128)(2,1)} %get-tuple-element.75.refs_0_, bf16[8,128,768]{2,1,0:T(8,128)(2,1)} %get-tuple-element.76.refs_1_, f32[8,8,128]{2,1,0:T(8,128)} %get-tuple-element.77.refs_2_), custom_call_target="tpu_custom_call" | custom-call | tf_op jit(solution)/shard_map/pallas_call | solution.py:82
  295.7 48.8 %shard_map.241 = (bf16[1024,768]{1,0:T(8,128)(2,1)}, f32[1024,128]{1,0:T(8,128)}, f32[1024,768]{1,0:T(8,128)}, bf16[1024,384]{1,0:T(8,128)(2,1)}, bf16[768,384]{...) custom-call(f32[1024,768]{1,0:T(8,128)} %get-tuple-element.62.h_ref, ...), custom_call_target="tpu_custom_call" | custom-call | flops 6442450944 | bytes 22692864 | tf_op jit(solution)/shard_map/pallas_call | solution.py:50
  344.6 1.9 slice_bitcast_fusion.22
  346.5 1.4 collective-permute-start
  348.5 2.3 concatenate.17.w_ref
  350.8 25.6 %shard_map.243 = (bf16[1024,768]{1,0:T(8,128)(2,1)}, bf16[768,1152]{1,0:T(8,128)(2,1)}) custom-call(bf16[3,1024,128]{2,1,0:T(8,128)(2,1)} %get-tuple-element.87.q_ref, bf16[3,1024,128]{2,1,0:T(8,128)(2,1)} %get-tuple-element.88.k_ref, bf16[3,1024,128]{2,1,0:T(8,128)(2,1)} %get-tuple-element.89.v_ref, bf16[1024,384]{1,0:T(8,128)(2,1)} %get-tuple-element.90.do_ref, ...), custom_call_target="tpu_custom_call" | custom-call | flops 11676942336 | bytes 11141120 | tf_op jit(solution)/shard_map/pallas_call | solution.py:50
  376.4 48.9 %shard_map.244.da_ref = bf16[2,1024,768]{2,1,0:T(8,128)(2,1)} custom-call(bf16[1024,768]{1,0:T(8,128)(2,1)} %get-tuple-element.94.refs_0_), custom_call_target="tpu_custom_call" | custom-call | tf_op jit(solution)/shard_map/pallas_call | solution.py:82
  425.3 6.3 shard_map.245
  436.4 2.3 concatenate.18
  438.7 2.6 concatenate.19
  441.4 1.6 pad_maximum_fusion.refs_0_
  444.3 75.9 %shard_map.247 = (bf16[2,8,96,768]{3,2,1,0:T(8,128)(2,1)}, f32[2,8,96,128]{3,2,1,0:T(8,128)}) custom-call(bf16[2,8,96,768]{3,2,1,0:T(8,128)(2,1)} %pad_maximum_fusion.refs_0_, f32[2,8,96,128]{3,2,1,0:T(8,128)} %broadcast_in_dim.20.refs_1_), custom_call_target="tpu_custom_call" | custom-call | tf_op jit(solution)/shard_map/pallas_call | solution.py:82
  520.2 1.2 reduce_sum.18
  521.4 3.1 add_convert_fusion
  525.7 1.3 add_convert_fusion.1
  527.0 1.3 collective-permute-start.6
  533.0 63.4 %shard_map.246 = bf16[2,1024,768]{2,1,0:T(8,128)(2,1)} custom-call(bf16[1024,768]{1,0:T(8,128)(2,1)} %get-tuple-element.95.in_ref), custom_call_target="tpu_custom_call" | custom-call | tf_op jit(solution)/shard_map/pallas_call | solution.py:82
  596.4 49.2 %shard_map.242 = bf16[2,1024,768]{2,1,0:T(8,128)(2,1)} custom-call(bf16[1024,768]{1,0:T(8,128)(2,1)} %get-tuple-element.85.in_ref), custom_call_target="tpu_custom_call" | custom-call | tf_op jit(solution)/shard_map/pallas_call | solution.py:82
  645.6 1.2 copy.98
  647.6 3.1 convert_add_fusion.1
  650.8 3.8 convert_add_fusion
  654.6 1.7 copy.108
  656.2 1.4 copy-done
  657.6 1.7 copy.109
  (76 shorter events, 23.4 us)
Async XLA Ops:
  0.6 8.6 %copy-start.13 = (s32[2,1024,2]{1,2,0:T(2,128)S(1)}, s32[2,1024,2]{1,2,0:T(2,128)}, u32[]{:S(2)}) copy-start(s32[2,1024,2]{1,2,0:T(2,128)} %param.18) | copy-start | bytes 49156
  157.8 49.8 %copy-start.2 = (bf16[2,1024,768]{2,1,0:T(8,128)(2,1)S(1)}, bf16[2,1024,768]{2,1,0:T(8,128)(2,1)}, u32[]{:S(2)}) copy-start(bf16[2,1024,768]{2,1,0:T(8,128)(2,1)} %tokens_ref.1) | copy-start | bytes 9437188
  206.5 318.6 %collective-permute-start.5 = (bf16[1,512,768]{2,1,0:T(8,128)(2,1)}, bf16[1,512,768]{2,1,0:T(8,128)(2,1)}, u32[]{:S(2)}, u32[]{:S(2)}) collective-permute-start(bf16[1,512,768]{2,1,0:T(8,128)(2,1)} %get-tuple-element.111), channel_id=1, source_target_pairs={{0,1},{1,0},{2,3},{3,2},{4,5},{5,4},{6,7},{7,6},{8,9},{9,8},{10,11... | collective-permute-start | bytes 2359304 | tf_op jit(solution)/shard_map/ppermute | solution.py:900
  206.6 441.0 %collective-permute-start.4 = (bf16[1,512,768]{2,1,0:T(8,128)(2,1)}, bf16[1,512,768]{2,1,0:T(8,128)(2,1)}, u32[]{:S(2)}, u32[]{:S(2)}) collective-permute-start(bf16[1,512,768]{2,1,0:T(8,128)(2,1)} %get-tuple-element.109), channel_id=1, source_target_pairs={{0,1},{1,0},{2,3},{3,2},{4,5},{5,4},{6,7},{7,6},{8,9},{9,8},{10,11... | collective-permute-start | bytes 2359304 | tf_op jit(solution)/shard_map/ppermute | solution.py:900
  207.1 314.3 %collective-permute-start.2 = (bf16[1,2,768,512]{3,2,1,0:T(8,128)(2,1)}, bf16[1,2,768,512]{3,2,1,0:T(8,128)(2,1)}, u32[]{:S(2)}, u32[]{:S(2)}) collective-permute-start(bf16[1,2,768,512]{3,2,1,0:T(8,128)(2,1)} %get-tuple-element.107), channel_id=1, source_target_pairs={{0,1},{1,0},{2,3},{3,2},{4,5},{5,4},{6,7},{7,6},{8,9},{9,8},{10,11... | collective-permute-start | bytes 4718600 | tf_op jit(solution)/shard_map/ppermute | solution.py:900
  207.2 443.6 %collective-permute-start.1 = (bf16[1,2,768,512]{3,2,1,0:T(8,128)(2,1)}, bf16[1,2,768,512]{3,2,1,0:T(8,128)(2,1)}, u32[]{:S(2)}, u32[]{:S(2)}) collective-permute-start(bf16[1,2,768,512]{3,2,1,0:T(8,128)(2,1)} %get-tuple-element.105), channel_id=1, source_target_pairs={{0,1},{1,0},{2,3},{3,2},{4,5},{5,4},{6,7},{7,6},{8,9},{9,8},{10,11... | collective-permute-start | bytes 4718600 | tf_op jit(solution)/shard_map/ppermute | solution.py:900
  210.9 4.9 copy-start.12
  295.7 52.2 %copy-start.7 = (bf16[2,768,896]{2,1,0:T(8,128)(2,1)S(1)}, bf16[2,768,896]{2,1,0:T(8,128)(2,1)}, u32[]{:S(2)}) copy-start(bf16[2,768,896]{2,1,0:T(8,128)(2,1)} %get-tuple-element.93) | copy-start | bytes 8257540
  346.5 299.1 %collective-permute-start = (f32[1024,12]{1,0:T(8,128)}, f32[1024,12]{1,0:T(8,128)}, u32[]{:S(2)}, u32[]{:S(2)}) collective-permute-start(f32[1024,12]{1,0:T(8,128)} %get-tuple-element.201), channel_id=1, source_target_pairs={{0,2},{2,0},{1,3},{3,1},{4,6},{6,4},{5,7},{7,5},{8,10},{10,8},{9,1... | collective-permute-start | bytes 147464 | tf_op jit(solution)/shard_map/ppermute | solution.py:896
  425.3 7.3 %copy-start.8 = (bf16[768,384]{1,0:T(8,128)(2,1)S(1)}, bf16[768,384]{1,0:T(8,128)(2,1)}, u32[]{:S(2)}) copy-start(bf16[768,384]{1,0:T(8,128)(2,1)} %get-tuple-element.98) | copy-start | bytes 1769476
  431.6 2.7 copy-start.3
  441.4 1.6 copy-start.10
  441.4 1.6 copy-start.11
  444.3 77.1 %copy-start.5 = (bf16[1,2,768,512]{3,2,1,0:T(8,128)(2,1)S(1)}, bf16[1,2,768,512]{3,2,1,0:T(8,128)(2,1)}, u32[]{:S(2)}) copy-start(bf16[1,2,768,512]{3,2,1,0:T(8,128)(2,1)} %get-tuple-element.106) | copy-start | bytes 4718596
  521.4 3.4 copy-start.4
  524.6 1.1 copy-start.9
  524.6 126.2 %collective-permute-start.3 = (bf16[1,2,768,512]{3,2,1,0:T(8,128)(2,1)}, bf16[1,2,768,512]{3,2,1,0:T(8,128)(2,1)S(1)}, u32[]{:S(2)}, u32[]{:S(2)}) collective-permute-start(bf16[1,2,768,512]{3,2,1,0:T(8,128)(2,1)} %add_convert_fusion), channel_id=1, source_target_pairs={{0,2},{2,0},{1,3},{3,1},{4,6},{6,4},{5,7},{7,5},{8,10},{10,8},{9,1... | collective-permute-start | bytes 4718600 | tf_op jit(solution)/shard_map/ppermute | solution.py:896
  527.0 120.6 %collective-permute-start.6 = (bf16[1,512,768]{2,1,0:T(8,128)(2,1)S(1)}, bf16[1,512,768]{2,1,0:T(8,128)(2,1)}, u32[]{:S(2)}, u32[]{:S(2)}) collective-permute-start(bf16[1,512,768]{2,1,0:T(8,128)(2,1)S(1)} %add_convert_fusion.1), channel_id=1, source_target_pairs={{0,2},{2,0},{1,3},{3,1},{4,6},{6,4},{5,7},{7,5},{8,10},{10,8},{9,1... | collective-permute-start | bytes 2359304 | tf_op jit(solution)/shard_map/ppermute | solution.py:896
  647.6 3.1 copy-start.6
  650.7 3.8 copy-start.1
  654.6 3.0 copy-start

commit v3 on v2

--- a/solution.py
+++ b/solution.py
@@ -16,7 +16,7 @@
 F32 = jnp.float32
 BF16 = jnp.bfloat16
 MESH = pl.DeviceIdType.MESH
-VMEM_LIMIT = 56 * 1024 * 1024
+VMEM_LIMIT = 60 * 1024 * 1024
 
 
 def mm(a, b):
@@ -41,23 +41,6 @@
 
 def struct(shape, dtype):
     return jax.ShapeDtypeStruct(shape, dtype)
-
-
-def compute_call(kernel, outs, *args, flops=1e9, scratch=()):
-    nbytes = sum(int(np.prod(a.shape)) * a.dtype.itemsize for a in args) + sum(
-        int(np.prod(o.shape)) * o.dtype.itemsize for o in outs
-    )
-    return pl.pallas_call(
-        kernel,
-        out_shape=outs,
-        in_specs=[vspec()] * len(args),
-        out_specs=[vspec()] * len(outs),
-        scratch_shapes=list(scratch),
-        compiler_params=pltpu.CompilerParams(vmem_limit_bytes=VMEM_LIMIT),
-        cost_estimate=pl.CostEstimate(
-            flops=int(flops), bytes_accessed=nbytes, transcendentals=0
-        ),
-    )(*args)
 
 
 def greet(peers):
@@ -78,39 +61,6 @@
     )
 
 
-def comm_call(kernel, outs, sems, cid, *args):
-    return pl.pallas_call(
-        kernel,
-        out_shape=outs,
-        in_specs=[aspec()] * len(args),
-        out_specs=[aspec()] * len(outs),
-        scratch_shapes=[pltpu.SemaphoreType.DMA(s) for s in sems],
-        compiler_params=pltpu.CompilerParams(collective_id=cid, has_side_effects=True),
-    )(*args)
-
-
-def core_share(cid, *arrays):
-    count = len(arrays)
-
-    def kernel(*refs):
-        ins, outs, (send, recv, local) = refs[:count], refs[count : 2 * count], refs[2 * count :]
-        d, t = lax.axis_index("dp"), lax.axis_index("tensor")
-        c = lax.rem(t, 2)
-        peer = (d, t + 1 - 2 * c)
-        greet([peer])
-        copies = []
-        for i in range(count):
-            copies.append(remote(ins[i], outs[i].at[c], send.at[i], recv.at[i], peer))
-            copies.append(pltpu.make_async_copy(ins[i], outs[i].at[c], local.at[i]))
-        for copy in copies:
-            copy.start()
-        for copy in copies:
-            copy.wait()
-
-    outs = [struct((2,) + a.shape, a.dtype) for a in arrays]
-    return comm_call(kernel, outs, [(count,)] * 3, cid, *arrays)
-
-
 def plane_peers(n, d, t):
     return [(lax.rem(d + j, n), t) for j in range(1, n)]
 
@@ -118,118 +68,6 @@
 def all_peers(n, d, t):
     other = lax.rem(t + 2, 4)
     return plane_peers(n, d, t) + [(lax.rem(d + j, n), other) for j in range(n)]
-
-
-def spread_gradients(cid, n, *arrays):
-    count = len(arrays)
-
-    def kernel(*refs):
-        ins, outs, (send, recv, local) = refs[:count], refs[count : 2 * count], refs[2 * count :]
-        d, t = lax.axis_index("dp"), lax.axis_index("tensor")
-        m = lax.div(t, 2)
-        peers = all_peers(n, d, t)
-        greet(peers)
-        copies = []
-        for k in range(count):
-            copies.append(
-                pltpu.make_async_copy(ins[k].at[m, d], outs[k].at[m, d], local.at[k])
-            )
-            for i, (pd, pt) in enumerate(peers):
-                pm = lax.div(pt, 2)
-                copies.append(
-                    remote(
-                        ins[k].at[pm, pd],
-                        outs[k].at[m, d],
-                        send.at[k, i],
-                        recv.at[k, i],
-                        (pd, pt),
-                    )
-                )
-        for copy in copies:
-            copy.start()
-        for copy in copies:
-            copy.wait()
-
-    outs = [struct(a.shape, a.dtype) for a in arrays]
-    return comm_call(kernel, outs, [(count, 2 * n), (count, 2 * n), (count,)], cid, *arrays)
-
-
-def give_back(cid, n, *arrays):
-    count = len(arrays)
-
-    def kernel(*refs):
-        ins, outs = refs[:count], refs[count : 2 * count]
-        send, recv, local, csend, crecv = refs[2 * count :]
-        d, t = lax.axis_index("dp"), lax.axis_index("tensor")
-        c = lax.rem(t, 2)
-        partner = (d, t + 1 - 2 * c)
-        peers = plane_peers(n, d, t)
-        greet(peers + [partner])
-        arrivals = []
-        own = []
-        passed = []
-        for k in range(count):
-            own.append(pltpu.make_async_copy(ins[k].at[d], outs[k].at[c, d], local.at[k]))
-            passed.append(
-                remote(ins[k].at[d], outs[k].at[c, d], csend.at[k, 0], crecv.at[k, 0], partner)
-            )
-            for i, (pd, pt) in enumerate(peers):
-                arrivals.append(
-                    remote(
-                        ins[k].at[pd], outs[k].at[c, d], send.at[k, i], recv.at[k, i], (pd, pt)
-                    )
-                )
-        for copy in own + passed + arrivals:
-            copy.start()
-        for k in range(count):
-            for i in range(n - 1):
-                arrivals[k * (n - 1) + i].wait_recv()
-                source = lax.rem(d + n - 1 - i, n)
-                block = outs[k].at[c, source]
-                copy = remote(block, block, csend.at[k, i + 1], crecv.at[k, i + 1], partner)
-                copy.start()
-                passed.append(copy)
-        for copy in arrivals:
-            copy.wait_send()
-        for copy in own + passed:
-            copy.wait()
-
-    outs = [struct((2,) + a.shape, a.dtype) for a in arrays]
-    return comm_call(
-        kernel, outs, [(count, n), (count, n), (count,), (count, n), (count, n)], cid, *arrays
-    )
-
-
-def share_output(cid, full):
-    rows = full.shape[0]
-    half = rows // 2
-
-    def kernel(in_ref, out_ref, send, recv, local):
-        d, t = lax.axis_index("dp"), lax.axis_index("tensor")
-        m, c = lax.div(t, 2), lax.rem(t, 2)
-        across = (d, lax.rem(t + 2, 4))
-        partner = (d, t + 1 - 2 * c)
-        greet([across, partner])
-        mine = pltpu.make_async_copy(in_ref, out_ref.at[m], local.at[0])
-        mine.start()
-        first = remote(
-            in_ref.at[pl.ds(c * half, half)],
-            out_ref.at[m, pl.ds(c * half, half)],
-            send.at[0],
-            recv.at[0],
-            across,
-        )
-        first.start()
-        first.wait_recv()
-        block = out_ref.at[1 - m, pl.ds(c * half, half)]
-        second = remote(block, block, send.at[1], recv.at[1], partner)
-        second.start()
-        first.wait_send()
-        second.wait()
-        mine.wait()
-
-    outs = [struct((2,) + full.shape, full.dtype)]
-    return comm_call(kernel, outs, [(2,), (2,), (1,)], cid, full)[0]
 
 
 def slot_hot(half, padded, base, places):
@@ -698,162 +536,334 @@
             dx_ref[s] = dx_acc[rows, :].astype(BF16)
 
 
-def back_kernel(
-    experts,
+def rear_kernel(
+    n,
     half,
     padded,
+    gathered,
+    part,
+    gy_src_ref,
+    dx_src_ref,
+    dg_src_ref,
+    tokens_ref,
+    cotangent_ref,
+    routes_all_ref,
+    o_all_ref,
     h_ref,
     ub_ref,
     stat_ref,
+    pos_ref,
+    small_ref,
+    extra_ref,
+    wo_ref,
+    q_ref,
+    k_ref,
+    v_ref,
+    a_ref,
+    lse_ref,
+    spread_ref,
+    cos_ref,
+    sin_ref,
+    result_ref,
+    grad_x_ref,
+    logit_ref,
+    grads_ref,
+    lines_ref,
+    x_ref,
+    dy_ref,
     routes_ref,
-    pos_ref,
-    dy_ref,
+    o_ref,
+    dx_ref,
     gy_ref,
-    dx_ref,
     dg_ref,
-    small_ref,
-    gain_ref,
-    vec_ref,
-    o_ref,
-    wo_ref,
-    result_ref,
-    prev_ref,
     dh_ref,
+    dzb_ref,
     do_ref,
-    grad_wo_ref,
-    grad_small_ref,
-    mixed_ref,
     low_ref,
-    dzb_ref,
     row_ref,
+    dp_ref,
+    dk_acc,
+    dv_acc,
+    wo_odd_ref,
+    pack_ref,
+    line_ref,
+    pack_in_ref,
+    line_in_ref,
+    cross_ref,
+    cross_in_ref,
+    cross_line_ref,
+    da_out_ref,
+    da_in_ref,
+    da_own_ref,
+    norm_ref,
+    norm_in_ref,
+    half_ref,
+    load,
+    dx_send,
+    dx_recv,
+    gy_send,
+    gy_recv,
+    dg_send,
+    dg_recv,
+    stay,
+    pass_send,
+    pass_recv,
+    grad_send,
+    grad_recv,
+    pair_send,
+    pair_recv,
+    out_send,
+    out_recv,
 ):
-    rows_all = h_ref.shape[0]
-    width = h_ref.shape[1]
+    rows_all, width = dy_ref.shape
+    blocks = rows_all // BLK
+    pairs = q_ref.shape[0]
+    local = pairs * LANES
+    columns = n + 4
+    slots = n * padded
+    d, t = lax.axis_index("dp"), lax.axis_index("tensor")
+    m, c = lax.div(t, 2), lax.rem(t, 2)
+    partner = (d, t + 1 - 2 * c)
+    across = (d, lax.rem(t + 2, 4))
+    rows_half = rows_all // 2
+    own = pl.multiple_of(c * local, LANES)
+    own_lanes = pl.ds(own, local)
+    place = pl.ds(pl.multiple_of(c * rows_half, BLK), rows_half)
+    loads = [
+        pltpu.make_async_copy(src, dst, load.at[i])
+        for i, (src, dst) in enumerate(
+            [
+                (routes_all_ref.at[m], routes_ref),
+                (cotangent_ref.at[m], dy_ref),
+                (tokens_ref.at[m, place], x_ref),
+                (o_all_ref.at[:, own_lanes], o_ref),
+            ]
+        )
+    ]
+    for copy in loads:
+        copy.start()
+    greet(plane_peers(n, d, t) + [partner, across])
+
+    kinds = [
+        (dx_src_ref, dx_ref, dx_send, dx_recv),
+        (dg_src_ref, dg_ref, dg_send, dg_recv),
+        (gy_src_ref, gy_ref, gy_send, gy_recv),
+    ]
+
+    def give(kind, j):
+        src, dst, send, recv = kinds[kind]
+        s = lax.rem(d + j, n)
+        return remote(src.at[s], dst.at[c, d], send.at[j], recv.at[j], (s, t))
+
+    def hand(kind, j):
+        dst = kinds[kind][1]
+        s = lax.rem(d + n - j, n)
+        block = dst.at[c, s]
+        return remote(block, block, pass_send.at[kind, j], pass_recv.at[kind, j], partner)
+
+    def keep(kind):
+        src, dst = kinds[kind][0:2]
+        return pltpu.make_async_copy(src.at[d], dst.at[c, d], stay.at[kind])
+
+    def begin(*chosen):
+        for kind in chosen:
+            keep(kind).start()
+
+        def step(j, carry):
+            for kind in chosen:
+                give(kind, j).start()
+            return carry
+
+        lax.fori_loop(1, n, step, 0)
+
+    def collect(*chosen):
+        for kind in chosen:
+            keep(kind).wait()
+            hand(kind, 0).start()
+
+        def step(j, carry):
+            for kind in chosen:
+                give(kind, j).wait_recv()
+                hand(kind, j).start()
+            return carry
+
+        lax.fori_loop(1, n, step, 0)
+
+    def settle(*chosen):
+        def step(j, carry):
+            for kind in chosen:
+                hand(kind, j).wait_recv()
+            return carry
+
+        lax.fori_loop(0, n, step, 0)
+
+    begin(0, 1)
     row_ref[...] = jnp.zeros_like(row_ref)
-    columns = experts + 4
-    for i in range(rows_all // BLK):
-        rows = pl.ds(i * BLK, BLK)
-        ids = lane_ids(BLK)
+    for copy in loads:
+        copy.wait()
+    collect(0, 1)
+    begin(2)
+    settle(0, 1)
+
+    gain_moe = extra_ref[columns + 5 : columns + 6, :]
+    vec0 = extra_ref[columns + 6 : columns + 7, :]
+    vec1 = extra_ref[columns + 7 : columns + 8, :]
+    group = max(1, min(n, (1024 if slots <= 1024 else 512) // padded))
+    span = group * padded
+
+    def combine(wheres, ref, lines=None):
+        total = jnp.zeros((BLK, width), F32)
+        entries = [jnp.zeros((BLK, 1), F32) for _ in wheres]
+        slot = lax.broadcasted_iota(jnp.int32, (BLK, span), 1)
+        for side in range(2):
+            for first in range(0, n, group):
+                start = side * slots + first * padded
+                hots = [slot == where - start for where in wheres]
+                hot = jnp.where(hots[0] | hots[1], 1.0, 0.0).astype(BF16)
+                block = ref[side, first : first + group].reshape(span, width)
+                total = total + mm(hot, block)
+                if lines is not None:
+                    line = jnp.concatenate(
+                        [lines[side, first + e, 0:1, :] for e in range(group)], axis=1
+                    )
+                    entries = [
+                        entry + jnp.sum(jnp.where(one, line, 0.0), axis=-1, keepdims=True)
+                        for entry, one in zip(entries, hots)
+                    ]
+        return total, entries
+
+    def facts(rows):
+        lane = lane_ids(BLK)
         stats = stat_ref[rows, :]
-        g0, g1, a00, a01, a10, a11, r = [stats[:, j : j + 1] for j in range(7)]
+        values = [stats[:, j : j + 1] for j in range(7)]
         e0, e1 = routes_ref[rows, 0:1], routes_ref[rows, 1:2]
-        hot0, hot1 = ids == e0, ids == e1
+        wheres = []
         places = pos_ref[rows, :]
-        sums = jnp.zeros((BLK, width), F32)
-        grads = jnp.zeros((BLK, width), F32)
-        gate_grads = jnp.zeros((BLK, LANES), F32)
-
-        def step(e, carry):
-            sums, grads, gate_grads = carry
-            place = pick(ids == e, places)
-            for side in range(2):
-                slot = lax.broadcasted_iota(jnp.int32, (BLK, padded), 1)
-                wanted = jnp.where(slot < half, slot + side * half, -2).astype(F32)
-                hot = wanted == place
-                low = hot.astype(F32).astype(BF16)
-                sums = sums + mm(low, gy_ref[side, e])
-                grads = grads + mm(low, dx_ref[side, e])
-                value = jnp.sum(
-                    jnp.where(hot, dg_ref[side, e, 0:1, :], 0.0), axis=-1, keepdims=True
-                )
-                gate_grads = gate_grads + jnp.where(ids == e, value, 0.0)
-            return sums, grads, gate_grads
-
-        sums, grads, gate_grads = lax.fori_loop(
-            0, experts, step, (sums, grads, gate_grads)
-        )
-        h = h_ref[rows, :]
-        n = h * r
-        u = n * gain_ref[...]
-        dy = dy_ref[rows, :].astype(F32)
-        vec0, vec1 = vec_ref[0:1, :], vec_ref[1:2, :]
+        for e in (e0, e1):
+            place = pick(lane == e, places).astype(jnp.int32)
+            side = (place >= half).astype(jnp.int32)
+            where = side * (slots - half) + e * padded + place
+            wheres.append(jnp.where(e < n, where, -1))
+        g0, g1 = values[0:2]
 
         def named(number):
             return jnp.where(e0 == number, g0, 0.0) + jnp.where(e1 == number, g1, 0.0)
 
-        copied, first, second = named(experts + 1), named(experts + 2), named(experts + 3)
-        on_u = copied + first * a00 + second * a10
-        result = h + (sums + on_u * u + (first * a01) * vec0 + (second * a11) * vec1)
-        result_ref[rows, :] = result.astype(BF16)
+        copied, first, second = named(n + 1), named(n + 2), named(n + 3)
+        on_u = copied + first * values[2] + second * values[4]
+        return values, e0, e1, wheres, first, second, on_u
+
+    def back(i, carry):
+        rows = pl.ds(pl.multiple_of(i * BLK, BLK), BLK)
+        values, e0, e1, wheres, first, second, on_u = facts(rows)
+        g0, g1, a00, a01, a10, a11, r = values
+        lane = lane_ids(BLK)
+        grads, (f0, f1) = combine(wheres, dx_ref, dg_ref)
+        h = h_ref[rows, :]
+        normed = h * r
+        u = normed * gain_moe
+        dy = dy_ref[rows, :].astype(F32)
         s_u = jnp.sum(dy * u, axis=-1, keepdims=True)
         s_0 = jnp.sum(dy * vec0, axis=-1, keepdims=True)
         s_1 = jnp.sum(dy * vec1, axis=-1, keepdims=True)
-        table = (
-            gate_grads
-            + jnp.where(ids == experts + 1, s_u, 0.0)
-            + jnp.where(ids == experts + 2, a00 * s_u + a01 * s_0, 0.0)
-            + jnp.where(ids == experts + 3, a10 * s_u + a11 * s_1, 0.0)
-        )
-        dg0, dg1 = pick(hot0, table), pick(hot1, table)
+
+        def other(e):
+            value = jnp.where(e == n + 1, s_u, 0.0)
+            value = jnp.where(e == n + 2, a00 * s_u + a01 * s_0, value)
+            return jnp.where(e == n + 3, a10 * s_u + a11 * s_1, value)
+
+        dg0, dg1 = f0 + other(e0), f1 + other(e1)
         mean = g0 * dg0 + g1 * dg1
-        dl = jnp.where(hot0, g0 * (dg0 - mean), 0.0) + jnp.where(hot1, g1 * (dg1 - mean), 0.0)
-        prev_ref[rows, :] = dl
+        dl = jnp.where(lane == e0, g0 * (dg0 - mean), 0.0) + jnp.where(
+            lane == e1, g1 * (dg1 - mean), 0.0
+        )
+        turned = jnp.transpose(dl)
+        logit_ref[m, :, rows] = turned[0 : logit_ref.shape[1], :]
         d00, d01 = first * s_u, first * s_0
         d10, d11 = second * s_u, second * s_1
         m0 = a00 * d00 + a01 * d01
         m1 = a10 * d10 + a11 * d11
-        mixing = (
-            jnp.where(ids == columns, a00 * (d00 - m0), 0.0)
-            + jnp.where(ids == columns + 1, a01 * (d01 - m0), 0.0)
-            + jnp.where(ids == columns + 2, a10 * (d10 - m1), 0.0)
-            + jnp.where(ids == columns + 3, a11 * (d11 - m1), 0.0)
-        )
-        low = (dl + mixing).astype(BF16)
+        low = dl
+        for j, value in enumerate(
+            [a00 * (d00 - m0), a01 * (d01 - m0), a10 * (d10 - m1), a11 * (d11 - m1)]
+        ):
+            low = jnp.where(lane == columns + j, value, low)
+        low = low.astype(BF16)
         low_ref[rows, :] = low
         du = grads + mm_nt(low, small_ref[...]) + on_u * dy
-        row_ref[0:1, :] += jnp.sum(du * n, axis=0, keepdims=True)
+        row_ref[0:1, :] += jnp.sum(du * normed, axis=0, keepdims=True)
         row_ref[1:2, :] += jnp.sum((first * a01) * dy, axis=0, keepdims=True)
         row_ref[2:3, :] += jnp.sum((second * a11) * dy, axis=0, keepdims=True)
-        dn = du * gain_ref[...]
-        dh = dy + r * (dn - n * jnp.mean(dn * n, axis=-1, keepdims=True))
-        dh_ref[rows, :] = dh
+        dn = du * gain_moe
+        dh = dy + r * (dn - normed * jnp.mean(dn * normed, axis=-1, keepdims=True))
+
+        @pl.when(lax.div(i, blocks // 2) == c)
+        def _():
+            near = pl.multiple_of(i * BLK - c * rows_half, BLK)
+            dh_ref[pl.ds(near, BLK), :] = dh
+
         dzb = dh.astype(BF16)
         dzb_ref[rows, :] = dzb
-        do_ref[rows, :] = mm(dzb, wo_ref[...]).astype(BF16)
-    grad_wo_ref[...] = mm_tn(dzb_ref[...], o_ref[...]).astype(BF16)
-    lines = jnp.concatenate([row_ref[...], jnp.zeros((LANES - 8, width), F32)], axis=0)
-    grad_small_ref[...] = mm_tn(ub_ref[...], low_ref[...])
-    mixed_ref[...] = jnp.transpose(lines)
-
-
-def attention_back_kernel(
-    q_ref,
-    k_ref,
-    v_ref,
-    do_ref,
-    lse_ref,
-    a_ref,
-    w_ref,
-    cos_ref,
-    sin_ref,
-    da_ref,
-    grad_w_ref,
-    dp_ref,
-    dk_acc,
-    dv_acc,
-):
-    pairs = q_ref.shape[0]
-    width = pairs * LANES
-    blocks = LEN // BLK
-    head = lax.broadcasted_iota(jnp.int32, (BLK, LANES), 1) < HD
-    for p in range(pairs):
-        lanes = pl.ds(p * LANES, LANES)
+        do_ref[rows, :] = mm(dzb, wo_ref[:, own_lanes]).astype(BF16)
+        return carry
+
+    lax.fori_loop(0, blocks, back, 0)
+    logit_copy = remote(
+        logit_ref.at[m], logit_ref.at[m], pair_send.at[0], pair_recv.at[0], across
+    )
+    logit_copy.start()
+    collect(2)
+
+    grad_wo = mm_tn(dzb_ref[...], o_ref[...])
+    pack_ref[0, :, 3 * LANES : 4 * LANES] = grad_wo[:, 0:LANES].astype(BF16)
+    pack_ref[1, :, 3 * LANES : 4 * LANES] = grad_wo[:, LANES : 2 * LANES].astype(BF16)
+    wo_odd_ref[...] = grad_wo[:, 2 * LANES : 3 * LANES]
+    line_ref[...] = mm_tn(ub_ref[...], low_ref[...])
+
+    def spread_rows(s, d_to):
+        place = pl.ds(pl.multiple_of(d_to * part, part), part)
+        return place
+
+    def grad_copy(s, stage, j):
+        e = lax.rem(d + j, n)
+        lanes = pl.ds(0, 4 * LANES) if stage == 0 else pl.ds(4 * LANES, 2 * LANES)
+        return remote(
+            pack_ref.at[s, spread_rows(s, e), lanes],
+            pack_in_ref.at[s, d, :, lanes],
+            grad_send.at[stage, s, j],
+            grad_recv.at[stage, s, j],
+            (e, t),
+        )
+
+    def line_copy(j):
+        e = lax.rem(d + j, n)
+        return remote(
+            line_ref.at[spread_rows(0, e), :],
+            line_in_ref.at[d],
+            grad_send.at[2, 0, j],
+            grad_recv.at[2, 0, j],
+            (e, t),
+        )
+
+    head = half_mask(BLK)
+
+    def attend_back(p):
         dk_acc[...] = jnp.zeros_like(dk_acc)
         dv_acc[...] = jnp.zeros_like(dv_acc)
+        dq = []
         for i in range(blocks):
             rows = pl.ds(i * BLK, BLK)
             seen = pl.ds(0, (i + 1) * BLK)
+            lanes = pl.ds(pl.multiple_of(p * LANES, LANES), LANES)
             q, do = q_ref[p, rows, :], do_ref[rows, lanes]
             k, v = k_ref[p, seen, :], v_ref[p, seen, :]
             zero = jnp.zeros_like(q)
             parts = []
-            dk = dk_acc[seen, :]
-            dv = dv_acc[seen, :]
+            dk, dv = dk_acc[seen, :], dv_acc[seen, :]
             for side in range(2):
-                mask = head if side == 0 else jnp.logical_not(head)
-                qm, dom = jnp.where(mask, q, zero), jnp.where(mask, do, zero)
-                log_total = lse_ref[2 * p + side, 0:1, rows]
-                prob = jnp.exp(mm_nt(k, qm) - log_total)
+                chosen = head if side == 0 else jnp.logical_not(head)
+                qm, dom = jnp.where(chosen, q, zero), jnp.where(chosen, do, zero)
+                prob = jnp.exp(mm_nt(k, qm) - lse_ref[2 * p + side, 0:1, rows])
                 grad_prob = mm_nt(v, dom)
                 total = jnp.sum(prob * grad_prob, axis=0, keepdims=True)
                 grad_score = (prob * (grad_prob - total)).astype(BF16)
@@ -862,34 +872,232 @@
                 parts.append(mm_tn(grad_score, k))
             dk_acc[seen, :] = dk
             dv_acc[seen, :] = dv
-            dq = jnp.where(head, parts[0], parts[1]) * (HD**-0.5)
-            dp_ref[rows, lanes] = turn(dq, cos_ref[rows, :], -sin_ref[rows, :]).astype(BF16)
-        dp_ref[:, pl.ds(width + p * LANES, LANES)] = turn(
-            dk_acc[...], cos_ref[...], -sin_ref[...]
+            value = jnp.where(head, parts[0], parts[1]) * (HD**-0.5)
+            dq.append(turn(value, cos_ref[rows, :], -sin_ref[rows, :]))
+        return (
+            jnp.concatenate(dq, axis=0),
+            turn(dk_acc[...], cos_ref[...], -sin_ref[...]),
+            dv_acc[...],
+        )
+
+    def shard_step(i, carry):
+        s = lax.rem(m + 1 + i, 2)
+        for j, value in enumerate(attend_back(s)):
+            dp_ref[s, :, j * LANES : (j + 1) * LANES] = value.astype(BF16)
+        for j in range(3):
+            lanes = pl.ds(j * LANES, LANES)
+            pack_ref[s, :, lanes] = mm_tn(a_ref[...], dp_ref[s, :, lanes]).astype(BF16)
+        if not gathered:
+
+            def send(j, carry):
+                grad_copy(s, 0, j).start()
+                return carry
+
+            lax.fori_loop(1, n, send, 0)
+        return carry
+
+    lax.fori_loop(0, 2, shard_step, 0)
+    dq, dk, dv = attend_back(2)
+    wide = half_mask(rows_all)
+    odd = [
+        (jnp.where(wide, dq, swap_halves(dk)), jnp.where(wide, dv, 0.0)),
+        (jnp.where(wide, swap_halves(dq), dk), jnp.where(wide, swap_halves(dv), 0.0)),
+    ]
+    tall = half_mask(width)
+    for s in range(2):
+        for j in range(2):
+            dp_ref[s, :, (3 + j) * LANES : (4 + j) * LANES] = odd[s][j].astype(BF16)
+    for s in range(2):
+        pack_ref[s, :, 4 * LANES : 5 * LANES] = mm_tn(
+            a_ref[...], dp_ref[s, :, 3 * LANES : 4 * LANES]
         ).astype(BF16)
-        dp_ref[:, pl.ds(2 * width + p * LANES, LANES)] = dv_acc[...].astype(BF16)
-    for i in range(blocks):
-        rows = pl.ds(i * BLK, BLK)
-        da_ref[rows, :] = mm_nt(dp_ref[rows, :], w_ref[...]).astype(BF16)
-    for j in range(3 * pairs):
-        lanes = pl.ds(j * LANES, LANES)
-        grad_w_ref[:, lanes] = mm_tn(a_ref[...], dp_ref[:, lanes]).astype(BF16)
-
-
-def finish_kernel(x_ref, dh_ref, da_ref, gain_ref, grad_ref, row_ref):
-    rows_all, width = x_ref.shape
-    total = jnp.zeros((1, width), F32)
-    for i in range(rows_all // BLK):
-        rows = pl.ds(i * BLK, BLK)
+        last = mm_tn(a_ref[...], dp_ref[s, :, 4 * LANES : 5 * LANES])
+        side = wo_odd_ref[...]
+        side = swap_halves(side) if s == 0 else side
+        pack_ref[s, :, 5 * LANES : 6 * LANES] = jnp.where(tall, last, side).astype(BF16)
+    if not gathered:
+        for s in range(2):
+
+            def send(j, carry, s=s):
+                grad_copy(s, 1, j).start()
+                return carry
+
+            lax.fori_loop(1, n, send, 0)
+
+    def da_rows(start):
+        rows = pl.ds(pl.multiple_of(start, BLK), BLK)
+        total = jnp.zeros((BLK, width), F32)
+        for s in range(2):
+            total = total + mm_nt(dp_ref[s, rows, 0 : 3 * LANES], spread_ref[s, :, 0 : 3 * LANES])
+            total = total + mm_nt(
+                dp_ref[s, rows, 3 * LANES : 5 * LANES], spread_ref[s, :, 4 * LANES : 6 * LANES]
+            )
+        return total
+
+    def da_other(i, carry):
+        rows = pl.ds(pl.multiple_of(i * BLK, BLK), BLK)
+        da_out_ref[rows, :] = da_rows((1 - c) * rows_half + i * BLK).astype(BF16)
+        return carry
+
+    lax.fori_loop(0, rows_half // BLK, da_other, 0)
+    da_copy = remote(da_out_ref, da_in_ref, pair_send.at[1], pair_recv.at[1], partner)
+    da_copy.start()
+
+    def da_own(i, carry):
+        rows = pl.ds(pl.multiple_of(i * BLK, BLK), BLK)
+        da_own_ref[rows, :] = da_rows(c * rows_half + i * BLK)
+        return carry
+
+    lax.fori_loop(0, rows_half // BLK, da_own, 0)
+    da_copy.wait()
+    gain_attn = extra_ref[columns + 4 : columns + 5, :]
+    norm_ref[...] = jnp.zeros_like(norm_ref)
+
+    def finish(i, carry):
+        rows = pl.ds(pl.multiple_of(i * BLK, BLK), BLK)
         x = x_ref[rows, :].astype(F32)
         r = lax.rsqrt(jnp.mean(x * x, axis=-1, keepdims=True) + EPSILON)
-        n = x * r
-        da = da_ref[0, rows, :].astype(F32) + da_ref[1, rows, :].astype(F32)
-        total = total + jnp.sum(da * n, axis=0, keepdims=True)
-        dn = da * gain_ref[...]
-        grad = dh_ref[rows, :] + r * (dn - n * jnp.mean(dn * n, axis=-1, keepdims=True))
-        grad_ref[rows, :] = grad.astype(BF16)
-    row_ref[...] = jnp.broadcast_to(total, row_ref.shape)
+        normed = x * r
+        da = da_own_ref[rows, :] + da_in_ref[rows, :].astype(F32)
+        norm_ref[0:1, :] += jnp.sum(da * normed, axis=0, keepdims=True)
+        dn = da * gain_attn
+        grad = dh_ref[rows, :] + r * (dn - normed * jnp.mean(dn * normed, axis=-1, keepdims=True))
+        half_ref[0, rows, :] = grad.astype(BF16)
+        return carry
+
+    lax.fori_loop(0, rows_half // BLK, finish, 0)
+    norm_copy = remote(norm_ref, norm_in_ref, pair_send.at[2], pair_recv.at[2], partner)
+    norm_copy.start()
+
+    def publish(kind, out_ref):
+        block = out_ref.at[m, place]
+        copies = [
+            remote(half_ref.at[kind], block, out_send.at[kind, 0], out_recv.at[kind, 0], across),
+            remote(half_ref.at[kind], block, out_send.at[kind, 1], out_recv.at[kind, 1], partner),
+            pltpu.make_async_copy(half_ref.at[kind], block, stay.at[3 + kind]),
+        ]
+        for copy in copies:
+            copy.start()
+        block = out_ref.at[1 - m, place]
+        relay = remote(block, block, out_send.at[kind, 2], out_recv.at[kind, 2], partner)
+        return copies, relay
+
+    grad_x_copies, grad_x_relay = publish(0, grad_x_ref)
+
+    settle(2)
+
+    def results(i, carry):
+        rows = pl.ds(pl.multiple_of(i * BLK, BLK), BLK)
+        far = pl.ds(pl.multiple_of(c * rows_half + i * BLK, BLK), BLK)
+        values, e0, e1, wheres, first, second, on_u = facts(far)
+        sums, _ = combine(wheres, gy_ref)
+        h = h_ref[far, :]
+        u = h * values[6] * gain_moe
+        result = h + (sums + on_u * u + (first * values[3]) * vec0 + (second * values[5]) * vec1)
+        half_ref[1, rows, :] = result.astype(BF16)
+        return carry
+
+    lax.fori_loop(0, rows_half // BLK, results, 0)
+    result_copies, result_relay = publish(1, result_ref)
+
+    norm_copy.wait()
+    row_ref[3:4, :] = norm_ref[0:1, :] + norm_in_ref[0:1, :]
+    turned = jnp.concatenate([row_ref[...], jnp.zeros((LANES - 8, width), F32)], axis=0)
+    turned = jnp.transpose(turned)
+    lane = lax.broadcasted_iota(jnp.int32, (width, LANES), 1)
+    lines = line_ref[...]
+    for j, source in enumerate([3, 0, 1, 2]):
+        lines = jnp.where(lane == columns + 4 + j, turned[:, source : source + 1], lines)
+    line_ref[...] = lines
+    if gathered:
+        stores = [
+            pltpu.make_async_copy(pack_ref, grads_ref, load.at[0]),
+            pltpu.make_async_copy(line_ref, lines_ref, load.at[1]),
+        ]
+        for copy in stores:
+            copy.start()
+        for copy in stores:
+            copy.wait()
+    else:
+
+        def send(j, carry):
+            line_copy(j).start()
+            return carry
+
+        lax.fori_loop(1, n, send, 0)
+        mine = pl.ds(pl.multiple_of(d * part, part), part)
+        for s in range(2):
+            pack_in_ref[s, d] = pack_ref[s, mine, :]
+        line_in_ref[d] = line_ref[mine, :]
+
+        def arrive(j, carry):
+            for s in range(2):
+                for stage in range(2):
+                    grad_copy(s, stage, j).wait_recv()
+            return carry
+
+        lax.fori_loop(1, n, arrive, 0)
+
+        def total(s):
+            value = pack_in_ref[s, 0].astype(F32)
+            for e in range(1, n):
+                value = value + pack_in_ref[s, e].astype(F32)
+            return value
+
+        cross_ref[...] = total(1 - m).astype(BF16)
+        cross_copy = remote(cross_ref, cross_in_ref, pair_send.at[3], pair_recv.at[3], across)
+        cross_copy.start()
+        grads_ref[...] = total(m)
+
+        def arrive_lines(j, carry):
+            line_copy(j).wait()
+            return carry
+
+        lax.fori_loop(1, n, arrive_lines, 0)
+        value = line_in_ref[0]
+        for e in range(1, n):
+            value = value + line_in_ref[e]
+        cross_line_ref[0] = value
+        cross_line_copy = remote(
+            cross_line_ref.at[0], cross_line_ref.at[1], pair_send.at[4], pair_recv.at[4], across
+        )
+        cross_line_copy.start()
+        cross_copy.wait()
+        grads_ref[...] += cross_in_ref[...].astype(F32)
+        cross_line_copy.wait()
+        lines_ref[...] = cross_line_ref[0] + cross_line_ref[1]
+
+        def sent(j, carry):
+            for s in range(2):
+                for stage in range(2):
+                    grad_copy(s, stage, j).wait_send()
+            return carry
+
+        lax.fori_loop(1, n, sent, 0)
+
+    for copies, relay in ((grad_x_copies, grad_x_relay), (result_copies, result_relay)):
+        copies[0].wait_recv()
+        relay.start()
+    for copies, relay in ((grad_x_copies, grad_x_relay), (result_copies, result_relay)):
+        copies[0].wait_send()
+        copies[1].wait()
+        copies[2].wait()
+        relay.wait()
+    logit_copy.wait()
+
+    def clear(j, carry):
+        for kind in range(3):
+            give(kind, j).wait_send()
+        return carry
+
+    lax.fori_loop(1, n, clear, 0)
+
+    def passed(j, carry):
+        for kind in range(3):
+            hand(kind, j).wait_send()
+        return carry
+
+    lax.fori_loop(0, n, passed, 0)
 
 
 def across_chips(value):
@@ -1037,32 +1245,6 @@
             collective_id=0, has_side_effects=True, vmem_limit_bytes=VMEM_LIMIT
         ),
     )(tokens, cotangent, prev_logits, routes, packed, cosine, sine, w_in, w_down)
-    gain_attn = extra[columns + 4 : columns + 5]
-    gain_moe = extra[columns + 5 : columns + 6]
-    vectors = extra[columns + 6 : columns + 8]
-    o = lax.dynamic_slice_in_dim(o_all, c * local, local, axis=1)
-    wo_own = lax.dynamic_slice_in_dim(wo_all, c * local, local, axis=1)
-
-    def group(j, g):
-        return spread[j, :, g * LANES : (g + 1) * LANES]
-
-    w_heads = jnp.concatenate(
-        [
-            group(0, 0),
-            group(1, 0),
-            group(0, 4)[:, :HD],
-            group(1, 4)[:, :HD],
-            group(0, 1),
-            group(1, 1),
-            group(0, 4)[:, HD:],
-            group(1, 4)[:, HD:],
-            group(0, 2),
-            group(1, 2),
-            group(0, 5)[:, :HD],
-            group(1, 5)[:, :HD],
-        ],
-        axis=1,
-    )
 
     hidden_width = w_in.shape[3]
     slots_all = experts * padded
@@ -1140,111 +1322,126 @@
     )
     gy, dx, dg = parts[0:3]
     gin, gdown = parts[3:7], parts[7:11]
-    gy_all, dx_all, dg_all = give_back(4, n, gy, dx, dg)
-
-    def total_in(own, core, chip, diagonal):
-        own = own.astype(F32) + across_cores(core).astype(F32)
+    def chip_part(core, chip, diagonal):
+        mine = across_cores(core)
         chip = (chip.astype(F32) + across_cores(diagonal).astype(F32)).astype(BF16)
-        return own + across_chips(chip).astype(F32)
-
-    grad_in = total_in(*gin)
-    grad_down = total_in(*gdown)
-
-    result, dl, dh, do, grad_wo, grad_small, grad_lines = compute_call(
-        functools.partial(back_kernel, experts, half, padded),
-        [
-            struct((rows, width), BF16),
-            struct((rows, LANES), F32),
-            struct((rows, width), F32),
-            struct((rows, local), BF16),
-            struct((width, local), BF16),
-            struct((width, LANES), F32),
-            struct((width, LANES), F32),
+        return mine, chip
+
+    mine_in, chip_in = chip_part(gin[1], gin[2], gin[3])
+    mine_down, chip_down = chip_part(gdown[1], gdown[2], gdown[3])
+    chip_in, chip_down, dx = lax.optimization_barrier((chip_in, chip_down, dx))
+    grad_in = gin[0].astype(F32) + mine_in.astype(F32) + across_chips(chip_in).astype(F32)
+    grad_down = gdown[0].astype(F32) + mine_down.astype(F32) + across_chips(chip_down).astype(F32)
+
+    groups = 6 * LANES
+    logit_rows = -(-columns // 8) * 8
+    rear_outs = [
+        struct((2, logit_rows, rows), F32),
+        struct((2, width, groups), BF16) if gathered else struct((part, groups), F32),
+        struct((width if gathered else part, LANES), F32),
+    ]
+    half_rows = rows // 2
+    spread_n = 1 if gathered else n
+    results, input_grads, logits, grads, lines = pl.pallas_call(
+        functools.partial(rear_kernel, n, half, padded, gathered, part),
+        out_shape=[struct((2, rows, width), BF16)] * 2 + rear_outs,
+        in_specs=[aspec()] * 7 + [vspec()] * 15,
+        out_specs=[aspec()] * 2 + [vspec()] + [aspec() if gathered else vspec()] * 2,
+        scratch_shapes=[
+            pltpu.VMEM((half_rows, width), BF16),
+            pltpu.VMEM((rows, width), BF16),
+            pltpu.VMEM((rows, 2), jnp.int32),
+            pltpu.VMEM((rows, local), BF16),
+            pltpu.VMEM((2, n, padded, width), BF16),
+            pltpu.VMEM((2, n, padded, width), BF16),
+            pltpu.VMEM((2, n, 8, padded), F32),
+            pltpu.VMEM((half_rows, width), F32),
+            pltpu.VMEM((rows, width), BF16),
+            pltpu.VMEM((rows, local), BF16),
+            pltpu.VMEM((rows, LANES), BF16),
+            pltpu.VMEM((8, width), F32),
+            pltpu.VMEM((2, rows, 5 * LANES), BF16),
+            pltpu.VMEM((rows, LANES), F32),
+            pltpu.VMEM((rows, LANES), F32),
+            pltpu.VMEM((width, LANES), F32),
+            pltpu.VMEM((2, width, groups), BF16),
+            pltpu.VMEM((width, LANES), F32),
+            pltpu.VMEM((2, spread_n, part, groups), BF16),
+            pltpu.VMEM((spread_n, part, LANES), F32),
+            pltpu.VMEM((part, groups), BF16),
+            pltpu.VMEM((part, groups), BF16),
+            pltpu.VMEM((2, part, LANES), F32),
+            pltpu.VMEM((half_rows, width), BF16),
+            pltpu.VMEM((half_rows, width), BF16),
+            pltpu.VMEM((half_rows, width), F32),
+            pltpu.VMEM((8, width), F32),
+            pltpu.VMEM((8, width), F32),
+            pltpu.VMEM((2, half_rows, width), BF16),
+            dma((4,)),
+            dma((n,)),
+            dma((n,)),
+            dma((n,)),
+            dma((n,)),
+            dma((n,)),
+            dma((n,)),
+            dma((5,)),
+            dma((3, n)),
+            dma((3, n)),
+            dma((3, 2, n)),
+            dma((3, 2, n)),
+            dma((5,)),
+            dma((5,)),
+            dma((2, 3)),
+            dma((2, 3)),
         ],
+        compiler_params=pltpu.CompilerParams(
+            collective_id=1, has_side_effects=True, vmem_limit_bytes=VMEM_LIMIT
+        ),
+    )(
+        gy,
+        dx,
+        dg,
+        tokens,
+        cotangent,
+        routes,
+        o_all,
         h,
         ub,
         stats,
-        choose,
         pos,
-        dy,
-        gy_all,
-        dx_all,
-        dg_all,
         small_all,
-        gain_moe,
-        vectors,
-        o,
-        wo_own,
-        flops=8 * experts * padded * rows * width,
-        scratch=[
-            pltpu.VMEM((rows, LANES), BF16),
-            pltpu.VMEM((rows, width), BF16),
-            pltpu.VMEM((8, width), F32),
-        ],
-    )
-    results = share_output(5, result)
-    da, grad_heads = compute_call(
-        attention_back_kernel,
-        [struct((rows, width), BF16), struct((width, 3 * local), BF16)],
+        extra,
+        wo_all,
         q,
         k,
         v,
-        do,
+        a,
         lse,
-        a,
-        w_heads,
+        spread,
         cosine,
         sine,
-        flops=4 * rows * width * 3 * local + 20 * rows * rows * local,
-        scratch=[
-            pltpu.VMEM((rows, 3 * local), BF16),
-            pltpu.VMEM((rows, LANES), F32),
-            pltpu.VMEM((rows, LANES), F32),
-        ],
     )
-    da_all = core_share(6, da)[0]
-    grad_x, grad_line = compute_call(
-        finish_kernel,
-        [struct((rows, width), BF16), struct((8, width), F32)],
-        x,
-        dh,
-        da_all,
-        gain_attn,
-    )
-    input_grads = share_output(7, grad_x)
-
-    grads = jnp.stack(
-        [
-            jnp.concatenate(
-                [
-                    piece[:, i * local + start : i * local + start + size]
-                    for piece, i in [(grad_heads, 0), (grad_heads, 1), (grad_heads, 2), (grad_wo, 0)]
-                    for start, size in [(j * LANES, LANES), (2 * LANES + j * HD, HD)]
-                ],
-                axis=1,
-            )
-            for j in range(2)
-        ]
-    ).reshape(2, n, part, 4 * share)
-    lines = grad_small + jnp.pad(
-        jnp.concatenate([grad_line[0:1].T, grad_lines[:, 0:3]], axis=1),
-        ((0, 0), (columns + 4, LANES - columns - 8)),
-    )
-    lines = jnp.broadcast_to(lines.reshape(1, n, part, LANES), (2, n, part, LANES))
-    grads_in, lines_in = spread_gradients(8, n, grads, lines)
-    grads = jnp.sum(grads_in.astype(F32), axis=(0, 1))
-    lines = jnp.sum(lines_in, axis=(0, 1))
-    dl = dl[:, :columns]
-    dl_x = across_chips(dl)
-    logit_grads = jnp.where(m == 0, jnp.stack([dl, dl_x]), jnp.stack([dl_x, dl]))
+    if gathered:
+        grads = lax.psum_scatter(grads.astype(F32), "dp", scatter_dimension=1, tiled=True)
+        lines = lax.psum_scatter(lines, "dp", scatter_dimension=0, tiled=True)
+        other = lax.dynamic_index_in_dim(grads, 1 - m, 0, keepdims=False)
+        grads = lax.dynamic_index_in_dim(grads, m, 0, keepdims=False) + across_chips(other)
+        lines = lines + across_chips(lines)
+
+    def heads(j):
+        start = (4 + (j % 4) // 2) * LANES + (j % 2) * HD
+        return jnp.concatenate(
+            [grads[:, j * LANES : (j + 1) * LANES], grads[:, start : start + HD]], axis=1
+        )
+
     return (
         results,
         input_grads,
-        logit_grads,
+        jnp.swapaxes(logits[:, :columns], 1, 2),
         lines[:, columns + 4],
         lines[:, columns + 5],
-        jnp.stack([grads[:, i * share : (i + 1) * share] for i in range(3)]),
-        grads[:, 3 * share :].T,
+        jnp.stack([heads(i) for i in range(3)]),
+        heads(3).T,
         lines[:, :columns],
         lines[:, columns : columns + 4],
         lines[:, columns + 6 : columns + 8].T,

time: 669 us -> 454 us (0.68)
  Pallas kernels: 591 us -> 356 us
  waiting for transfers between devices: 0.02 us -> 49.3 us
  local copies, waits for them, and re-layouts: 46.7 us -> 25.5 us
    pallas_call x8 -> x1, Pallas kernels: 396 us -> 162 us  [body(): pl.pallas_call(functools.partial(rear_kernel, n, half, padded, gathered,...]
    ppermute x3 -> x2, waiting for transfers between devices: 0.01 us -> 44.5 us  [across_chips(): return lax.ppermute(value, 'tensor', [(0, 2), (2, 0), (1, 3), (3, 1)])]
    concatenate x3 -> x0, local copies, waits for them, and re-layouts: 7.25 us -> none  [the longest x2 4.98 us: body(): jnp.concatenate([piece[:, i * local + start:i * local + start + size] for...]
    unnamed x40 -> x27, local copies, waits for them, and re-layouts: 14.8 us -> 15.7 us
  transfers between devices with their start and end apart: 7 -> 6, of which waited for: 0 -> 2; matrix products, arithmetic and copies ran while one was open for 7% -> 4% of each run, Pallas kernels for 60% -> 36%
where the time goes in v3:
time: 454 us; the launch traced here: 447 us
  Pallas kernels  356 us (78%)
  waiting for transfers between devices  49.3 us (11%)
  local copies, waits for them, and re-layouts  25.5 us (6%)
  other arithmetic  11 us (2%)
    pallas_call x1, Pallas kernels, body(): pl.pallas_call(functools.partial(rear_kernel, n, half, padded, gathered,...  162 us
    pallas_call x1, Pallas kernels, body(): pl.pallas_call(functools.partial(front_kernel, n, half, padded, gathered)...  146 us
    pallas_call x1, Pallas kernels, body(): pl.pallas_call(functools.partial(expert_kernel, n, padded), grid=(4 * per...  48.1 us
    ppermute x2, waiting for transfers between devices, across_chips(): return lax.ppermute(value, 'tensor', [(0, 2), (2, 0), (1, 3), (3, 1)])  44.5 us
    unnamed x27, local copies, waits for them, and re-layouts  15.7 us
  transfers between devices with their start and end apart: 6, of which 2 were waited for; matrix products, arithmetic and copies ran while one was open for 4% of the time, Pallas kernels for 36%

profile of v3, /device:TPU:26, one launch (start us, length us, event | category | flops | bytes accessed | tf_op | source)
XLA Modules:
  0.0 446.6 jit_solution(788556596895312504)
XLA Ops:
  0.7 0.9 copy.41
  1.6 0.8 slice_bitcast_fusion.2
  2.4 0.8 slice_bitcast_fusion.5
  3.2 0.8 copy.45
  3.9 0.8 copy.46
  4.7 0.8 copy.43
  5.5 0.8 copy.44
  6.3 0.8 copy.42
  7.1 2.1 copy.48.routes_all_ref
  9.2 1.3 copy.47.prev_all_ref
  10.5 0.8 concatenate.15.packed_ref
  11.3 146.3 %shard_map.238 = (bf16[1024,768]{1,0:T(8,128)(2,1)}, bf16[3,1024,128]{2,1,0:T(8,128)(2,1)}, bf16[3,1024,128]{2,1,0:T(8,128)(2,1)}, bf16[3,1024,128]{2,1,0:T(8,12...) custom-call(bf16[2,1024,768]{2,1,0:T(8,128)(2,1)} %tokens_ref.3, ...), custom_call_target="tpu_custom_call" | custom-call | tf_op jit(solution)/shard_map/pallas_call | solution.py:1214
  157.6 48.1 %shard_map.239 = (bf16[8,128,768]{2,1,0:T(8,128)(2,1)}, bf16[8,128,768]{2,1,0:T(8,128)(2,1)}, f32[8,8,128]{2,1,0:T(8,128)}, bf16[1,2,768,512]{3,2,1,0:T(8,128)(2...) custom-call(bf16[1024,768]{1,0:T(8,128)(2,1)} %bitcast.37, ...), custom_call_target="tpu_custom_call" | custom-call | flops 28991029248 | bytes 30000000 | tf_op jit(solution)/shard_map/pallas_call | solution.py:1277
  206.9 4.8 %collective-permute-done.1 = bf16[1,512,768]{2,1,0:T(8,128)(2,1)S(1)} collective-permute-done((bf16[1,512,768]{2,1,0:T(8,128)(2,1)}, bf16[1,512,768]{2,1,0:T(8,128)(2,1)S(1)}, u32[]{:S(2)}, u32[]{:S(2)}) %collective-permute-start.1) | collective-permute-done | bytes 786464 | tf_op jit(solution)/shard_map/ppermute | solution.py:1108
  211.7 2.2 add_convert_fusion.1
  214.4 162.1 %shard_map.240 = (bf16[2,1024,768]{2,1,0:T(8,128)(2,1)}, bf16[2,1024,768]{2,1,0:T(8,128)(2,1)}, f32[2,16,1024]{2,1,0:T(8,128)}, f32[96,768]{1,0:T(8,128)}, f32[96,128]{1,0:T(8,128)}) custom-call(bf16[8,128,768]{2,1,0:T(8,128)(2,1)} %get-tuple-element.63.gy_src_ref, bf16[8,128,768]{2,1,0:T(8,128)(2,1)} %get-tuple-element.69.dx_src_ref, ...), custom_call_target="tpu_custom_call" | custom-call | tf_op jit(solution)/shard_map/pallas_call | solution.py:1345
  376.5 0.9 slice.86
  377.4 0.9 slice_bitcast_fusion.1
  378.3 1.5 copy.52
  381.7 0.9 slice_bitcast_fusion
  383.3 1.4 collective-permute-start.5
  384.7 1.0 fusion.1
  385.7 1.5 fusion
  387.2 0.7 copy.51
  388.7 0.8 maximum_bitcast_fusion.2
  389.5 0.7 pad_maximum_fusion
  390.2 44.4 %collective-permute-done.5 = bf16[1,512,768]{2,1,0:T(8,128)(2,1)} collective-permute-done((bf16[1,512,768]{2,1,0:T(8,128)(2,1)}, bf16[1,512,768]{2,1,0:T(8,128)(2,1)}, u32[]{:S(2)}, u32[]{:S(2)}) %collective-permute-start.5) | collective-permute-done | bytes 786464 | tf_op jit(solution)/shard_map/ppermute | solution.py:1104
  434.7 3.0 convert_add_fusion.1
  437.7 3.8 convert_add_fusion
  441.5 1.7 copy.57
  443.2 1.4 copy-done
  444.5 1.7 copy.58
  (32 shorter events, 4.9 us)
Async XLA Ops:
  0.6 8.5 %copy-start.6 = (f32[2,1024,12]{1,0,2:T(2,128)S(1)}, f32[2,1024,12]{1,0,2:T(2,128)}, u32[]{:S(2)}) copy-start(f32[2,1024,12]{1,0,2:T(2,128)} %param.17) | copy-start | bytes 294916
  205.8 8.2 %copy-start.2 = (bf16[1,2,768,512]{3,2,1,0:T(8,128)(2,1)S(1)}, bf16[1,2,768,512]{3,2,1,0:T(8,128)(2,1)}, u32[]{:S(2)}) copy-start(bf16[1,2,768,512]{3,2,1,0:T(8,128)(2,1)} %get-tuple-element.64) | copy-start | bytes 4718596
  205.8 8.2 %collective-permute-start = (bf16[1,2,768,512]{3,2,1,0:T(8,128)(2,1)}, bf16[1,2,768,512]{3,2,1,0:T(8,128)(2,1)S(1)}, u32[]{:S(2)}, u32[]{:S(2)}) collective-permute-start(bf16[1,2,768,512]{3,2,1,0:T(8,128)(2,1)} %get-tuple-element.65), channel_id=1, source_target_pairs={{0,1},{1,0},{2,3},{3,2},{4,5},{5,4},{6,7},{7,6},{8,9},{9,8},{10,11... | collective-permute-start | bytes 4718600 | tf_op jit(solution)/shard_map/ppermute | solution.py:1108
  205.8 5.9 %collective-permute-start.1 = (bf16[1,512,768]{2,1,0:T(8,128)(2,1)}, bf16[1,512,768]{2,1,0:T(8,128)(2,1)S(1)}, u32[]{:S(2)}, u32[]{:S(2)}) collective-permute-start(bf16[1,512,768]{2,1,0:T(8,128)(2,1)} %get-tuple-element.67), channel_id=1, source_target_pairs={{0,1},{1,0},{2,3},{3,2},{4,5},{5,4},{6,7},{7,6},{8,9},{9,8},{10,11... | collective-permute-start | bytes 2359304 | tf_op jit(solution)/shard_map/ppermute | solution.py:1108
  206.3 183.9 %collective-permute-start.4 = (bf16[1,512,768]{2,1,0:T(8,128)(2,1)}, bf16[1,512,768]{2,1,0:T(8,128)(2,1)}, u32[]{:S(2)}, u32[]{:S(2)}) collective-permute-start(bf16[1,512,768]{2,1,0:T(8,128)(2,1)} %get-tuple-element.94), channel_id=1, source_target_pairs={{0,1},{1,0},{2,3},{3,2},{4,5},{5,4},{6,7},{7,6},{8,9},{9,8},{10,11... | collective-permute-start | bytes 2359304 | tf_op jit(solution)/shard_map/ppermute | solution.py:1108
  206.4 231.3 %collective-permute-start.2 = (bf16[1,2,768,512]{3,2,1,0:T(8,128)(2,1)}, bf16[1,2,768,512]{3,2,1,0:T(8,128)(2,1)S(1)}, u32[]{:S(2)}, u32[]{:S(2)}) collective-permute-start(bf16[1,2,768,512]{3,2,1,0:T(8,128)(2,1)} %get-tuple-element.91), channel_id=1, source_target_pairs={{0,1},{1,0},{2,3},{3,2},{4,5},{5,4},{6,7},{7,6},{8,9},{9,8},{10,11... | collective-permute-start | bytes 4718600 | tf_op jit(solution)/shard_map/ppermute | solution.py:1108
  376.5 11.5 %copy-start.4 = (f32[96,128]{1,0:T(8,128)S(1)}, f32[96,128]{1,0:T(8,128)}, u32[]{:S(2)}) copy-start(f32[96,128]{1,0:T(8,128)} %get-tuple-element.88) | copy-start | bytes 147460
  381.1 56.6 %collective-permute-start.3 = (bf16[1,2,768,512]{3,2,1,0:T(8,128)(2,1)S(1)}, bf16[1,2,768,512]{3,2,1,0:T(8,128)(2,1)}, u32[]{:S(2)}, u32[]{:S(2)}) collective-permute-start(bf16[1,2,768,512]{3,2,1,0:T(8,128)(2,1)S(1)} %add_convert_fusion), channel_id=1, source_target_pairs={{0,2},{2,0},{1,3},{3,1},{4,6},{6,4},{5,7},{7,5},{8,10},{10,8},{9,1... | collective-permute-start | bytes 4718600 | tf_op jit(solution)/shard_map/ppermute | solution.py:1104
  383.3 51.4 %collective-permute-start.5 = (bf16[1,512,768]{2,1,0:T(8,128)(2,1)}, bf16[1,512,768]{2,1,0:T(8,128)(2,1)}, u32[]{:S(2)}, u32[]{:S(2)}) collective-permute-start(bf16[1,512,768]{2,1,0:T(8,128)(2,1)} %add_convert_fusion.1), channel_id=1, source_target_pairs={{0,2},{2,0},{1,3},{3,1},{4,6},{6,4},{5,7},{7,5},{8,10},{10,8},{9,1... | collective-permute-start | bytes 2359304 | tf_op jit(solution)/shard_map/ppermute | solution.py:1104
  388.0 46.7 %copy-start.5 = (bf16[1,512,768]{2,1,0:T(8,128)(2,1)S(1)}, bf16[1,512,768]{2,1,0:T(8,128)(2,1)}, u32[]{:S(2)}) copy-start(bf16[1,512,768]{2,1,0:T(8,128)(2,1)} %get-tuple-element.93) | copy-start | bytes 2359300
  434.7 3.0 copy-start.3
  437.7 3.8 copy-start.1
  441.5 3.0 copy-start

commit v4 on v3

--- a/solution.py
+++ b/solution.py
@@ -63,11 +63,6 @@
 
 def plane_peers(n, d, t):
     return [(lax.rem(d + j, n), t) for j in range(1, n)]
-
-
-def all_peers(n, d, t):
-    other = lax.rem(t + 2, 4)
-    return plane_peers(n, d, t) + [(lax.rem(d + j, n), other) for j in range(n)]
 
 
 def slot_hot(half, padded, base, places):
@@ -202,27 +197,77 @@
     ]
     for copy in loads:
         copy.start()
-    peers = all_peers(n, d, t)
-    greet(peers + [partner])
-    pack_copies = []
+    greet(plane_peers(n, d, t) + [partner, across])
+    part = packed_ref.shape[0]
+    beside = (d + 1 - 2 * lax.rem(d, 2), t)
+    lanes_a = pl.ds(0, 4 * LANES)
+    lanes_b = pl.ds(4 * LANES, packed_ref.shape[-1] - 4 * LANES)
+
+    def behind(j):
+        return lax.rem(d + n - 2 * j, n)
+
+    def shard(chip, owner, lanes):
+        return spread_ref.at[chip, pl.ds(pl.multiple_of(owner * part, part), part), lanes]
+
+    def pass_on(chip, owner, lanes, row, j, peer):
+        block = shard(chip, owner, lanes)
+        return remote(block, block, pack_send.at[row, j], pack_recv.at[row, j], peer)
+
+    def ahead(j):
+        return (lax.rem(d + 2 * j, n), t)
+
+    ring = n // 2
     if gathered:
         spread_ref[...] = packed_ref[...]
     else:
-        part = packed_ref.shape[0]
-        place = pl.ds(pl.multiple_of(d * part, part), part)
-        spread_ref[m, place, :] = packed_ref[...]
-        for i, peer in enumerate(peers):
-            pack_copies.append(
-                remote(
-                    packed_ref,
-                    spread_ref.at[m, place, :],
-                    pack_send.at[i],
-                    pack_recv.at[i],
-                    peer,
-                )
-            )
-        for copy in pack_copies:
+        spread_ref[m, pl.ds(pl.multiple_of(d * part, part), part), :] = packed_ref[...]
+        a_x = pass_on(m, d, lanes_a, 4, 0, across)
+        sends = [a_x]
+        for j in range(1, ring):
+            sends.append(pass_on(m, d, lanes_a, 0, j, ahead(j)))
+            sends.append(pass_on(m, d, lanes_b, 4, j, ahead(j)))
+        sends.append(pass_on(m, d, lanes_a, 2, 0, beside))
+        sends.append(pass_on(m, d, lanes_b, 5, 0, beside))
+        sends.append(pass_on(m, d, lanes_b, 6, 0, across))
+        for copy in sends:
             copy.start()
+
+    def relay_gather():
+        if gathered:
+            return
+        a_x.wait_recv()
+        more = [pass_on(1 - m, d, lanes_a, 1, j, ahead(j)) for j in range(1, ring)]
+        more.append(pass_on(1 - m, d, lanes_a, 3, 0, beside))
+        for copy in more:
+            copy.start()
+        sends.extend(more)
+        for j in range(1, ring):
+            pass_on(m, d, lanes_b, 4, j, ahead(j)).wait_recv()
+            more = [
+                pass_on(m, behind(j), lanes_b, 5, j, beside),
+                pass_on(m, behind(j), lanes_b, 6, j, across),
+            ]
+            pass_on(m, d, lanes_a, 0, j, ahead(j)).wait_recv()
+            more.append(pass_on(m, behind(j), lanes_a, 2, j, beside))
+            for copy in more:
+                copy.start()
+            sends.extend(more)
+        for j in range(1, ring):
+            pass_on(1 - m, d, lanes_a, 1, j, ahead(j)).wait_recv()
+            copy = pass_on(1 - m, behind(j), lanes_a, 3, j, beside)
+            copy.start()
+            sends.append(copy)
+        for j in range(ring):
+            pass_on(m, d, lanes_b, 5, j, beside).wait_recv()
+            owner = lax.rem(beside[0] + n - 2 * j, n)
+            copy = pass_on(m, owner, lanes_b, 7, j, across)
+            copy.start()
+            sends.append(copy)
+        for j in range(ring):
+            pass_on(m, d, lanes_a, 2, j, beside).wait_recv()
+            pass_on(m, d, lanes_a, 3, j, beside).wait_recv()
+            pass_on(m, d, lanes_b, 6, j, across).wait_recv()
+            pass_on(m, d, lanes_b, 7, j, across).wait_recv()
 
     loads[0].wait()
     line = lax.broadcasted_iota(jnp.int32, (rows_all, LANES), 1)
@@ -278,18 +323,17 @@
         e = lax.rem(d + j, n)
         hot = slot_hot(half, padded, base, place_ref[pl.ds(e, 1), :])
         dy_slot_ref[e] = mm(hot, dy_ref[...]).astype(BF16)
-
-        @pl.when(i < n - 1)
-        def _():
-            dy_copy(j).start()
-
         return carry
 
     lax.fori_loop(0, n, dy_step, 0)
+    relay_gather()
     stays[0].start()
 
-    for copy in pack_copies:
-        copy.wait_recv()
+    def dy_start(j, carry):
+        dy_copy(j).start()
+        return carry
+
+    lax.fori_loop(1, n, dy_start, 0)
     weight_copies = [
         remote(win_ref, in_x_ref, w_send.at[0], w_recv.at[0], across),
         remote(wdown_ref, down_x_ref, w_send.at[1], w_recv.at[1], across),
@@ -459,7 +503,7 @@
     lax.fori_loop(1, n, finish, 0)
     for copy in stays:
         copy.wait()
-    for copy in pack_copies + weight_copies[0:2]:
+    for copy in ([] if gathered else sends) + weight_copies[0:2]:
         copy.wait_send()
     for copy in weight_copies[2:6]:
         copy.wait()
@@ -587,7 +631,8 @@
     wo_odd_ref,
     pack_ref,
     line_ref,
-    pack_in_ref,
+    y_in_ref,
+    z_in_ref,
     line_in_ref,
     cross_ref,
     cross_in_ref,
@@ -610,6 +655,8 @@
     pass_recv,
     grad_send,
     grad_recv,
+    line_send,
+    line_recv,
     pair_send,
     pair_recv,
     out_send,
@@ -820,28 +867,57 @@
     wo_odd_ref[...] = grad_wo[:, 2 * LANES : 3 * LANES]
     line_ref[...] = mm_tn(ub_ref[...], low_ref[...])
 
-    def spread_rows(s, d_to):
-        place = pl.ds(pl.multiple_of(d_to * part, part), part)
-        return place
-
-    def grad_copy(s, stage, j):
-        e = lax.rem(d + j, n)
-        lanes = pl.ds(0, 4 * LANES) if stage == 0 else pl.ds(4 * LANES, 2 * LANES)
+    def slab(owner):
+        return pl.ds(pl.multiple_of(owner * part, part), part)
+
+    ring = n // 2
+    y_own = lax.rem(d, 2)
+    beside = (d + 1 - 2 * y_own, t)
+    z_own = lax.div(d, 2)
+    wide_lanes = (pl.ds(0, 4 * LANES), pl.ds(4 * LANES, 2 * LANES))
+
+    def y_copy(s, stage, z):
+        lanes = wide_lanes[stage]
         return remote(
-            pack_ref.at[s, spread_rows(s, e), lanes],
-            pack_in_ref.at[s, d, :, lanes],
-            grad_send.at[stage, s, j],
-            grad_recv.at[stage, s, j],
-            (e, t),
-        )
+            pack_ref.at[s, slab(2 * z + 1 - y_own), lanes],
+            y_in_ref.at[s, z, :, lanes],
+            grad_send.at[stage, s, z],
+            grad_recv.at[stage, s, z],
+            beside,
+        )
+
+    def z_copy(s, stage, j):
+        lanes = wide_lanes[stage]
+        z = lax.rem(z_own + j, ring)
+        return remote(
+            pack_ref.at[s, slab(2 * z + y_own), lanes],
+            z_in_ref.at[s, j, :, lanes],
+            grad_send.at[2 + stage, s, j],
+            grad_recv.at[2 + stage, s, j],
+            (2 * z + y_own, t),
+        )
+
+    def y_start(s, stage):
+        for z in range(ring):
+            y_copy(s, stage, z).start()
+
+    def z_start(s, stage):
+        lanes = wide_lanes[stage]
+        for z in range(ring):
+            y_copy(s, stage, z).wait()
+            rows = slab(2 * z + y_own)
+            value = pack_ref[s, rows, lanes].astype(F32) + y_in_ref[s, z, :, lanes].astype(F32)
+            pack_ref[s, rows, lanes] = value.astype(BF16)
+        for j in range(1, ring):
+            z_copy(s, stage, j).start()
 
     def line_copy(j):
         e = lax.rem(d + j, n)
         return remote(
-            line_ref.at[spread_rows(0, e), :],
+            line_ref.at[slab(e), :],
             line_in_ref.at[d],
-            grad_send.at[2, 0, j],
-            grad_recv.at[2, 0, j],
+            line_send.at[j],
+            line_recv.at[j],
             (e, t),
         )
 
@@ -888,12 +964,12 @@
             lanes = pl.ds(j * LANES, LANES)
             pack_ref[s, :, lanes] = mm_tn(a_ref[...], dp_ref[s, :, lanes]).astype(BF16)
         if not gathered:
-
-            def send(j, carry):
-                grad_copy(s, 0, j).start()
-                return carry
-
-            lax.fori_loop(1, n, send, 0)
+            y_start(s, 0)
+
+            @pl.when(i == 1)
+            def _():
+                z_start(lax.rem(m + 1, 2), 0)
+
         return carry
 
     lax.fori_loop(0, 2, shard_step, 0)
@@ -916,13 +992,9 @@
         side = swap_halves(side) if s == 0 else side
         pack_ref[s, :, 5 * LANES : 6 * LANES] = jnp.where(tall, last, side).astype(BF16)
     if not gathered:
-        for s in range(2):
-
-            def send(j, carry, s=s):
-                grad_copy(s, 1, j).start()
-                return carry
-
-            lax.fori_loop(1, n, send, 0)
+        y_start(0, 1)
+        y_start(1, 1)
+        z_start(m, 0)
 
     def da_rows(start):
         rows = pl.ds(pl.multiple_of(start, BLK), BLK)
@@ -949,6 +1021,9 @@
         return carry
 
     lax.fori_loop(0, rows_half // BLK, da_own, 0)
+    if not gathered:
+        z_start(0, 1)
+        z_start(1, 1)
     da_copy.wait()
     gain_attn = extra_ref[columns + 4 : columns + 5, :]
     norm_ref[...] = jnp.zeros_like(norm_ref)
@@ -1025,23 +1100,16 @@
             return carry
 
         lax.fori_loop(1, n, send, 0)
-        mine = pl.ds(pl.multiple_of(d * part, part), part)
+        line_in_ref[d] = line_ref[slab(d), :]
         for s in range(2):
-            pack_in_ref[s, d] = pack_ref[s, mine, :]
-        line_in_ref[d] = line_ref[mine, :]
-
-        def arrive(j, carry):
-            for s in range(2):
-                for stage in range(2):
-                    grad_copy(s, stage, j).wait_recv()
-            return carry
-
-        lax.fori_loop(1, n, arrive, 0)
+            for stage in range(2):
+                for j in range(1, ring):
+                    z_copy(s, stage, j).wait()
 
         def total(s):
-            value = pack_in_ref[s, 0].astype(F32)
-            for e in range(1, n):
-                value = value + pack_in_ref[s, e].astype(F32)
+            value = pack_ref[s, slab(d), :].astype(F32)
+            for j in range(1, ring):
+                value = value + z_in_ref[s, j].astype(F32)
             return value
 
         cross_ref[...] = total(1 - m).astype(BF16)
@@ -1066,14 +1134,6 @@
         grads_ref[...] += cross_in_ref[...].astype(F32)
         cross_line_copy.wait()
         lines_ref[...] = cross_line_ref[0] + cross_line_ref[1]
-
-        def sent(j, carry):
-            for s in range(2):
-                for stage in range(2):
-                    grad_copy(s, stage, j).wait_send()
-            return carry
-
-        lax.fori_loop(1, n, sent, 0)
 
     for copies, relay in ((grad_x_copies, grad_x_relay), (result_copies, result_relay)):
         copies[0].wait_recv()
@@ -1227,8 +1287,8 @@
             pltpu.VMEM((n, 8, padded), F32),
             pltpu.VMEM((n, padded, width), BF16),
             dma((4,)),
-            dma((2 * n,)),
-            dma((2 * n,)),
+            dma((8, n // 2)),
+            dma((8, n // 2)),
             dma((n,)),
             dma((n,)),
             dma((n,)),
@@ -1243,6 +1303,9 @@
         ],
         compiler_params=pltpu.CompilerParams(
             collective_id=0, has_side_effects=True, vmem_limit_bytes=VMEM_LIMIT
+        ),
+        cost_estimate=pl.CostEstimate(
+            flops=60_000_000_000, bytes_accessed=60_000_000, transcendentals=0
         ),
     )(tokens, cotangent, prev_logits, routes, packed, cosine, sine, w_in, w_down)
 
@@ -1341,7 +1404,8 @@
         struct((width if gathered else part, LANES), F32),
     ]
     half_rows = rows // 2
-    spread_n = 1 if gathered else n
+    spread_n = 1 if gathered else n // 2
+    line_n = 1 if gathered else n
     results, input_grads, logits, grads, lines = pl.pallas_call(
         functools.partial(rear_kernel, n, half, padded, gathered, part),
         out_shape=[struct((2, rows, width), BF16)] * 2 + rear_outs,
@@ -1367,7 +1431,8 @@
             pltpu.VMEM((2, width, groups), BF16),
             pltpu.VMEM((width, LANES), F32),
             pltpu.VMEM((2, spread_n, part, groups), BF16),
-            pltpu.VMEM((spread_n, part, LANES), F32),
+            pltpu.VMEM((2, spread_n, part, groups), BF16),
+            pltpu.VMEM((line_n, part, LANES), F32),
             pltpu.VMEM((part, groups), BF16),
             pltpu.VMEM((part, groups), BF16),
             pltpu.VMEM((2, part, LANES), F32),
@@ -1387,8 +1452,10 @@
             dma((5,)),
             dma((3, n)),
             dma((3, n)),
-            dma((3, 2, n)),
-            dma((3, 2, n)),
+            dma((4, 2, n // 2)),
+            dma((4, 2, n // 2)),
+            dma((n,)),
+            dma((n,)),
             dma((5,)),
             dma((5,)),
             dma((2, 3)),
@@ -1396,6 +1463,9 @@
         ],
         compiler_params=pltpu.CompilerParams(
             collective_id=1, has_side_effects=True, vmem_limit_bytes=VMEM_LIMIT
+        ),
+        cost_estimate=pl.CostEstimate(
+            flops=100_000_000_000, bytes_accessed=60_000_000, transcendentals=0
         ),
     )(
         gy,

time: 454 us -> 428 us (0.943)
  Pallas kernels: 356 us -> 331 us
    pallas_call x1, Pallas kernels: 146 us -> 111 us  [body(): pl.pallas_call(functools.partial(front_kernel, n, half, padded, gathered)...]
    pallas_call x1, Pallas kernels: 162 us -> 171 us  [body(): pl.pallas_call(functools.partial(rear_kernel, n, half, padded, gathered,...]
  transfers between devices with their start and end apart: 6 -> 6, of which waited for: 2 -> 2; matrix products, arithmetic and copies ran while one was open for 4% -> 4% of each run, Pallas kernels for 36% -> 41%
where the time goes in v4:
time: 428 us; the launch traced here: 421 us
  Pallas kernels  331 us (77%)
  waiting for transfers between devices  49.3 us (12%)
  local copies, waits for them, and re-layouts  25.5 us (6%)
  other arithmetic  11 us (3%)
    pallas_call x1, Pallas kernels, body(): pl.pallas_call(functools.partial(rear_kernel, n, half, padded, gathered,...  171 us
    pallas_call x1, Pallas kernels, body(): pl.pallas_call(functools.partial(front_kernel, n, half, padded, gathered)...  111 us
    pallas_call x1, Pallas kernels, body(): pl.pallas_call(functools.partial(expert_kernel, n, padded), grid=(4 * per...  48.1 us
    ppermute x2, waiting for transfers between devices, across_chips(): return lax.ppermute(value, 'tensor', [(0, 2), (2, 0), (1, 3), (3, 1)])  44.5 us
    unnamed x27, local copies, waits for them, and re-layouts  15.7 us
  transfers between devices with their start and end apart: 6, of which 2 were waited for; matrix products, arithmetic and copies ran while one was open for 4% of the time, Pallas kernels for 41%

profile of v4, /device:TPU:26, one launch (start us, length us, event | category | flops | bytes accessed | tf_op | source)
XLA Modules:
  0.0 420.7 jit_solution(18423396890170915744)
XLA Ops:
  0.7 0.9 copy.41
  1.6 0.8 slice_bitcast_fusion.2
  2.4 0.8 slice_bitcast_fusion.5
  3.2 0.8 copy.45
  3.9 0.8 copy.46
  4.7 0.8 copy.43
  5.5 0.8 copy.44
  6.3 0.8 copy.42
  7.1 2.1 copy.48.routes_all_ref
  9.2 1.3 copy.47.prev_all_ref
  10.5 0.8 concatenate.15.packed_ref
  11.3 111.2 %shard_map.238 = (bf16[1024,768]{1,0:T(8,128)(2,1)}, bf16[3,1024,128]{2,1,0:T(8,128)(2,1)}, bf16[3,1024,128]{2,1,0:T(8,128)(2,1)}, bf16[3,1024,128]{2,1,0:T(8,12...) custom-call(bf16[2,1024,768]{2,1,0:T(8,128)(2,1)} %tokens_ref.3, ...), custom_call_target="tpu_custom_call" | custom-call | flops 60000002048 | bytes 60000000 | tf_op jit(solution)/shard_map/pallas_call | solution.py:1274
  122.6 48.1 %shard_map.239 = (bf16[8,128,768]{2,1,0:T(8,128)(2,1)}, bf16[8,128,768]{2,1,0:T(8,128)(2,1)}, f32[8,8,128]{2,1,0:T(8,128)}, bf16[1,2,768,512]{3,2,1,0:T(8,128)(2...) custom-call(bf16[1024,768]{1,0:T(8,128)(2,1)} %bitcast.37, ...), custom_call_target="tpu_custom_call" | custom-call | flops 28991029248 | bytes 30000000 | tf_op jit(solution)/shard_map/pallas_call | solution.py:1340
  171.8 4.8 %collective-permute-done.1 = bf16[1,512,768]{2,1,0:T(8,128)(2,1)S(1)} collective-permute-done((bf16[1,512,768]{2,1,0:T(8,128)(2,1)}, bf16[1,512,768]{2,1,0:T(8,128)(2,1)S(1)}, u32[]{:S(2)}, u32[]{:S(2)}) %collective-permute-start.1) | collective-permute-done | bytes 786464 | tf_op jit(solution)/shard_map/ppermute | solution.py:1168
  176.6 2.2 add_convert_fusion.1
  179.3 171.2 %shard_map.240 = (bf16[2,1024,768]{2,1,0:T(8,128)(2,1)}, bf16[2,1024,768]{2,1,0:T(8,128)(2,1)}, f32[2,16,1024]{2,1,0:T(8,128)}, f32[96,768]{1,0:T(8,128)}, f32[96,128]{1,0:T(8,128)}) custom-call(bf16[8,128,768]{2,1,0:T(8,128)(2,1)} %get-tuple-element.63.gy_src_ref, bf16[8,128,768]{2,1,0:T(8,128)(2,1)} %get-tuple-element.69.dx_src_ref, ...), custom_call_target="tpu_custom_call" | custom-call | flops 99999997952 | bytes 60000000 | tf_op jit(solution)/shard_map/pallas_call | solution.py:1409
  350.5 0.9 slice.86
  351.4 0.9 slice_bitcast_fusion.1
  352.3 1.5 copy.52
  355.6 0.9 slice_bitcast_fusion
  357.3 1.5 collective-permute-start.5
  358.8 1.0 fusion.1
  359.7 1.5 fusion
  361.2 0.7 copy.51
  362.7 0.8 maximum_bitcast_fusion.2
  363.5 0.7 pad_maximum_fusion
  364.3 44.4 %collective-permute-done.5 = bf16[1,512,768]{2,1,0:T(8,128)(2,1)} collective-permute-done((bf16[1,512,768]{2,1,0:T(8,128)(2,1)}, bf16[1,512,768]{2,1,0:T(8,128)(2,1)}, u32[]{:S(2)}, u32[]{:S(2)}) %collective-permute-start.5) | collective-permute-done | bytes 786464 | tf_op jit(solution)/shard_map/ppermute | solution.py:1164
  408.7 3.0 convert_add_fusion.1
  411.7 3.8 convert_add_fusion
  415.5 1.7 copy.57
  417.2 1.4 copy-done
  418.6 1.7 copy.58
  (32 shorter events, 4.8 us)
Async XLA Ops:
  0.6 8.5 %copy-start.6 = (f32[2,1024,12]{1,0,2:T(2,128)S(1)}, f32[2,1024,12]{1,0,2:T(2,128)}, u32[]{:S(2)}) copy-start(f32[2,1024,12]{1,0,2:T(2,128)} %param.17) | copy-start | bytes 294916
  170.7 8.2 %copy-start.2 = (bf16[1,2,768,512]{3,2,1,0:T(8,128)(2,1)S(1)}, bf16[1,2,768,512]{3,2,1,0:T(8,128)(2,1)}, u32[]{:S(2)}) copy-start(bf16[1,2,768,512]{3,2,1,0:T(8,128)(2,1)} %get-tuple-element.64) | copy-start | bytes 4718596
  170.7 8.2 %collective-permute-start = (bf16[1,2,768,512]{3,2,1,0:T(8,128)(2,1)}, bf16[1,2,768,512]{3,2,1,0:T(8,128)(2,1)S(1)}, u32[]{:S(2)}, u32[]{:S(2)}) collective-permute-start(bf16[1,2,768,512]{3,2,1,0:T(8,128)(2,1)} %get-tuple-element.65), channel_id=1, source_target_pairs={{0,1},{1,0},{2,3},{3,2},{4,5},{5,4},{6,7},{7,6},{8,9},{9,8},{10,11... | collective-permute-start | bytes 4718600 | tf_op jit(solution)/shard_map/ppermute | solution.py:1168
  170.8 5.9 %collective-permute-start.1 = (bf16[1,512,768]{2,1,0:T(8,128)(2,1)}, bf16[1,512,768]{2,1,0:T(8,128)(2,1)S(1)}, u32[]{:S(2)}, u32[]{:S(2)}) collective-permute-start(bf16[1,512,768]{2,1,0:T(8,128)(2,1)} %get-tuple-element.67), channel_id=1, source_target_pairs={{0,1},{1,0},{2,3},{3,2},{4,5},{5,4},{6,7},{7,6},{8,9},{9,8},{10,11... | collective-permute-start | bytes 2359304 | tf_op jit(solution)/shard_map/ppermute | solution.py:1168
  171.3 193.0 %collective-permute-start.4 = (bf16[1,512,768]{2,1,0:T(8,128)(2,1)}, bf16[1,512,768]{2,1,0:T(8,128)(2,1)}, u32[]{:S(2)}, u32[]{:S(2)}) collective-permute-start(bf16[1,512,768]{2,1,0:T(8,128)(2,1)} %get-tuple-element.94), channel_id=1, source_target_pairs={{0,1},{1,0},{2,3},{3,2},{4,5},{5,4},{6,7},{7,6},{8,9},{9,8},{10,11... | collective-permute-start | bytes 2359304 | tf_op jit(solution)/shard_map/ppermute | solution.py:1168
  171.3 240.3 %collective-permute-start.2 = (bf16[1,2,768,512]{3,2,1,0:T(8,128)(2,1)}, bf16[1,2,768,512]{3,2,1,0:T(8,128)(2,1)S(1)}, u32[]{:S(2)}, u32[]{:S(2)}) collective-permute-start(bf16[1,2,768,512]{3,2,1,0:T(8,128)(2,1)} %get-tuple-element.91), channel_id=1, source_target_pairs={{0,1},{1,0},{2,3},{3,2},{4,5},{5,4},{6,7},{7,6},{8,9},{9,8},{10,11... | collective-permute-start | bytes 4718600 | tf_op jit(solution)/shard_map/ppermute | solution.py:1168
  350.5 11.5 %copy-start.4 = (f32[96,128]{1,0:T(8,128)S(1)}, f32[96,128]{1,0:T(8,128)}, u32[]{:S(2)}) copy-start(f32[96,128]{1,0:T(8,128)} %get-tuple-element.88) | copy-start | bytes 147460
  355.1 56.6 %collective-permute-start.3 = (bf16[1,2,768,512]{3,2,1,0:T(8,128)(2,1)S(1)}, bf16[1,2,768,512]{3,2,1,0:T(8,128)(2,1)}, u32[]{:S(2)}, u32[]{:S(2)}) collective-permute-start(bf16[1,2,768,512]{3,2,1,0:T(8,128)(2,1)S(1)} %add_convert_fusion), channel_id=1, source_target_pairs={{0,2},{2,0},{1,3},{3,1},{4,6},{6,4},{5,7},{7,5},{8,10},{10,8},{9,1... | collective-permute-start | bytes 4718600 | tf_op jit(solution)/shard_map/ppermute | solution.py:1164
  357.3 51.4 %collective-permute-start.5 = (bf16[1,512,768]{2,1,0:T(8,128)(2,1)}, bf16[1,512,768]{2,1,0:T(8,128)(2,1)}, u32[]{:S(2)}, u32[]{:S(2)}) collective-permute-start(bf16[1,512,768]{2,1,0:T(8,128)(2,1)} %add_convert_fusion.1), channel_id=1, source_target_pairs={{0,2},{2,0},{1,3},{3,1},{4,6},{6,4},{5,7},{7,5},{8,10},{10,8},{9,1... | collective-permute-start | bytes 2359304 | tf_op jit(solution)/shard_map/ppermute | solution.py:1164
  362.0 46.7 %copy-start.5 = (bf16[1,512,768]{2,1,0:T(8,128)(2,1)S(1)}, bf16[1,512,768]{2,1,0:T(8,128)(2,1)}, u32[]{:S(2)}) copy-start(bf16[1,512,768]{2,1,0:T(8,128)(2,1)} %get-tuple-element.93) | copy-start | bytes 2359300
  408.7 3.0 copy-start.3
  411.7 3.8 copy-start.1
  415.5 3.0 copy-start
